TPU v7x, 512 devices: a whole 4x8x8 slice. The times are simulated.
512 devices in a mesh: row: 16 (over y, z_lo), col: 32 (over z_hi, x, core).
Axes of the slice: x: 4, y: 8, z: 8 (z_hi: 4, z_lo: 2; z = z_hi * 2 + z_lo), core: 2. Of those that a mesh axis runs over, the one named last changes fastest.
Arguments:
- tiles: bfloat16 [16, 32, 32, 256, 256], P('row', 'col'), may hold values from -6 to 6
- tile_ids: int32 [16, 32, 2, 32], P('row', 'col'), may hold values from 0 to 7, as said below
- tile_count: int32 [16, 32], P('row', 'col'), may hold values from 8 to 32
- query_degree: int32 [32768], P('row'), may hold values from 1 to 32
- product_degree: int32 [65536], P('col'), may hold values from 1 to 32
- panel: float32 [64, 65536], P(None, ('col', 'row')), may hold values from -6 to 6
Outputs:
- basis: float32 [64, 65536], P(None, ('col', 'row'))
Inputs may be any that keep to these rules, and one draw needn't show every extreme that they name: `tile_ids`: on each device the 32 (tile row, tile column) pairs are distinct; tile row is below 8 and tile column below 8.
All inputs are finite; a program needn't handle non-finite values.
Results may differ from a plain program's by a relative error of at most 0.0042.
Values may be sent and summed in bfloat16 or wider, within the bound.
A program may use at most 64 MiB of HBM per device.

v0:
```python
import math

import jax
import jax.numpy as jnp
from jax import lax
from jax.sharding import PartitionSpec as P

ITERS = 2


HIGH = lax.Precision.HIGHEST


def orthonormal(lifted, gram):
    lower = jnp.linalg.cholesky(gram)
    return lax.linalg.triangular_solve(lower, lifted, left_side=True, lower=True)


def shards(tiles, tile_ids, tile_count, query_degree, product_degree, panel):
    tile_set = tiles[0, 0]
    slot_ids = tile_ids[0, 0]
    live_count = tile_count[0, 0]
    slots = tile_set.shape[0]
    side = tile_set.shape[1]
    width = panel.shape[0]
    query_tiles = query_degree.shape[0] // side
    product_tiles = product_degree.shape[0] // side
    live_slot = (jnp.arange(slots, dtype=jnp.int32) < live_count).astype(jnp.float32)
    row_hot = (slot_ids[0][:, None] == jnp.arange(query_tiles, dtype=jnp.int32)[None, :]).astype(
        jnp.float32
    ) * live_slot[:, None]
    col_hot = (slot_ids[1][:, None] == jnp.arange(product_tiles, dtype=jnp.int32)[None, :]).astype(
        jnp.float32
    ) * live_slot[:, None]
    qscale = 1.0 / jnp.sqrt(query_degree.astype(jnp.float32))
    pscale = 1.0 / jnp.sqrt(product_degree.astype(jnp.float32))
    row_at = lax.axis_index("row")
    col_at = lax.axis_index("col")
    share = panel.shape[1]
    my_pscale = lax.dynamic_slice_in_dim(pscale, row_at * share, share)
    root_count = math.sqrt(product_degree.shape[0] * lax.axis_size("col"))
    current = panel
    for iteration in range(ITERS):
        scaled = (current * my_pscale[None, :]).astype(jnp.bfloat16)
        scaled_block = lax.all_gather(scaled, "row", axis=1, tiled=True)
        picked = jnp.take(scaled_block.reshape(width, product_tiles, side), slot_ids[1], axis=1)
        products = jnp.einsum("rkj,kij->kri", picked, tile_set, preferred_element_type=jnp.float32)
        partial_sum = jnp.einsum("kq,kri->rqi", row_hot, products, precision=HIGH).reshape(
            width, query_tiles * side
        )
        query_share = lax.psum_scatter(partial_sum, "col", scatter_dimension=1, tiled=True)
        columns = query_share.shape[1]
        my_qscale = lax.dynamic_slice_in_dim(qscale, col_at * columns, columns)
        rounded = (query_share * my_qscale[None, :]).astype(jnp.bfloat16)
        query_block = lax.all_gather(rounded, "col", axis=1, tiled=True)
        backward_picked = jnp.take(
            query_block.reshape(width, query_tiles, side), slot_ids[0], axis=1
        )
        backward_products = jnp.einsum(
            "rki,kij->krj", backward_picked, tile_set, preferred_element_type=jnp.float32
        )
        lifted = (
            lax.psum_scatter(
                jnp.einsum("kp,krj->rpj", col_hot, backward_products, precision=HIGH).reshape(
                    width, product_tiles * side
                ),
                "row",
                scatter_dimension=1,
                tiled=True,
            )
            * my_pscale[None, :]
        )
        gram = lax.psum(jnp.einsum("ri,si->rs", lifted, lifted, precision=HIGH), ("row", "col"))
        current = orthonormal(lifted, gram)
    return current * root_count


def solution(mesh):
    in_specs = (
        P("row", "col", None, None, None),
        P("row", "col", None, None),
        P("row", "col"),
        P("row"),
        P("col"),
        P(None, ("col", "row")),
    )
    out_specs = P(None, ("col", "row"))
    return jax.shard_map(shards, mesh=mesh, in_specs=in_specs, out_specs=out_specs, check_vma=False)
```

profile of v0, /device:TPU:6, one launch (start us, length us, event | category | flops | bytes accessed | tf_op | source)
XLA Modules:
  0.0 754.6 jit_solution(1532699937566994767)
XLA Ops:
  10.3 36.3 %all_gather.12 = bf16[64,2048]{1,0:T(8,128)(2,1)S(1)} all-gather(bf16[64,128]{1,0:T(8,128)(2,1)S(1)} %multiply_convert_fusion.2), channel_id=1, replica_groups=mesh['row'=16,'col'=32] {'row'}, dimensions={1}, use_global_device_ids=true | all-gather | bytes 278528 | tf_op jit(solution)/shard_map/all_gather | solution.py:45
  47.3 3.6 fusion.6
  50.8 2.4 fusion.16
  53.2 1.4 copy.55
  55.4 97.3 %reduce-scatter.13.cloned.1.call-done = f32[64,64]{1,0:T(8,128)} async-done(((f32[2048,64]{1,0:T(8,128)}), f32[64,64]{1,0:T(8,128)}) %reduce-scatter.13.cloned.1.call-update) | async-done | bytes 16400
  152.7 0.8 copy.52
  153.6 36.5 %all_gather.13 = bf16[64,2048]{0,1:T(8,128)(2,1)S(1)} all-gather(bf16[64,64]{0,1:T(8,128)(2,1)S(1)} %copy.31), channel_id=1, replica_groups=mesh['row'=16,'col'=32] {'col'}, dimensions={1}, use_global_device_ids=true | all-gather | bytes 270336 | tf_op jit(solution)/shard_map/all_gather | solution.py:55
  191.0 3.1 fusion.4
  194.1 2.4 fusion.12
  196.4 1.0 copy.59
  197.4 77.2 %reduce-scatter.9.cloned.1.call-done = f32[64,128]{1,0:T(8,128)} async-done(((f32[64,2048]{1,0:T(8,128)}), f32[64,128]{1,0:T(8,128)}) %reduce-scatter.9.cloned.1.call-update) | async-done | bytes 32784 | tf_op jit(solution)/shard_map/reduce_scatter | solution.py:63
  274.7 1.0 fusion.51
  275.7 93.6 %psum.14 = f32[64,64]{0,1:T(8,128)S(1)} all-reduce(f32[64,64]{0,1:T(8,128)S(1)} %fusion.51), channel_id=1, replica_groups=mesh['row'=16,'col'=32] {'row','col'}, use_global_device_ids=true, to_apply=%region_2.4 | all-reduce | flops 4096 | bytes 32768 | tf_op jit(solution)/shard_map/psum | solution.py:73
  369.4 5.8 cholesky.44
  376.5 4.9 custom-call.6
  381.4 1.0 fusion.22
  382.5 32.9 %all_gather.14 = bf16[64,2048]{1,0:T(8,128)(2,1)S(1)} all-gather(bf16[64,128]{1,0:T(8,128)(2,1)S(1)} %fusion.22), channel_id=1, replica_groups=mesh['row'=16,'col'=32] {'row'}, dimensions={1}, use_global_device_ids=true | all-gather | bytes 278528 | tf_op jit(solution)/shard_map/all_gather | solution.py:45
  416.0 3.6 fusion.2
  419.6 2.4 fusion.19
  422.0 1.4 copy.56
  423.4 94.3 %reduce-scatter.15.cloned.1.call-done = f32[64,64]{1,0:T(8,128)} async-done(((f32[2048,64]{1,0:T(8,128)}), f32[64,64]{1,0:T(8,128)}) %reduce-scatter.15.cloned.1.call-update) | async-done | bytes 16400
  517.7 0.8 copy.54
  518.6 36.6 %all_gather.15 = bf16[64,2048]{0,1:T(8,128)(2,1)S(1)} all-gather(bf16[64,64]{0,1:T(8,128)(2,1)S(1)} %copy.39), channel_id=1, replica_groups=mesh['row'=16,'col'=32] {'col'}, dimensions={1}, use_global_device_ids=true | all-gather | bytes 270336 | tf_op jit(solution)/shard_map/all_gather | solution.py:55
  556.0 3.1 fusion
  559.1 2.4 fusion.8
  561.4 1.0 copy.60
  562.4 77.3 %reduce-scatter.11.cloned.1.call-done = f32[64,128]{1,0:T(8,128)} async-done(((f32[64,2048]{1,0:T(8,128)}), f32[64,128]{1,0:T(8,128)}) %reduce-scatter.11.cloned.1.call-update) | async-done | bytes 32784 | tf_op jit(solution)/shard_map/reduce_scatter | solution.py:63
  639.7 1.0 fusion.48
  640.7 93.6 %psum.15 = f32[64,64]{0,1:T(8,128)S(1)} all-reduce(f32[64,64]{0,1:T(8,128)S(1)} %fusion.48), channel_id=1, replica_groups=mesh['row'=16,'col'=32] {'row','col'}, use_global_device_ids=true, to_apply=%region_7.11 | all-reduce | flops 4096 | bytes 32768 | tf_op jit(solution)/shard_map/psum | solution.py:73
  734.4 5.8 cholesky.55
  741.6 4.9 custom-call.7
  746.5 1.6 convolution_multiply_fusion
  (38 shorter events, 9.9 us)
Async XLA Ops:
  6.5 146.2 %reduce-scatter.13.cloned.1.call-start = ((), (), s32[]{:S(2)}) async-start(), calls=%async_computation.6 | async-start | bytes 1081344
  54.6 220.1 %reduce-scatter.9.cloned.1.call-start = ((), (), s32[]{:S(2)}) async-start(), calls=%async_computation.4 | async-start | bytes 557056 | tf_op jit(solution)/shard_map/reduce_scatter | solution.py:63
  197.4 320.3 %reduce-scatter.15.cloned.1.call-start = ((), (), s32[]{:S(2)}) async-start(), calls=%async_computation.7 | async-start | bytes 1081344
  423.4 216.3 %reduce-scatter.11.cloned.1.call-start = ((), (), s32[]{:S(2)}) async-start(), calls=%async_computation.5 | async-start | bytes 557056 | tf_op jit(solution)/shard_map/reduce_scatter | solution.py:63
Sparse Core Ops, SparseCore 0:
  54.7 97.9 reduce-scatter.12
  197.5 77.1 reduce-scatter.8
  423.5 94.1 reduce-scatter.14
  562.5 77.0 reduce-scatter.10
where the time goes:
time: 759 us; the launch traced here: 755 us
  waiting for transfers between devices  346 us (46%)
  blocking collectives  329 us (43%)
  matrix products  27.4 us (4%)
  other arithmetic  27.3 us (4%)
  between operations  14 us (2%)
  local copies, waits for them, and re-layouts  10.3 us (1%)
    unnamed x6, waiting for transfers between devices  192 us
    psum x2, blocking collectives, shards(): lax.psum(jnp.einsum('ri,si->rs', lifted, lifted, precision=HIGH), ('row',...  187 us
    reduce_scatter x2, waiting for transfers between devices, shards(): lax.psum_scatter(jnp.einsum('kp,krj->rpj', col_hot, backward_products, pr...  154 us
    all_gather x2, blocking collectives, shards(): query_block = lax.all_gather(rounded, 'col', axis=1, tiled=True)  73.1 us
    all_gather x2, blocking collectives, shards(): scaled_block = lax.all_gather(scaled, 'row', axis=1, tiled=True)  69.3 us
  transfers between devices with their start and end apart: 4, of which 4 were waited for; matrix products, arithmetic and copies ran while one was open for 0% of the time, Pallas kernels for 0%

commit v1 on v0

v1 whole, which is shorter than its diff:
```python
import functools
import math

import jax
import jax.numpy as jnp
from jax import lax
from jax.experimental import pallas as pl
from jax.experimental.pallas import tpu as pltpu
from jax.sharding import PartitionSpec as P

ITERS = 2


HIGH = lax.Precision.HIGHEST

AXES = ("row", "col")


def _device(axis, peer):
    if axis == "row":
        return (peer, lax.axis_index("col"))
    return (lax.axis_index("row"), peer)


def _exchange_kernel(x_ref, y_ref, buf, send_sems, recv_sems, *, axis, n, bcast):
    me = lax.axis_index(axis)
    barrier = pltpu.get_barrier_semaphore()

    def greet(k, carry):
        peer = lax.rem(me + k, n)
        pl.semaphore_signal(barrier, inc=1, device_id=_device(axis, peer),
                            device_id_type=pl.DeviceIdType.MESH)
        return carry

    lax.fori_loop(1, n, greet, 0)
    pl.semaphore_wait(barrier, n - 1)

    def source(peer):
        return x_ref.at[0] if bcast else x_ref.at[peer]

    def send(k, carry):
        peer = lax.rem(me + k, n)
        pltpu.make_async_remote_copy(
            src_ref=source(peer), dst_ref=buf.at[me],
            send_sem=send_sems.at[peer], recv_sem=recv_sems.at[me],
            device_id=_device(axis, peer), device_id_type=pl.DeviceIdType.MESH,
        ).start()
        return carry

    lax.fori_loop(1, n, send, 0)
    if bcast:
        y_ref[me] = x_ref[0]
    else:
        y_ref[me] = x_ref[me]

    def finish(k, carry):
        peer = lax.rem(me + k, n)
        pltpu.make_async_remote_copy(
            src_ref=source(peer), dst_ref=buf.at[me],
            send_sem=send_sems.at[peer], recv_sem=recv_sems.at[me],
            device_id=_device(axis, peer), device_id_type=pl.DeviceIdType.MESH,
        ).wait_send()
        pltpu.make_async_remote_copy(
            src_ref=source(peer), dst_ref=buf.at[peer],
            send_sem=send_sems.at[peer], recv_sem=recv_sems.at[peer],
            device_id=_device(axis, peer), device_id_type=pl.DeviceIdType.MESH,
        ).wait_recv()
        y_ref[peer] = buf[peer]
        return carry

    lax.fori_loop(1, n, finish, 0)


def exchange(x, axis, n, bcast, cid):
    chunk = x.shape[1:]
    nbytes = n * math.prod(chunk) * x.dtype.itemsize
    return pl.pallas_call(
        functools.partial(_exchange_kernel, axis=axis, n=n, bcast=bcast),
        out_shape=jax.ShapeDtypeStruct((n,) + chunk, x.dtype),
        in_specs=[pl.BlockSpec(memory_space=pltpu.VMEM)],
        out_specs=pl.BlockSpec(memory_space=pltpu.VMEM),
        scratch_shapes=[
            pltpu.VMEM((n,) + chunk, x.dtype),
            pltpu.SemaphoreType.DMA((n,)),
            pltpu.SemaphoreType.DMA((n,)),
        ],
        compiler_params=pltpu.CompilerParams(collective_id=cid, has_side_effects=True),
        cost_estimate=pl.CostEstimate(flops=0, transcendentals=0, bytes_accessed=3 * nbytes),
    )(x)


def orthonormal(lifted, gram):
    lower = jnp.linalg.cholesky(gram)
    return lax.linalg.triangular_solve(lower, lifted, left_side=True, lower=True)


def shards(tiles, tile_ids, tile_count, query_degree, product_degree, panel):
    tile_set = tiles[0, 0]
    slot_ids = tile_ids[0, 0]
    live_count = tile_count[0, 0]
    slots = tile_set.shape[0]
    side = tile_set.shape[1]
    width = panel.shape[0]
    query_tiles = query_degree.shape[0] // side
    product_tiles = product_degree.shape[0] // side
    n_row = lax.axis_size("row")
    n_col = lax.axis_size("col")
    live_slot = (jnp.arange(slots, dtype=jnp.int32) < live_count).astype(jnp.float32)
    row_hot = (slot_ids[0][:, None] == jnp.arange(query_tiles, dtype=jnp.int32)[None, :]).astype(
        jnp.float32
    ) * live_slot[:, None]
    col_hot = (slot_ids[1][:, None] == jnp.arange(product_tiles, dtype=jnp.int32)[None, :]).astype(
        jnp.float32
    ) * live_slot[:, None]
    qscale = 1.0 / jnp.sqrt(query_degree.astype(jnp.float32))
    pscale = 1.0 / jnp.sqrt(product_degree.astype(jnp.float32))
    row_at = lax.axis_index("row")
    col_at = lax.axis_index("col")
    share = panel.shape[1]
    block = pscale.shape[0]
    qchunk = query_degree.shape[0] // n_col
    my_pscale = lax.dynamic_slice_in_dim(pscale, row_at * share, share)
    my_qscale = lax.dynamic_slice_in_dim(qscale, col_at * qchunk, qchunk)
    root_count = math.sqrt(product_degree.shape[0] * n_col)

    scaled0 = (panel * my_pscale[None, :]).astype(jnp.bfloat16)
    gathered = exchange(scaled0[None], "row", n_row, True, 0)
    scaled_block = jnp.transpose(gathered, (1, 0, 2)).reshape(width, block)
    current = None
    for iteration in range(ITERS):
        if current is not None:
            scaled_block = (current * pscale[None, :]).astype(jnp.bfloat16)
        picked = jnp.take(scaled_block.reshape(width, product_tiles, side), slot_ids[1], axis=1)
        products = jnp.einsum("rkj,kij->kri", picked, tile_set, preferred_element_type=jnp.float32)
        partial_sum = jnp.einsum("kq,kri->rqi", row_hot, products, precision=HIGH).reshape(
            width, n_col, qchunk
        )
        pieces = exchange(jnp.transpose(partial_sum, (1, 0, 2)), "col", n_col, False, 1)
        query_share = jnp.sum(pieces, axis=0)
        rounded = (query_share * my_qscale[None, :]).astype(jnp.bfloat16)
        query_pieces = exchange(rounded[None], "col", n_col, True, 2)
        query_block = jnp.transpose(query_pieces, (1, 0, 2)).reshape(width, query_tiles * side)
        backward_picked = jnp.take(
            query_block.reshape(width, query_tiles, side), slot_ids[0], axis=1
        )
        backward_products = jnp.einsum(
            "rki,kij->krj", backward_picked, tile_set, preferred_element_type=jnp.float32
        )
        product_partial = jnp.einsum(
            "kp,krj->rpj", col_hot, backward_products, precision=HIGH
        ).reshape(width, n_row, share)
        product_pieces = exchange(jnp.transpose(product_partial, (1, 0, 2)), "row", n_row, False, 3)
        lifted_share = jnp.sum(product_pieces, axis=0) * my_pscale[None, :]
        lifted_pieces = exchange(lifted_share[None], "row", n_row, True, 4)
        lifted = jnp.transpose(lifted_pieces, (1, 0, 2)).reshape(width, block)
        gram_part = jnp.einsum("ri,si->rs", lifted, lifted, precision=HIGH)
        gram = jnp.sum(exchange(gram_part[None], "col", n_col, True, 5), axis=0)
        current = orthonormal(lifted, gram)
    mine = lax.dynamic_slice_in_dim(current, row_at * share, share, axis=1)
    return mine * root_count


def solution(mesh):
    in_specs = (
        P("row", "col", None, None, None),
        P("row", "col", None, None),
        P("row", "col"),
        P("row"),
        P("col"),
        P(None, ("col", "row")),
    )
    out_specs = P(None, ("col", "row"))
    return jax.shard_map(shards, mesh=mesh, in_specs=in_specs, out_specs=out_specs, check_vma=False)
```

time: 759 us -> 376 us (0.50)
  the two profiles are of different devices: /device:TPU:6 before, /device:TPU:71 now
where the time goes in v1:
time: 376 us; the launch traced here: 374 us
  Pallas kernels  292 us (78%)
  other arithmetic  38.3 us (10%)
  matrix products  28.9 us (8%)
  local copies, waits for them, and re-layouts  13.9 us (4%)
    pallas_call x11, Pallas kernels, exchange(): pl.pallas_call(functools.partial(_exchange_kernel, axis=axis, n=n, bcast=...  292 us
    another operation x6, other arithmetic, orthonormal(): lower = jnp.linalg.cholesky(gram)  13 us
    another operation x4, other arithmetic, orthonormal(): lax.linalg.triangular_solve(lower, lifted, left_side=True, lower=True)  11.1 us

profile of v1, /device:TPU:71, one launch (start us, length us, event | category | flops | bytes accessed | tf_op | source)
XLA Modules:
  0.0 374.3 jit_solution(18407745061026950519)
XLA Ops:
  3.7 1.4 fusion.62.x_ref
  5.1 15.2 %shard_map.64 = bf16[16,64,128]{2,1,0:T(8,128)(2,1)} custom-call(bf16[1,64,128]{2,1,0:T(8,128)(2,1)} %fusion.62.x_ref), custom_call_target="tpu_custom_call" | custom-call | bytes 786432 | tf_op jit(solution)/shard_map/pallas_call | solution.py:77
  22.2 3.6 fusion.6
  25.8 2.4 fusion.17
  28.4 1.6 copy.76
  30.0 43.1 %shard_map.65 = f32[32,64,64]{2,1,0:T(8,128)} custom-call(f32[32,64,64]{2,1,0:T(8,128)} %bitcast.129), custom_call_target="tpu_custom_call" | custom-call | bytes 1572864 | tf_op jit(solution)/shard_map/pallas_call | solution.py:77
  73.1 1.3 reduce_sum.62
  75.1 20.5 %shard_map.66 = bf16[32,64,64]{2,1,0:T(8,128)(2,1)} custom-call(bf16[1,64,64]{2,1,0:T(8,128)(2,1)} %fusion.59.x_ref), custom_call_target="tpu_custom_call" | custom-call | bytes 786432 | tf_op jit(solution)/shard_map/pallas_call | solution.py:77
  95.6 1.4 copy.28
  98.0 3.1 fusion.4
  101.1 2.4 fusion.20
  104.5 20.7 %shard_map.67 = f32[16,64,128]{2,1,0:T(8,128)} custom-call(f32[16,64,128]{2,1,0:T(8,128)} %bitcast.132), custom_call_target="tpu_custom_call" | custom-call | bytes 1572864 | tf_op jit(solution)/shard_map/pallas_call | solution.py:77
  126.9 18.2 %shard_map.68 = f32[16,64,128]{2,1,0:T(8,128)} custom-call(f32[1,64,128]{2,1,0:T(8,128)} %bitcast_multiply_fusion.2.x_ref), custom_call_target="tpu_custom_call" | custom-call | bytes 1572864 | tf_op jit(solution)/shard_map/pallas_call | solution.py:77
  145.1 2.4 convolution_bitcast_fusion.1.x_ref
  147.5 37.3 %shard_map.69 = f32[32,64,64]{2,1,0:T(8,128)} custom-call(f32[1,64,64]{2,1,0:T(8,128)} %convolution_bitcast_fusion.1.x_ref), custom_call_target="tpu_custom_call" | custom-call | bytes 1572864 | tf_op jit(solution)/shard_map/pallas_call | solution.py:77
  186.3 5.8 %cholesky.44 = f32[64,64]{1,0:T(8,128)S(1)} custom-call(f32[64,64]{1,0:T(8,128)S(1)} %fusion.58), custom_call_target="Cholesky" | custom-call | tf_op jit(solution)/shard_map/jit(cholesky)/cholesky | solution.py:93
  193.5 4.9 %custom-call.6 = f32[1,64,64]{1,2,0:T(8,128)S(1)} custom-call(f32[1,64,64]{2,1,0:T(8,128)S(1)} %fusion.52), custom_call_target="InvertDiagBlocksLowerTriangular" | custom-call | tf_op jit(solution)/shard_map/triangular_solve/custom-call.0 | solution.py:94
  199.7 3.6 fusion.2
  203.2 2.4 fusion.23
  205.8 1.6 copy.75
  207.4 36.3 %shard_map.70 = f32[32,64,64]{2,1,0:T(8,128)} custom-call(f32[32,64,64]{2,1,0:T(8,128)} %bitcast.130), custom_call_target="tpu_custom_call" | custom-call | bytes 1572864 | tf_op jit(solution)/shard_map/pallas_call | solution.py:77
  243.8 1.3 reduce_sum.67
  245.7 21.0 %shard_map.71 = bf16[32,64,64]{2,1,0:T(8,128)(2,1)} custom-call(bf16[1,64,64]{2,1,0:T(8,128)(2,1)} %fusion.56.x_ref), custom_call_target="tpu_custom_call" | custom-call | bytes 786432 | tf_op jit(solution)/shard_map/pallas_call | solution.py:77
  266.7 1.4 copy.37
  269.1 3.1 fusion
  272.2 2.4 fusion.26
  275.6 20.8 %shard_map.72 = f32[16,64,128]{2,1,0:T(8,128)} custom-call(f32[16,64,128]{2,1,0:T(8,128)} %bitcast.134), custom_call_target="tpu_custom_call" | custom-call | bytes 1572864 | tf_op jit(solution)/shard_map/pallas_call | solution.py:77
  298.1 19.9 %shard_map.73 = f32[16,64,128]{2,1,0:T(8,128)} custom-call(f32[1,64,128]{2,1,0:T(8,128)} %bitcast_multiply_fusion.x_ref), custom_call_target="tpu_custom_call" | custom-call | bytes 1572864 | tf_op jit(solution)/shard_map/pallas_call | solution.py:77
  318.1 2.4 convolution_bitcast_fusion.x_ref
  320.5 39.0 %shard_map.74 = f32[32,64,64]{2,1,0:T(8,128)} custom-call(f32[1,64,64]{2,1,0:T(8,128)} %convolution_bitcast_fusion.x_ref), custom_call_target="tpu_custom_call" | custom-call | bytes 1572864 | tf_op jit(solution)/shard_map/pallas_call | solution.py:77
  360.9 5.8 %cholesky.55 = f32[64,64]{1,0:T(8,128)S(1)} custom-call(f32[64,64]{1,0:T(8,128)S(1)} %fusion.55), custom_call_target="Cholesky" | custom-call | tf_op jit(solution)/shard_map/jit(cholesky)/cholesky | solution.py:93
  368.1 4.9 %custom-call.7 = f32[1,64,64]{1,2,0:T(8,128)S(1)} custom-call(f32[1,64,64]{2,1,0:T(8,128)S(1)} %fusion.53), custom_call_target="InvertDiagBlocksLowerTriangular" | custom-call | tf_op jit(solution)/shard_map/triangular_solve/custom-call.0 | solution.py:94
  (50 shorter events, 21.9 us)
Async XLA Ops:
  145.1 53.3 %copy-start = (f32[16,64,128]{2,1,0:T(8,128)S(1)}, f32[16,64,128]{2,1,0:T(8,128)}, u32[]{:S(2)}) copy-start(f32[16,64,128]{2,1,0:T(8,128)} %shard_map.68) | copy-start | bytes 1572868
  318.0 54.9 %copy-start.1 = (f32[16,64,128]{2,1,0:T(8,128)S(1)}, f32[16,64,128]{2,1,0:T(8,128)}, u32[]{:S(2)}) copy-start(f32[16,64,128]{2,1,0:T(8,128)} %shard_map.73) | copy-start | bytes 1572868

commit v2 on v0

v2 whole, which is shorter than its diff:
```python
import functools
import math

import jax
import jax.numpy as jnp
from jax import lax
from jax.experimental import pallas as pl
from jax.experimental.pallas import tpu as pltpu
from jax.sharding import PartitionSpec as P

ITERS = 2


HIGH = lax.Precision.HIGHEST

AXES = ("row", "col")


def _device(axis, peer):
    if axis == "row":
        return (peer, lax.axis_index("col"))
    return (lax.axis_index("row"), peer)


def _staged_kernel(*refs, axis, factors, mode, has_scale, epilogue):
    if has_scale:
        x_ref, s_ref, y_ref = refs[:3]
        rest = refs[3:]
    else:
        x_ref, y_ref = refs[:2]
        s_ref = None
        rest = refs[2:]
    stages = len(factors)
    n_rs = stages if mode in ("reduce", "sum") else 0
    rbufs = rest[:n_rs]
    gbuf = rest[n_rs] if mode != "sum" else None
    sems = rest[-1]
    me = lax.axis_index(axis)
    strides = [math.prod(factors[:s]) for s in range(stages)]
    mine = [lax.rem(lax.div(me, strides[s]), factors[s]) for s in range(stages)]

    def peer_of(s, d):
        return me + (d - mine[s]) * strides[s]

    def other(s, k):
        return lax.rem(mine[s] + k, factors[s])

    barrier = pltpu.get_barrier_semaphore()
    for s in range(stages):
        for k in range(1, factors[s]):
            pl.semaphore_signal(barrier, inc=1, device_id=_device(axis, peer_of(s, other(s, k))),
                                device_id_type=pl.DeviceIdType.MESH)
    pl.semaphore_wait(barrier, sum(f - 1 for f in factors))

    def exchange_stage(kind, s, src_of, dst_of):
        copies = []
        for k in range(1, factors[s]):
            d = other(s, k)
            c = pltpu.make_async_remote_copy(
                src_ref=src_of(d), dst_ref=dst_of(mine[s]),
                send_sem=sems.at[kind, s, d], recv_sem=sems.at[kind + 1, s, mine[s]],
                device_id=_device(axis, peer_of(s, d)), device_id_type=pl.DeviceIdType.MESH,
            )
            c.start()
            copies.append((d, c))
        for d, c in copies:
            c.wait_send()
            pltpu.make_async_remote_copy(
                src_ref=src_of(d), dst_ref=dst_of(d),
                send_sem=sems.at[kind, s, d], recv_sem=sems.at[kind + 1, s, d],
                device_id=_device(axis, peer_of(s, d)), device_id_type=pl.DeviceIdType.MESH,
            ).wait_recv()

    if mode == "sum":
        acc = x_ref
        for s in range(stages):
            rb = rbufs[s]
            rb[mine[s]] = acc[...]
            exchange_stage(0, s, lambda d: acc, lambda d, rb=rb: rb.at[d])
            total = rb[0]
            for d in range(1, factors[s]):
                total = total + rb[d]
            if s == stages - 1:
                y_ref[...] = total
            else:
                rbufs[s + 1][mine[s + 1]] = total
                acc = rbufs[s + 1].at[mine[s + 1]]
        return

    if mode == "reduce":
        cur = x_ref
        for s in range(stages):
            lead = stages - 1 - s

            def src_of(d, cur=cur, lead=lead):
                return cur.at[(slice(None),) * lead + (d,)]

            rb = rbufs[s]
            exchange_stage(0, s, src_of, lambda d, rb=rb: rb.at[d])
            total = cur[(slice(None),) * lead + (mine[s],)]
            for k in range(1, factors[s]):
                total = total + rb[other(s, k)]
            rb[mine[s]] = total
            cur = rb.at[mine[s]]
        own = epilogue(cur[...], s_ref)
    else:
        own = x_ref[...]
    gbuf[tuple(mine[::-1])] = own.astype(gbuf.dtype)
    for s in reversed(range(stages)):
        lead = stages - 1 - s

        def view(d, s=s, lead=lead):
            return gbuf.at[(slice(None),) * lead + (d,) + tuple(mine[s - 1::-1] if s else ())]

        exchange_stage(2, s, lambda d, s=s: view(mine[s]), view)
    y_ref[...] = gbuf[...]


def staged(x, axis, factors, mode, cid, scale=None, epilogue=None, out_dtype=None):
    n = math.prod(factors)
    stages = len(factors)
    out_dtype = out_dtype or x.dtype
    if mode == "reduce":
        chunk = x.shape[1:]
        x = x.reshape(tuple(reversed(factors)) + chunk)
    else:
        chunk = x.shape
    scratch = []
    if mode in ("reduce", "sum"):
        for s in range(stages):
            rest = tuple(reversed(factors[s + 1:])) if mode == "reduce" else ()
            scratch.append(pltpu.VMEM((factors[s],) + rest + chunk, jnp.float32))
    if mode != "sum":
        scratch.append(pltpu.VMEM(tuple(reversed(factors)) + chunk, out_dtype))
    scratch.append(pltpu.SemaphoreType.DMA((4, stages, max(factors))))
    if mode == "sum":
        out_shape = chunk
    else:
        out_shape = tuple(reversed(factors)) + chunk
    args = (x,) if scale is None else (x, scale)
    nbytes = n * math.prod(chunk) * 4
    y = pl.pallas_call(
        functools.partial(_staged_kernel, axis=axis, factors=tuple(factors), mode=mode,
                          has_scale=scale is not None, epilogue=epilogue),
        out_shape=jax.ShapeDtypeStruct(out_shape, out_dtype),
        in_specs=[pl.BlockSpec(memory_space=pltpu.VMEM)] * len(args),
        out_specs=pl.BlockSpec(memory_space=pltpu.VMEM),
        scratch_shapes=scratch,
        compiler_params=pltpu.CompilerParams(collective_id=cid, has_side_effects=True),
        cost_estimate=pl.CostEstimate(flops=0, transcendentals=0, bytes_accessed=2 * nbytes),
    )(*args)
    if mode == "sum":
        return y
    return y.reshape((n,) + chunk)


COL_FACTORS = (2, 4, 4)
ROW_FACTORS = (2, 4, 2)


def _query_epilogue(total, s_ref):
    return (total * s_ref[...]).astype(jnp.bfloat16)


def _product_epilogue(total, s_ref):
    return total * s_ref[...]


def orthonormal(lifted, gram):
    lower = jnp.linalg.cholesky(gram)
    return lax.linalg.triangular_solve(lower, lifted, left_side=True, lower=True)


def shards(tiles, tile_ids, tile_count, query_degree, product_degree, panel):
    tile_set = tiles[0, 0]
    slot_ids = tile_ids[0, 0]
    live_count = tile_count[0, 0]
    slots = tile_set.shape[0]
    side = tile_set.shape[1]
    width = panel.shape[0]
    query_tiles = query_degree.shape[0] // side
    product_tiles = product_degree.shape[0] // side
    n_row = lax.axis_size("row")
    n_col = lax.axis_size("col")
    live_slot = (jnp.arange(slots, dtype=jnp.int32) < live_count).astype(jnp.float32)
    row_hot = (slot_ids[0][:, None] == jnp.arange(query_tiles, dtype=jnp.int32)[None, :]).astype(
        jnp.float32
    ) * live_slot[:, None]
    col_hot = (slot_ids[1][:, None] == jnp.arange(product_tiles, dtype=jnp.int32)[None, :]).astype(
        jnp.float32
    ) * live_slot[:, None]
    qscale = 1.0 / jnp.sqrt(query_degree.astype(jnp.float32))
    pscale = 1.0 / jnp.sqrt(product_degree.astype(jnp.float32))
    row_at = lax.axis_index("row")
    col_at = lax.axis_index("col")
    share = panel.shape[1]
    block = pscale.shape[0]
    qchunk = query_degree.shape[0] // n_col
    my_pscale = lax.dynamic_slice_in_dim(pscale, row_at * share, share)
    my_qscale = lax.dynamic_slice_in_dim(qscale, col_at * qchunk, qchunk)
    root_count = math.sqrt(product_degree.shape[0] * n_col)

    scaled0 = (panel * my_pscale[None, :]).astype(jnp.bfloat16)
    gathered = staged(scaled0, "row", ROW_FACTORS, "gather", 0)
    scaled_block = jnp.transpose(gathered, (1, 0, 2)).reshape(width, block)
    current = None
    for iteration in range(ITERS):
        if current is not None:
            scaled_block = (current * pscale[None, :]).astype(jnp.bfloat16)
        picked = jnp.take(scaled_block.reshape(width, product_tiles, side), slot_ids[1], axis=1)
        products = jnp.einsum("rkj,kij->kri", picked, tile_set, preferred_element_type=jnp.float32)
        partial_sum = jnp.einsum("kq,kri->rqi", row_hot, products, precision=HIGH).reshape(
            width, n_col, qchunk
        )
        query_pieces = staged(jnp.transpose(partial_sum, (1, 0, 2)), "col", COL_FACTORS, "reduce", 1,
                              scale=my_qscale[None, :], epilogue=_query_epilogue,
                              out_dtype=jnp.bfloat16)
        query_block = jnp.transpose(query_pieces, (1, 0, 2)).reshape(width, query_tiles * side)
        backward_picked = jnp.take(
            query_block.reshape(width, query_tiles, side), slot_ids[0], axis=1
        )
        backward_products = jnp.einsum(
            "rki,kij->krj", backward_picked, tile_set, preferred_element_type=jnp.float32
        )
        product_partial = jnp.einsum(
            "kp,krj->rpj", col_hot, backward_products, precision=HIGH
        ).reshape(width, n_row, share)
        lifted_pieces = staged(jnp.transpose(product_partial, (1, 0, 2)), "row", ROW_FACTORS, "reduce",
                               2, scale=my_pscale[None, :], epilogue=_product_epilogue)
        lifted = jnp.transpose(lifted_pieces, (1, 0, 2)).reshape(width, block)
        gram_part = jnp.einsum("ri,si->rs", lifted, lifted, precision=HIGH)
        gram = staged(gram_part, "col", COL_FACTORS, "sum", 3)
        current = orthonormal(lifted, gram)
    mine = lax.dynamic_slice_in_dim(current, row_at * share, share, axis=1)
    return mine * root_count


def solution(mesh):
    in_specs = (
        P("row", "col", None, None, None),
        P("row", "col", None, None),
        P("row", "col"),
        P("row"),
        P("col"),
        P(None, ("col", "row")),
    )
    out_specs = P(None, ("col", "row"))
    return jax.shard_map(shards, mesh=mesh, in_specs=in_specs, out_specs=out_specs, check_vma=False)
```

time: 759 us -> 290 us (0.38)
  waiting for transfers between devices: 346 us -> 0 us
  blocking collectives: 329 us -> 0 us
  Pallas kernels: 0 us -> 208 us
  between operations: 14 us -> 0.97 us
  local copies, waits for them, and re-layouts: 10.3 us -> 18 us
    pallas_call x0 -> x7, Pallas kernels: none -> 208 us  [staged(): pl.pallas_call(functools.partial(_staged_kernel, axis=axis, factors=tuple...]
    unnamed x6 -> x0, waiting for transfers between devices: 192 us -> none
    psum x2 -> x0, blocking collectives: 187 us -> none  [shards(): lax.psum(jnp.einsum('ri,si->rs', lifted, lifted, precision=HIGH), ('row',...]
    reduce_scatter x2 -> x0, waiting for transfers between devices: 154 us -> none  [shards(): lax.psum_scatter(jnp.einsum('kp,krj->rpj', col_hot, backward_products, pr...]
    all_gather x4 -> x0, blocking collectives: 142 us -> none  [the longest x2 73.1 us: shards(): query_block = lax.all_gather(rounded, 'col', axis=1, tiled=True)]
    reshape x2 -> x13, local copies, waits for them, and re-layouts: 0.39 us -> 12.2 us  [the longest x5 6.63 us: staged(): return y.reshape((n,) + chunk)]
  transfers between devices with their start and end apart: 4 -> 0, of which waited for: 4 -> 0; matrix products, arithmetic and copies ran while one was open for 0% -> 0% of each run, Pallas kernels for 0% -> 0%
where the time goes in v2:
time: 290 us; the launch traced here: 287 us
  Pallas kernels  208 us (72%)
  other arithmetic  30.8 us (11%)
  matrix products  29 us (10%)
  local copies, waits for them, and re-layouts  18 us (6%)
    pallas_call x7, Pallas kernels, staged(): pl.pallas_call(functools.partial(_staged_kernel, axis=axis, factors=tuple...  208 us
    another operation x6, other arithmetic, orthonormal(): lower = jnp.linalg.cholesky(gram)  13.2 us
    another operation x4, other arithmetic, orthonormal(): lax.linalg.triangular_solve(lower, lifted, left_side=True, lower=True)  11.3 us
    dot_general x2, matrix products, shards(): jnp.einsum('rkj,kij->kri', picked, tile_set, preferred_element_type=jnp.f...  7.15 us
    reshape x5, local copies, waits for them, and re-layouts, staged(): return y.reshape((n,) + chunk)  6.63 us
    dot_general x2, matrix products, shards(): jnp.einsum('rki,kij->krj', backward_picked, tile_set, preferred_element_t...  6.15 us

profile of v2, /device:TPU:6, one launch (start us, length us, event | category | flops | bytes accessed | tf_op | source)
XLA Modules:
  0.0 287.2 jit_solution(9713170117022085854)
XLA Ops:
  0.8 1.4 multiply_convert_fusion.refs_0_
  2.1 21.1 %shard_map.64 = bf16[2,4,2,64,128]{4,3,2,1,0:T(8,128)(2,1)} custom-call(bf16[64,128]{1,0:T(8,128)(2,1)} %multiply_convert_fusion.refs_0_), custom_call_target="tpu_custom_call" | custom-call | bytes 1048576 | tf_op jit(solution)/shard_map/pallas_call | solution.py:142
  23.3 1.1 copy.74
  26.0 3.6 %fusion.6 = f32[32,64,256]{2,1,0:T(8,128)S(1)} fusion(bf16[1,1,32,256,256]{4,3,2,1,0:T(8,128)(2,1)} %param.11, bf16[32,64,256]{2,1,0:T(8,128)(2,1)S(1)} %gather_fusion, pred[32]{0:T(512)(128)(4,1)S(1)} %get-tuple-element.14), kind=kOutput, calls=%fused_computation.10 | convolution fusion | flops 268959744 | bytes 7340064 | tf_op jit(solution)/shard_map/rkj,kij->kri/dot_general | solution.py:211
  30.2 2.4 fusion.17
  32.8 1.6 copy.15
  34.4 1.3 fusion.79.refs_1_
  35.7 37.9 %shard_map.65 = bf16[4,4,2,64,64]{4,3,2,1,0:T(8,128)(2,1)} custom-call(f32[4,4,2,64,64]{4,3,2,1,0:T(8,128)} %bitcast.132, f32[1,64]{1,0:T(1,128)} %fusion.79.refs_1_), custom_call_target="tpu_custom_call" | custom-call | bytes 1048576 | tf_op jit(solution)/shard_map/pallas_call | solution.py:142
  73.6 1.4 copy.72
  76.0 3.1 %fusion.4 = f32[32,64,256]{2,1,0:T(8,128)S(1)} fusion(bf16[1,1,32,256,256]{4,3,2,1,0:T(8,128)(2,1)} %param.11, bf16[32,64,256]{2,1,0:T(8,128)(2,1)S(1)} %gather_fusion.1, pred[32]{0:T(512)(128)(4,1)S(1)} %get-tuple-element.6), kind=kOutput, calls=%fused_computation.8 | convolution fusion | flops 268959744 | bytes 7340064 | tf_op jit(solution)/shard_map/rki,kij->krj/dot_general | solution.py:222
  79.1 2.4 fusion.20
  81.5 1.0 copy.18
  83.1 42.5 %shard_map.66 = f32[2,4,2,64,128]{4,3,2,1,0:T(8,128)} custom-call(f32[2,4,2,64,128]{4,3,2,1,0:T(8,128)} %bitcast.135, f32[1,128]{1,0:T(1,128)} %dynamic-slice_bitcast_fusion.refs_1_), custom_call_target="tpu_custom_call" | custom-call | bytes 1048576 | tf_op jit(solution)/shard_map/pallas_call | solution.py:142
  125.6 2.4 convolution_bitcast_fusion.1.refs_0_
  128.0 16.1 %shard_map.67 = f32[64,64]{1,0:T(8,128)} custom-call(f32[64,64]{1,0:T(8,128)} %convolution_bitcast_fusion.1.refs_0_), custom_call_target="tpu_custom_call" | custom-call | bytes 1048576 | tf_op jit(solution)/shard_map/pallas_call | solution.py:142
  145.7 5.8 %cholesky.44 = f32[64,64]{1,0:T(8,128)S(1)} custom-call(f32[64,64]{1,0:T(8,128)S(1)} %fusion.55), custom_call_target="Cholesky" | custom-call | tf_op jit(solution)/shard_map/jit(cholesky)/cholesky | solution.py:170
  152.9 5.1 %custom-call.6 = f32[1,64,64]{1,2,0:T(8,128)S(1)} custom-call(f32[1,64,64]{2,1,0:T(8,128)S(1)} %fusion.50), custom_call_target="InvertDiagBlocksLowerTriangular" | custom-call | tf_op jit(solution)/shard_map/triangular_solve/custom-call.0 | solution.py:171
  157.9 1.4 copy.19
  160.7 3.6 %fusion.2 = f32[32,64,256]{2,1,0:T(8,128)S(1)} fusion(bf16[1,1,32,256,256]{4,3,2,1,0:T(8,128)(2,1)} %param.11, bf16[32,64,256]{2,1,0:T(8,128)(2,1)S(1)} %gather_fusion.2, pred[32]{0:T(512)(128)(4,1)S(1)} %get-tuple-element.14), kind=kOutput, calls=%fused_computation.6 | convolution fusion | flops 268959744 | bytes 7340064 | tf_op jit(solution)/shard_map/rkj,kij->kri/dot_general | solution.py:211
  164.3 2.4 fusion.23
  166.8 1.6 copy.24
  168.5 32.8 %shard_map.68 = bf16[4,4,2,64,64]{4,3,2,1,0:T(8,128)(2,1)} custom-call(f32[4,4,2,64,64]{4,3,2,1,0:T(8,128)} %bitcast.133, f32[1,64]{1,0:T(1,128)} %fusion.79.refs_1_), custom_call_target="tpu_custom_call" | custom-call | bytes 1048576 | tf_op jit(solution)/shard_map/pallas_call | solution.py:142
  201.3 1.4 copy.71
  203.7 3.1 %fusion = f32[32,64,256]{2,1,0:T(8,128)S(1)} fusion(bf16[1,1,32,256,256]{4,3,2,1,0:T(8,128)(2,1)} %param.11, bf16[32,64,256]{2,1,0:T(8,128)(2,1)S(1)} %gather_fusion.3, pred[32]{0:T(512)(128)(4,1)S(1)} %get-tuple-element.6), kind=kOutput, calls=%fused_computation.4 | convolution fusion | flops 268959744 | bytes 7340064 | tf_op jit(solution)/shard_map/rki,kij->krj/dot_general | solution.py:222
  206.8 2.4 fusion.26
  209.2 1.0 copy.27
  210.2 41.1 %shard_map.69 = f32[2,4,2,64,128]{4,3,2,1,0:T(8,128)} custom-call(f32[2,4,2,64,128]{4,3,2,1,0:T(8,128)} %bitcast.137, f32[1,128]{1,0:T(1,128)} %dynamic-slice_bitcast_fusion.refs_1_), custom_call_target="tpu_custom_call" | custom-call | bytes 1048576 | tf_op jit(solution)/shard_map/pallas_call | solution.py:142
  251.3 2.4 convolution_bitcast_fusion.refs_0_
  253.7 16.9 %shard_map.70 = f32[64,64]{1,0:T(8,128)} custom-call(f32[64,64]{1,0:T(8,128)} %convolution_bitcast_fusion.refs_0_), custom_call_target="tpu_custom_call" | custom-call | bytes 1048576 | tf_op jit(solution)/shard_map/pallas_call | solution.py:142
  272.1 6.0 %cholesky.55 = f32[64,64]{1,0:T(8,128)S(1)} custom-call(f32[64,64]{1,0:T(8,128)S(1)} %fusion.53), custom_call_target="Cholesky" | custom-call | tf_op jit(solution)/shard_map/jit(cholesky)/cholesky | solution.py:170
  279.5 4.9 %custom-call.7 = f32[1,64,64]{1,2,0:T(8,128)S(1)} custom-call(f32[1,64,64]{2,1,0:T(8,128)S(1)} %fusion.51), custom_call_target="InvertDiagBlocksLowerTriangular" | custom-call | tf_op jit(solution)/shard_map/triangular_solve/custom-call.0 | solution.py:171
  284.4 1.4 copy.28
  (37 shorter events, 14.0 us)
Async XLA Ops:
  25.9 4.3 %copy-start = (s32[1,1,2,32]{3,2,1,0:T(2,128)S(1)}, s32[1,1,2,32]{3,2,1,0:T(2,128)}, u32[]{:S(2)}) copy-start(s32[1,1,2,32]{3,2,1,0:T(2,128)} %param.12) | copy-start | bytes 772

commit v3 on v2

--- a/solution.py
+++ b/solution.py
@@ -154,8 +154,9 @@
     return y.reshape((n,) + chunk)
 
 
-COL_FACTORS = (2, 4, 4)
-ROW_FACTORS = (2, 4, 2)
+QUERY_FACTORS = (2, 4, 4)
+GRAM_FACTORS = (4, 8)
+ROW_FACTORS = (4, 4)
 
 
 def _query_epilogue(total, s_ref):
@@ -198,6 +199,7 @@
     qchunk = query_degree.shape[0] // n_col
     my_pscale = lax.dynamic_slice_in_dim(pscale, row_at * share, share)
     my_qscale = lax.dynamic_slice_in_dim(qscale, col_at * qchunk, qchunk)
+    dense_qscale = jnp.concatenate([my_qscale, my_qscale])[None, :]
     root_count = math.sqrt(product_degree.shape[0] * n_col)
 
     scaled0 = (panel * my_pscale[None, :]).astype(jnp.bfloat16)
@@ -212,9 +214,10 @@
         partial_sum = jnp.einsum("kq,kri->rqi", row_hot, products, precision=HIGH).reshape(
             width, n_col, qchunk
         )
-        query_pieces = staged(jnp.transpose(partial_sum, (1, 0, 2)), "col", COL_FACTORS, "reduce", 1,
-                              scale=my_qscale[None, :], epilogue=_query_epilogue,
-                              out_dtype=jnp.bfloat16)
+        dense = jnp.transpose(partial_sum, (1, 0, 2)).reshape(n_col, width // 2, 2 * qchunk)
+        query_pieces = staged(dense, "col", QUERY_FACTORS, "reduce", 1,
+                              scale=dense_qscale, epilogue=_query_epilogue,
+                              out_dtype=jnp.bfloat16).reshape(n_col, width, qchunk)
         query_block = jnp.transpose(query_pieces, (1, 0, 2)).reshape(width, query_tiles * side)
         backward_picked = jnp.take(
             query_block.reshape(width, query_tiles, side), slot_ids[0], axis=1
@@ -229,7 +232,7 @@
                                2, scale=my_pscale[None, :], epilogue=_product_epilogue)
         lifted = jnp.transpose(lifted_pieces, (1, 0, 2)).reshape(width, block)
         gram_part = jnp.einsum("ri,si->rs", lifted, lifted, precision=HIGH)
-        gram = staged(gram_part, "col", COL_FACTORS, "sum", 3)
+        gram = staged(gram_part, "col", GRAM_FACTORS, "sum", 3)
         current = orthonormal(lifted, gram)
     mine = lax.dynamic_slice_in_dim(current, row_at * share, share, axis=1)
     return mine * root_count

time: 290 us -> 259 us (0.89)
  Pallas kernels: 208 us -> 179 us
    pallas_call x7, Pallas kernels: 208 us -> 179 us  [staged(): pl.pallas_call(functools.partial(_staged_kernel, axis=axis, factors=tuple...]
    another operation x0 -> x6, local copies, waits for them, and re-layouts: none -> 5.06 us  [the longest x4 3.07 us: shards(): query_pieces = staged(dense, 'col', QUERY_FACTORS, 'reduce', 1, scale=den...]
    reshape x5 -> x3, local copies, waits for them, and re-layouts: 6.63 us -> 3.86 us  [staged(): return y.reshape((n,) + chunk)]
where the time goes in v3:
time: 259 us; the launch traced here: 258 us
  Pallas kernels  179 us (69%)
  other arithmetic  30.7 us (12%)
  matrix products  29 us (11%)
  local copies, waits for them, and re-layouts  18.3 us (7%)
    pallas_call x7, Pallas kernels, staged(): pl.pallas_call(functools.partial(_staged_kernel, axis=axis, factors=tuple...  179 us
    another operation x6, other arithmetic, orthonormal(): lower = jnp.linalg.cholesky(gram)  13.1 us
    another operation x4, other arithmetic, orthonormal(): lax.linalg.triangular_solve(lower, lifted, left_side=True, lower=True)  11.1 us
    dot_general x2, matrix products, shards(): jnp.einsum('rkj,kij->kri', picked, tile_set, preferred_element_type=jnp.f...  7.15 us
    dot_general x2, matrix products, shards(): jnp.einsum('rki,kij->krj', backward_picked, tile_set, preferred_element_t...  6.14 us

profile of v3, /device:TPU:6, one launch (start us, length us, event | category | flops | bytes accessed | tf_op | source)
XLA Modules:
  0.0 257.7 jit_solution(12352710860325229026)
XLA Ops:
  0.8 1.4 multiply_convert_fusion.refs_0_
  2.1 16.2 %shard_map.64 = bf16[4,4,64,128]{3,2,1,0:T(8,128)(2,1)} custom-call(bf16[64,128]{1,0:T(8,128)(2,1)} %multiply_convert_fusion.refs_0_), custom_call_target="tpu_custom_call" | custom-call | bytes 1048576 | tf_op jit(solution)/shard_map/pallas_call | solution.py:142
  18.4 1.1 copy.78
  21.1 3.6 %fusion.6 = f32[32,64,256]{2,1,0:T(8,128)S(1)} fusion(bf16[1,1,32,256,256]{4,3,2,1,0:T(8,128)(2,1)} %param.11, bf16[32,64,256]{2,1,0:T(8,128)(2,1)S(1)} %gather_fusion, pred[32]{0:T(512)(128)(4,1)S(1)} %get-tuple-element.14), kind=kOutput, calls=%fused_computation.10 | convolution fusion | flops 268959744 | bytes 7340064 | tf_op jit(solution)/shard_map/rkj,kij->kri/dot_general | solution.py:213
  25.3 2.4 fusion.17
  28.5 1.0 reshape_reshape.22.refs_0_
  31.0 32.5 %shard_map.65 = bf16[4,4,2,32,128]{4,3,2,1,0:T(8,128)(2,1)} custom-call(f32[4,4,2,32,128]{4,3,2,1,0:T(8,128)} %reshape_reshape.22.refs_0_, f32[1,128]{1,0:T(1,128)} %maximum_bitcast_fusion.refs_1_), custom_call_target="tpu_custom_call" | custom-call | bytes 1048576 | tf_op jit(solution)/shard_map/pallas_call | solution.py:142
  63.4 1.2 reshape_reshape.23
  66.0 3.1 %fusion.4 = f32[32,64,256]{2,1,0:T(8,128)S(1)} fusion(bf16[1,1,32,256,256]{4,3,2,1,0:T(8,128)(2,1)} %param.11, bf16[32,64,256]{2,1,0:T(8,128)(2,1)S(1)} %gather_fusion.1, pred[32]{0:T(512)(128)(4,1)S(1)} %get-tuple-element.6), kind=kOutput, calls=%fused_computation.8 | convolution fusion | flops 268959744 | bytes 7340064 | tf_op jit(solution)/shard_map/rki,kij->krj/dot_general | solution.py:225
  69.1 2.4 fusion.20
  71.5 1.0 copy.18
  73.0 32.4 %shard_map.66 = f32[4,4,64,128]{3,2,1,0:T(8,128)} custom-call(f32[4,4,64,128]{3,2,1,0:T(8,128)} %bitcast.137, f32[1,128]{1,0:T(1,128)} %dynamic-slice_bitcast_fusion.refs_1_), custom_call_target="tpu_custom_call" | custom-call | bytes 1048576 | tf_op jit(solution)/shard_map/pallas_call | solution.py:142
  105.4 2.4 convolution_bitcast_fusion.1.refs_0_
  107.8 20.9 %shard_map.67 = f32[64,64]{1,0:T(8,128)} custom-call(f32[64,64]{1,0:T(8,128)} %convolution_bitcast_fusion.1.refs_0_), custom_call_target="tpu_custom_call" | custom-call | bytes 1048576 | tf_op jit(solution)/shard_map/pallas_call | solution.py:142
  128.7 0.8 copy.22
  130.3 5.9 %cholesky.44 = f32[64,64]{1,0:T(8,128)S(1)} custom-call(f32[64,64]{1,0:T(8,128)S(1)} %fusion.55), custom_call_target="Cholesky" | custom-call | tf_op jit(solution)/shard_map/jit(cholesky)/cholesky | solution.py:171
  137.6 4.9 %custom-call.6 = f32[1,64,64]{1,2,0:T(8,128)S(1)} custom-call(f32[1,64,64]{2,1,0:T(8,128)S(1)} %fusion.50), custom_call_target="InvertDiagBlocksLowerTriangular" | custom-call | tf_op jit(solution)/shard_map/triangular_solve/custom-call.0 | solution.py:172
  142.5 1.4 copy.19
  145.2 3.6 %fusion.2 = f32[32,64,256]{2,1,0:T(8,128)S(1)} fusion(bf16[1,1,32,256,256]{4,3,2,1,0:T(8,128)(2,1)} %param.11, bf16[32,64,256]{2,1,0:T(8,128)(2,1)S(1)} %gather_fusion.2, pred[32]{0:T(512)(128)(4,1)S(1)} %get-tuple-element.14), kind=kOutput, calls=%fused_computation.6 | convolution fusion | flops 268959744 | bytes 7340064 | tf_op jit(solution)/shard_map/rkj,kij->kri/dot_general | solution.py:213
  148.8 2.4 fusion.23
  152.0 1.0 reshape_reshape.25.refs_0_
  153.0 26.0 %shard_map.68 = bf16[4,4,2,32,128]{4,3,2,1,0:T(8,128)(2,1)} custom-call(f32[4,4,2,32,128]{4,3,2,1,0:T(8,128)} %reshape_reshape.25.refs_0_, f32[1,128]{1,0:T(1,128)} %maximum_bitcast_fusion.refs_1_), custom_call_target="tpu_custom_call" | custom-call | bytes 1048576 | tf_op jit(solution)/shard_map/pallas_call | solution.py:142
  179.0 1.2 reshape_reshape.26
  181.5 3.1 %fusion = f32[32,64,256]{2,1,0:T(8,128)S(1)} fusion(bf16[1,1,32,256,256]{4,3,2,1,0:T(8,128)(2,1)} %param.11, bf16[32,64,256]{2,1,0:T(8,128)(2,1)S(1)} %gather_fusion.3, pred[32]{0:T(512)(128)(4,1)S(1)} %get-tuple-element.6), kind=kOutput, calls=%fused_computation.4 | convolution fusion | flops 268959744 | bytes 7340064 | tf_op jit(solution)/shard_map/rki,kij->krj/dot_general | solution.py:225
  184.6 2.4 fusion.26
  187.0 1.0 copy.27
  188.0 29.4 %shard_map.69 = f32[4,4,64,128]{3,2,1,0:T(8,128)} custom-call(f32[4,4,64,128]{3,2,1,0:T(8,128)} %bitcast.138, f32[1,128]{1,0:T(1,128)} %dynamic-slice_bitcast_fusion.refs_1_), custom_call_target="tpu_custom_call" | custom-call | bytes 1048576 | tf_op jit(solution)/shard_map/pallas_call | solution.py:142
  217.4 2.4 convolution_bitcast_fusion.refs_0_
  219.8 21.5 %shard_map.70 = f32[64,64]{1,0:T(8,128)} custom-call(f32[64,64]{1,0:T(8,128)} %convolution_bitcast_fusion.refs_0_), custom_call_target="tpu_custom_call" | custom-call | bytes 1048576 | tf_op jit(solution)/shard_map/pallas_call | solution.py:142
  242.8 5.8 %cholesky.55 = f32[64,64]{1,0:T(8,128)S(1)} custom-call(f32[64,64]{1,0:T(8,128)S(1)} %fusion.53), custom_call_target="Cholesky" | custom-call | tf_op jit(solution)/shard_map/jit(cholesky)/cholesky | solution.py:171
  250.0 4.9 %custom-call.7 = f32[1,64,64]{1,2,0:T(8,128)S(1)} custom-call(f32[1,64,64]{2,1,0:T(8,128)S(1)} %fusion.51), custom_call_target="InvertDiagBlocksLowerTriangular" | custom-call | tf_op jit(solution)/shard_map/triangular_solve/custom-call.0 | solution.py:172
  254.9 1.4 copy.28
  (42 shorter events, 16.5 us)
Async XLA Ops:
  21.1 4.3 %copy-start = (s32[1,1,2,32]{3,2,1,0:T(2,128)S(1)}, s32[1,1,2,32]{3,2,1,0:T(2,128)}, u32[]{:S(2)}) copy-start(s32[1,1,2,32]{3,2,1,0:T(2,128)} %param.12) | copy-start | bytes 772

commit v4 on v3

--- a/solution.py
+++ b/solution.py
@@ -167,6 +167,48 @@
     return total * s_ref[...]
 
 
+def _products_kernel(ids_ref, count_ref, src_ref, tiles_ref, out_ref, *, forward):
+    out_ref[...] = jnp.zeros_like(out_ref)
+    src_row, dst_row = (1, 0) if forward else (0, 1)
+
+    def body(k, carry):
+        @pl.when(k < count_ref[0])
+        def _():
+            x = src_ref[ids_ref[src_row, k]]
+            t = tiles_ref[k]
+            if forward:
+                y = lax.dot_general(x, t, (((1,), (1,)), ((), ())),
+                                    preferred_element_type=jnp.float32)
+            else:
+                y = jnp.dot(x, t, preferred_element_type=jnp.float32)
+            d = ids_ref[dst_row, k]
+            out_ref[d] = out_ref[d] + y
+
+        return carry
+
+    lax.fori_loop(0, tiles_ref.shape[0], body, 0)
+
+
+def tile_products(slot_ids, live_count, src, tile_set, blocks, forward):
+    slots, side, _ = tile_set.shape
+    width = src.shape[1]
+    return pl.pallas_call(
+        functools.partial(_products_kernel, forward=forward),
+        out_shape=jax.ShapeDtypeStruct((blocks, width, side), jnp.float32),
+        in_specs=[
+            pl.BlockSpec(memory_space=pltpu.SMEM),
+            pl.BlockSpec(memory_space=pltpu.SMEM),
+            pl.BlockSpec(memory_space=pltpu.VMEM),
+            pl.BlockSpec(memory_space=pltpu.VMEM),
+        ],
+        out_specs=pl.BlockSpec(memory_space=pltpu.VMEM),
+        cost_estimate=pl.CostEstimate(
+            flops=2 * slots * width * side * side, transcendentals=0,
+            bytes_accessed=slots * side * side * 2 + src.size * 2 + blocks * width * side * 4,
+        ),
+    )(slot_ids, live_count.reshape(1), src, tile_set)
+
+
 def orthonormal(lifted, gram):
     lower = jnp.linalg.cholesky(gram)
     return lax.linalg.triangular_solve(lower, lifted, left_side=True, lower=True)
@@ -176,63 +218,52 @@
     tile_set = tiles[0, 0]
     slot_ids = tile_ids[0, 0]
     live_count = tile_count[0, 0]
-    slots = tile_set.shape[0]
     side = tile_set.shape[1]
     width = panel.shape[0]
     query_tiles = query_degree.shape[0] // side
     product_tiles = product_degree.shape[0] // side
     n_row = lax.axis_size("row")
     n_col = lax.axis_size("col")
-    live_slot = (jnp.arange(slots, dtype=jnp.int32) < live_count).astype(jnp.float32)
-    row_hot = (slot_ids[0][:, None] == jnp.arange(query_tiles, dtype=jnp.int32)[None, :]).astype(
-        jnp.float32
-    ) * live_slot[:, None]
-    col_hot = (slot_ids[1][:, None] == jnp.arange(product_tiles, dtype=jnp.int32)[None, :]).astype(
-        jnp.float32
-    ) * live_slot[:, None]
-    qscale = 1.0 / jnp.sqrt(query_degree.astype(jnp.float32))
-    pscale = 1.0 / jnp.sqrt(product_degree.astype(jnp.float32))
+    qscale = (1.0 / jnp.sqrt(query_degree.astype(jnp.float32))).reshape(query_tiles, 1, side)
+    pscale = (1.0 / jnp.sqrt(product_degree.astype(jnp.float32))).reshape(product_tiles, 1, side)
     row_at = lax.axis_index("row")
     col_at = lax.axis_index("col")
     share = panel.shape[1]
-    block = pscale.shape[0]
-    qchunk = query_degree.shape[0] // n_col
-    my_pscale = lax.dynamic_slice_in_dim(pscale, row_at * share, share)
-    my_qscale = lax.dynamic_slice_in_dim(qscale, col_at * qchunk, qchunk)
-    dense_qscale = jnp.concatenate([my_qscale, my_qscale])[None, :]
+    block = product_degree.shape[0]
+    q_per_tile = n_col // query_tiles
+    p_per_tile = n_row // product_tiles
+    my_qscale = lax.dynamic_index_in_dim(qscale, col_at // q_per_tile, keepdims=False)
+    my_pscale = lax.dynamic_index_in_dim(pscale, row_at // p_per_tile, keepdims=False)
     root_count = math.sqrt(product_degree.shape[0] * n_col)
 
-    scaled0 = (panel * my_pscale[None, :]).astype(jnp.bfloat16)
+    panel_pscale = lax.dynamic_slice_in_dim(pscale.reshape(block), row_at * share, share)
+    scaled0 = (panel * panel_pscale[None, :]).astype(jnp.bfloat16)
     gathered = staged(scaled0, "row", ROW_FACTORS, "gather", 0)
-    scaled_block = jnp.transpose(gathered, (1, 0, 2)).reshape(width, block)
+    per_tile = side // share
+    scaled_tiles = jnp.transpose(
+        gathered.reshape(product_tiles, per_tile, width, share), (0, 2, 1, 3)
+    ).reshape(product_tiles, width, side)
     current = None
     for iteration in range(ITERS):
         if current is not None:
-            scaled_block = (current * pscale[None, :]).astype(jnp.bfloat16)
-        picked = jnp.take(scaled_block.reshape(width, product_tiles, side), slot_ids[1], axis=1)
-        products = jnp.einsum("rkj,kij->kri", picked, tile_set, preferred_element_type=jnp.float32)
-        partial_sum = jnp.einsum("kq,kri->rqi", row_hot, products, precision=HIGH).reshape(
-            width, n_col, qchunk
+            scaled_tiles = (
+                jnp.transpose(current.reshape(width, product_tiles, side), (1, 0, 2)) * pscale
+            ).astype(jnp.bfloat16)
+        partial_sum = tile_products(slot_ids, live_count, scaled_tiles, tile_set, query_tiles, True)
+        query_tiles_panel = staged(
+            partial_sum.reshape(n_col, width // q_per_tile, side), "col", QUERY_FACTORS, "reduce", 1,
+            scale=my_qscale, epilogue=_query_epilogue, out_dtype=jnp.bfloat16,
+        ).reshape(query_tiles, width, side)
+        product_partial = tile_products(
+            slot_ids, live_count, query_tiles_panel, tile_set, product_tiles, False
         )
-        dense = jnp.transpose(partial_sum, (1, 0, 2)).reshape(n_col, width // 2, 2 * qchunk)
-        query_pieces = staged(dense, "col", QUERY_FACTORS, "reduce", 1,
-                              scale=dense_qscale, epilogue=_query_epilogue,
-                              out_dtype=jnp.bfloat16).reshape(n_col, width, qchunk)
-        query_block = jnp.transpose(query_pieces, (1, 0, 2)).reshape(width, query_tiles * side)
-        backward_picked = jnp.take(
-            query_block.reshape(width, query_tiles, side), slot_ids[0], axis=1
-        )
-        backward_products = jnp.einsum(
-            "rki,kij->krj", backward_picked, tile_set, preferred_element_type=jnp.float32
-        )
-        product_partial = jnp.einsum(
-            "kp,krj->rpj", col_hot, backward_products, precision=HIGH
-        ).reshape(width, n_row, share)
-        lifted_pieces = staged(jnp.transpose(product_partial, (1, 0, 2)), "row", ROW_FACTORS, "reduce",
-                               2, scale=my_pscale[None, :], epilogue=_product_epilogue)
-        lifted = jnp.transpose(lifted_pieces, (1, 0, 2)).reshape(width, block)
-        gram_part = jnp.einsum("ri,si->rs", lifted, lifted, precision=HIGH)
+        lifted_tiles = staged(
+            product_partial.reshape(n_row, width // p_per_tile, side), "row", ROW_FACTORS, "reduce", 2,
+            scale=my_pscale, epilogue=_product_epilogue,
+        ).reshape(product_tiles, width, side)
+        gram_part = jnp.einsum("pri,psi->rs", lifted_tiles, lifted_tiles, precision=HIGH)
         gram = staged(gram_part, "col", GRAM_FACTORS, "sum", 3)
+        lifted = jnp.transpose(lifted_tiles, (1, 0, 2)).reshape(width, block)
         current = orthonormal(lifted, gram)
     mine = lax.dynamic_slice_in_dim(current, row_at * share, share, axis=1)
     return mine * root_count

time: 259 us -> 257 us (level)
  Pallas kernels: 179 us -> 211 us
  matrix products: 29 us -> 6.02 us
  local copies, waits for them, and re-layouts: 18.3 us -> 7.12 us
    dot_general x10 -> x2, matrix products: 27.5 us -> 4.76 us  [shards(): jnp.einsum('pri,psi->rs', lifted_tiles, lifted_tiles, precision=HIGH)]
    pallas_call x0 -> x4, Pallas kernels: none -> 18.9 us  [tile_products(): pl.pallas_call(functools.partial(_products_kernel, forward=forward), out_...]
    pallas_call x7, Pallas kernels: 179 us -> 192 us  [staged(): pl.pallas_call(functools.partial(_staged_kernel, axis=axis, factors=tuple...]
    reshape x12 -> x1, local copies, waits for them, and re-layouts: 7.52 us -> 0.87 us  [shards(): scaled_tiles = jnp.transpose(gathered.reshape(product_tiles, per_tile, wi...]
    another operation x12 -> x1, local copies, waits for them, and re-layouts: 5.96 us -> 1.22 us  [shards(): gathered.reshape(product_tiles, per_tile, width, share)]
where the time goes in v4:
time: 257 us; the launch traced here: 254 us
  Pallas kernels  211 us (82%)
  other arithmetic  29.8 us (12%)
  local copies, waits for them, and re-layouts  7.12 us (3%)
  matrix products  6.02 us (2%)
    pallas_call x7, Pallas kernels, staged(): pl.pallas_call(functools.partial(_staged_kernel, axis=axis, factors=tuple...  192 us
    pallas_call x4, Pallas kernels, tile_products(): pl.pallas_call(functools.partial(_products_kernel, forward=forward), out_...  18.9 us
    another operation x6, other arithmetic, orthonormal(): lower = jnp.linalg.cholesky(gram)  13 us
    another operation x4, other arithmetic, orthonormal(): lax.linalg.triangular_solve(lower, lifted, left_side=True, lower=True)  11.1 us

profile of v4, /device:TPU:6, one launch (start us, length us, event | category | flops | bytes accessed | tf_op | source)
XLA Modules:
  0.0 254.3 jit_solution(7281959651841397318)
XLA Ops:
  0.7 0.7 convert_rsqrt_fusion.1
  2.0 0.7 convert_rsqrt_fusion
  3.2 1.4 multiply_convert_fusion.refs_0_
  4.6 16.2 %shard_map.64 = bf16[4,4,64,128]{3,2,1,0:T(8,128)(2,1)} custom-call(bf16[64,128]{1,0:T(8,128)(2,1)} %multiply_convert_fusion.refs_0_), custom_call_target="tpu_custom_call" | custom-call | bytes 1048576 | tf_op jit(solution)/shard_map/pallas_call | solution.py:142
  20.8 1.2 copy.25
  22.1 0.9 reshape.31.src_ref
  22.9 4.8 %shard_map.65 = f32[8,64,256]{2,1,0:T(8,128)} custom-call(s32[2,32]{1,0:T(2,128)} %bitcast.92, s32[1]{0:T(128)} %bitcast.68.count_ref, bf16[8,64,256]{2,1,0:T(8,128)(2,1)} %reshape.31.src_ref, bf16[32,256,256]{2,1,0:T(8,128)(2,1)} %bitcast.72), custom_call_target="tpu_custom_call" | custom-call | flops 268435456 | bytes 4980736 | tf_op jit(solution)/shard_map/pallas_call | solution.py:195
  27.8 36.4 %shard_map.66 = bf16[4,4,2,16,256]{4,3,2,1,0:T(8,128)(2,1)} custom-call(f32[4,4,2,16,256]{4,3,2,1,0:T(8,128)} %bitcast.83, f32[1,256]{1,0:T(1,128)} %dynamic-slice_bitcast_fusion.1.refs_1_), custom_call_target="tpu_custom_call" | custom-call | bytes 1048576 | tf_op jit(solution)/shard_map/pallas_call | solution.py:142
  64.2 4.6 %shard_map.67 = f32[8,64,256]{2,1,0:T(8,128)} custom-call(s32[2,32]{1,0:T(2,128)} %bitcast.93, s32[1]{0:T(128)} %bitcast.69.count_ref, bf16[8,64,256]{2,1,0:T(8,128)(2,1)} %bitcast.88, bf16[32,256,256]{2,1,0:T(8,128)(2,1)} %bitcast.73), custom_call_target="tpu_custom_call" | custom-call | flops 268435456 | bytes 4980736 | tf_op jit(solution)/shard_map/pallas_call | solution.py:195
  68.8 34.4 %shard_map.68 = f32[4,4,32,256]{3,2,1,0:T(8,128)} custom-call(f32[4,4,32,256]{3,2,1,0:T(8,128)} %bitcast.81, f32[1,256]{1,0:T(1,128)} %dynamic-slice_bitcast_fusion.refs_1_), custom_call_target="tpu_custom_call" | custom-call | bytes 1048576 | tf_op jit(solution)/shard_map/pallas_call | solution.py:142
  103.2 2.4 convolution_bitcast_fusion.1.refs_0_
  105.5 22.5 %shard_map.69 = f32[64,64]{1,0:T(8,128)} custom-call(f32[64,64]{1,0:T(8,128)} %convolution_bitcast_fusion.1.refs_0_), custom_call_target="tpu_custom_call" | custom-call | bytes 1048576 | tf_op jit(solution)/shard_map/pallas_call | solution.py:142
  128.1 0.8 copy.11
  128.9 0.8 fusion.9
  129.7 5.8 %cholesky.44 = f32[64,64]{1,0:T(8,128)S(1)} custom-call(f32[64,64]{1,0:T(8,128)S(1)} %fusion.9), custom_call_target="Cholesky" | custom-call | tf_op jit(solution)/shard_map/jit(cholesky)/cholesky | solution.py:213
  135.5 0.6 compare_reduce_fusion.1
  136.2 0.7 fusion.2
  136.9 4.9 %custom-call.6 = f32[1,64,64]{1,2,0:T(8,128)S(1)} custom-call(f32[1,64,64]{2,1,0:T(8,128)S(1)} %fusion.2), custom_call_target="InvertDiagBlocksLowerTriangular" | custom-call | tf_op jit(solution)/shard_map/triangular_solve/custom-call.0 | solution.py:214
  141.8 1.1 copy.17
  143.5 0.8 fusion.1.src_ref
  144.2 4.8 %shard_map.70 = f32[8,64,256]{2,1,0:T(8,128)} custom-call(s32[2,32]{1,0:T(2,128)} %bitcast.94, s32[1]{0:T(128)} %bitcast.70.count_ref, bf16[8,64,256]{2,1,0:T(8,128)(2,1)} %fusion.1.src_ref, bf16[32,256,256]{2,1,0:T(8,128)(2,1)} %bitcast.74), custom_call_target="tpu_custom_call" | custom-call | flops 268435456 | bytes 4980736 | tf_op jit(solution)/shard_map/pallas_call | solution.py:195
  149.1 30.6 %shard_map.71 = bf16[4,4,2,16,256]{4,3,2,1,0:T(8,128)(2,1)} custom-call(f32[4,4,2,16,256]{4,3,2,1,0:T(8,128)} %bitcast.82, f32[1,256]{1,0:T(1,128)} %dynamic-slice_bitcast_fusion.1.refs_1_), custom_call_target="tpu_custom_call" | custom-call | bytes 1048576 | tf_op jit(solution)/shard_map/pallas_call | solution.py:142
  179.7 4.6 %shard_map.72 = f32[8,64,256]{2,1,0:T(8,128)} custom-call(s32[2,32]{1,0:T(2,128)} %bitcast.95, s32[1]{0:T(128)} %bitcast.71.count_ref, bf16[8,64,256]{2,1,0:T(8,128)(2,1)} %bitcast.87, bf16[32,256,256]{2,1,0:T(8,128)(2,1)} %bitcast.75), custom_call_target="tpu_custom_call" | custom-call | flops 268435456 | bytes 4980736 | tf_op jit(solution)/shard_map/pallas_call | solution.py:195
  184.2 31.1 %shard_map.73 = f32[4,4,32,256]{3,2,1,0:T(8,128)} custom-call(f32[4,4,32,256]{3,2,1,0:T(8,128)} %bitcast.80, f32[1,256]{1,0:T(1,128)} %dynamic-slice_bitcast_fusion.refs_1_), custom_call_target="tpu_custom_call" | custom-call | bytes 1048576 | tf_op jit(solution)/shard_map/pallas_call | solution.py:142
  215.3 2.4 convolution_bitcast_fusion.refs_0_
  217.7 20.5 %shard_map.74 = f32[64,64]{1,0:T(8,128)} custom-call(f32[64,64]{1,0:T(8,128)} %convolution_bitcast_fusion.refs_0_), custom_call_target="tpu_custom_call" | custom-call | bytes 1048576 | tf_op jit(solution)/shard_map/pallas_call | solution.py:142
  238.2 0.8 copy.14
  239.1 0.8 fusion.6
  239.9 5.8 %cholesky.55 = f32[64,64]{1,0:T(8,128)S(1)} custom-call(f32[64,64]{1,0:T(8,128)S(1)} %fusion.6), custom_call_target="Cholesky" | custom-call | tf_op jit(solution)/shard_map/jit(cholesky)/cholesky | solution.py:213
  246.4 0.7 fusion.3
  247.0 4.9 %custom-call.7 = f32[1,64,64]{1,2,0:T(8,128)S(1)} custom-call(f32[1,64,64]{2,1,0:T(8,128)S(1)} %fusion.3), custom_call_target="InvertDiagBlocksLowerTriangular" | custom-call | tf_op jit(solution)/shard_map/triangular_solve/custom-call.0 | solution.py:214
  251.9 1.1 copy.18
  (10 shorter events, 3.8 us)

commit v5 on v4

--- a/solution.py
+++ b/solution.py
@@ -44,13 +44,6 @@
 
     def other(s, k):
         return lax.rem(mine[s] + k, factors[s])
-
-    barrier = pltpu.get_barrier_semaphore()
-    for s in range(stages):
-        for k in range(1, factors[s]):
-            pl.semaphore_signal(barrier, inc=1, device_id=_device(axis, peer_of(s, other(s, k))),
-                                device_id_type=pl.DeviceIdType.MESH)
-    pl.semaphore_wait(barrier, sum(f - 1 for f in factors))
 
     def exchange_stage(kind, s, src_of, dst_of):
         copies = []
@@ -146,7 +139,7 @@
         in_specs=[pl.BlockSpec(memory_space=pltpu.VMEM)] * len(args),
         out_specs=pl.BlockSpec(memory_space=pltpu.VMEM),
         scratch_shapes=scratch,
-        compiler_params=pltpu.CompilerParams(collective_id=cid, has_side_effects=True),
+        compiler_params=pltpu.CompilerParams(has_side_effects=True),
         cost_estimate=pl.CostEstimate(flops=0, transcendentals=0, bytes_accessed=2 * nbytes),
     )(*args)
     if mode == "sum":
@@ -167,7 +160,20 @@
     return total * s_ref[...]
 
 
-def _products_kernel(ids_ref, count_ref, src_ref, tiles_ref, out_ref, *, forward):
+GROUP = 4
+
+
+def _products_kernel(ids_ref, count_ref, src_ref, tiles_hbm, out_ref, tiles, sems, *, forward):
+    slots = tiles.shape[0]
+    groups = slots // GROUP
+
+    def fetch(g):
+        return pltpu.make_async_copy(
+            tiles_hbm.at[pl.ds(g * GROUP, GROUP)], tiles.at[pl.ds(g * GROUP, GROUP)], sems.at[g]
+        )
+
+    for g in range(groups):
+        fetch(g).start()
     out_ref[...] = jnp.zeros_like(out_ref)
     src_row, dst_row = (1, 0) if forward else (0, 1)
 
@@ -175,7 +181,7 @@
         @pl.when(k < count_ref[0])
         def _():
             x = src_ref[ids_ref[src_row, k]]
-            t = tiles_ref[k]
+            t = tiles[k]
             if forward:
                 y = lax.dot_general(x, t, (((1,), (1,)), ((), ())),
                                     preferred_element_type=jnp.float32)
@@ -186,7 +192,9 @@
 
         return carry
 
-    lax.fori_loop(0, tiles_ref.shape[0], body, 0)
+    for g in range(groups):
+        fetch(g).wait()
+        lax.fori_loop(g * GROUP, (g + 1) * GROUP, body, 0)
 
 
 def tile_products(slot_ids, live_count, src, tile_set, blocks, forward):
@@ -199,9 +207,13 @@
             pl.BlockSpec(memory_space=pltpu.SMEM),
             pl.BlockSpec(memory_space=pltpu.SMEM),
             pl.BlockSpec(memory_space=pltpu.VMEM),
-            pl.BlockSpec(memory_space=pltpu.VMEM),
+            pl.BlockSpec(memory_space=pl.ANY),
         ],
         out_specs=pl.BlockSpec(memory_space=pltpu.VMEM),
+        scratch_shapes=[
+            pltpu.VMEM(tile_set.shape, tile_set.dtype),
+            pltpu.SemaphoreType.DMA((slots // GROUP,)),
+        ],
         cost_estimate=pl.CostEstimate(
             flops=2 * slots * width * side * side, transcendentals=0,
             bytes_accessed=slots * side * side * 2 + src.size * 2 + blocks * width * side * 4,

time: 257 us -> 338 us (1.32)
  Pallas kernels: 211 us -> 290 us
    pallas_call x7, Pallas kernels: 192 us -> 262 us  [staged(): pl.pallas_call(functools.partial(_staged_kernel, axis=axis, factors=tuple...]
    pallas_call x4, Pallas kernels: 18.9 us -> 28 us  [tile_products(): pl.pallas_call(functools.partial(_products_kernel, forward=forward), out_...]
where the time goes in v5:
time: 338 us; the launch traced here: 334 us
  Pallas kernels  290 us (86%)
  other arithmetic  29.8 us (9%)
  local copies, waits for them, and re-layouts  7.12 us (2%)
  matrix products  6.02 us (2%)
    pallas_call x7, Pallas kernels, staged(): pl.pallas_call(functools.partial(_staged_kernel, axis=axis, factors=tuple...  262 us
    pallas_call x4, Pallas kernels, tile_products(): pl.pallas_call(functools.partial(_products_kernel, forward=forward), out_...  28 us
    another operation x6, other arithmetic, orthonormal(): lower = jnp.linalg.cholesky(gram)  13 us
    another operation x4, other arithmetic, orthonormal(): lax.linalg.triangular_solve(lower, lifted, left_side=True, lower=True)  11.1 us

profile of v5, /device:TPU:6, one launch (start us, length us, event | category | flops | bytes accessed | tf_op | source)
XLA Modules:
  0.0 334.2 jit_solution(48272224070509750)
XLA Ops:
  0.7 0.7 convert_rsqrt_fusion.1
  2.0 0.7 convert_rsqrt_fusion
  3.2 1.4 multiply_convert_fusion.refs_0_
  4.6 32.3 %shard_map.64 = bf16[4,4,64,128]{3,2,1,0:T(8,128)(2,1)} custom-call(bf16[64,128]{1,0:T(8,128)(2,1)} %multiply_convert_fusion.refs_0_), custom_call_target="tpu_custom_call" | custom-call | bytes 1048576 | tf_op jit(solution)/shard_map/pallas_call | solution.py:135
  36.9 1.2 copy.25
  38.1 0.9 reshape.31.src_ref
  39.0 7.4 %shard_map.65 = f32[8,64,256]{2,1,0:T(8,128)} custom-call(s32[2,32]{1,0:T(2,128)} %bitcast.92, s32[1]{0:T(128)} %bitcast.68.count_ref, bf16[8,64,256]{2,1,0:T(8,128)(2,1)} %reshape.31.src_ref, bf16[32,256,256]{2,1,0:T(8,128)(2,1)} %bitcast.72), custom_call_target="tpu_custom_call" | custom-call | flops 268435456 | bytes 4980736 | tf_op jit(solution)/shard_map/pallas_call | solution.py:203
  46.4 39.0 %shard_map.66 = bf16[4,4,2,16,256]{4,3,2,1,0:T(8,128)(2,1)} custom-call(f32[4,4,2,16,256]{4,3,2,1,0:T(8,128)} %bitcast.83, f32[1,256]{1,0:T(1,128)} %dynamic-slice_bitcast_fusion.1.refs_1_), custom_call_target="tpu_custom_call" | custom-call | bytes 1048576 | tf_op jit(solution)/shard_map/pallas_call | solution.py:135
  85.4 6.6 %shard_map.67 = f32[8,64,256]{2,1,0:T(8,128)} custom-call(s32[2,32]{1,0:T(2,128)} %bitcast.93, s32[1]{0:T(128)} %bitcast.69.count_ref, bf16[8,64,256]{2,1,0:T(8,128)(2,1)} %bitcast.88, bf16[32,256,256]{2,1,0:T(8,128)(2,1)} %bitcast.73), custom_call_target="tpu_custom_call" | custom-call | flops 268435456 | bytes 4980736 | tf_op jit(solution)/shard_map/pallas_call | solution.py:203
  92.0 41.6 %shard_map.68 = f32[4,4,32,256]{3,2,1,0:T(8,128)} custom-call(f32[4,4,32,256]{3,2,1,0:T(8,128)} %bitcast.81, f32[1,256]{1,0:T(1,128)} %dynamic-slice_bitcast_fusion.refs_1_), custom_call_target="tpu_custom_call" | custom-call | bytes 1048576 | tf_op jit(solution)/shard_map/pallas_call | solution.py:135
  133.6 2.4 convolution_bitcast_fusion.1.refs_0_
  136.0 34.7 %shard_map.69 = f32[64,64]{1,0:T(8,128)} custom-call(f32[64,64]{1,0:T(8,128)} %convolution_bitcast_fusion.1.refs_0_), custom_call_target="tpu_custom_call" | custom-call | bytes 1048576 | tf_op jit(solution)/shard_map/pallas_call | solution.py:135
  170.7 0.8 copy.11
  171.5 0.8 fusion.9
  172.3 5.8 %cholesky.44 = f32[64,64]{1,0:T(8,128)S(1)} custom-call(f32[64,64]{1,0:T(8,128)S(1)} %fusion.9), custom_call_target="Cholesky" | custom-call | tf_op jit(solution)/shard_map/jit(cholesky)/cholesky | solution.py:225
  178.2 0.6 compare_reduce_fusion.1
  178.8 0.7 fusion.2
  179.5 4.9 %custom-call.6 = f32[1,64,64]{1,2,0:T(8,128)S(1)} custom-call(f32[1,64,64]{2,1,0:T(8,128)S(1)} %fusion.2), custom_call_target="InvertDiagBlocksLowerTriangular" | custom-call | tf_op jit(solution)/shard_map/triangular_solve/custom-call.0 | solution.py:226
  184.4 1.1 copy.17
  186.1 0.8 fusion.1.src_ref
  186.9 7.4 %shard_map.70 = f32[8,64,256]{2,1,0:T(8,128)} custom-call(s32[2,32]{1,0:T(2,128)} %bitcast.94, s32[1]{0:T(128)} %bitcast.70.count_ref, bf16[8,64,256]{2,1,0:T(8,128)(2,1)} %fusion.1.src_ref, bf16[32,256,256]{2,1,0:T(8,128)(2,1)} %bitcast.74), custom_call_target="tpu_custom_call" | custom-call | flops 268435456 | bytes 4980736 | tf_op jit(solution)/shard_map/pallas_call | solution.py:203
  194.3 38.5 %shard_map.71 = bf16[4,4,2,16,256]{4,3,2,1,0:T(8,128)(2,1)} custom-call(f32[4,4,2,16,256]{4,3,2,1,0:T(8,128)} %bitcast.82, f32[1,256]{1,0:T(1,128)} %dynamic-slice_bitcast_fusion.1.refs_1_), custom_call_target="tpu_custom_call" | custom-call | bytes 1048576 | tf_op jit(solution)/shard_map/pallas_call | solution.py:135
  232.8 6.6 %shard_map.72 = f32[8,64,256]{2,1,0:T(8,128)} custom-call(s32[2,32]{1,0:T(2,128)} %bitcast.95, s32[1]{0:T(128)} %bitcast.71.count_ref, bf16[8,64,256]{2,1,0:T(8,128)(2,1)} %bitcast.87, bf16[32,256,256]{2,1,0:T(8,128)(2,1)} %bitcast.75), custom_call_target="tpu_custom_call" | custom-call | flops 268435456 | bytes 4980736 | tf_op jit(solution)/shard_map/pallas_call | solution.py:203
  239.4 41.6 %shard_map.73 = f32[4,4,32,256]{3,2,1,0:T(8,128)} custom-call(f32[4,4,32,256]{3,2,1,0:T(8,128)} %bitcast.80, f32[1,256]{1,0:T(1,128)} %dynamic-slice_bitcast_fusion.refs_1_), custom_call_target="tpu_custom_call" | custom-call | bytes 1048576 | tf_op jit(solution)/shard_map/pallas_call | solution.py:135
  281.0 2.4 convolution_bitcast_fusion.refs_0_
  283.4 34.7 %shard_map.74 = f32[64,64]{1,0:T(8,128)} custom-call(f32[64,64]{1,0:T(8,128)} %convolution_bitcast_fusion.refs_0_), custom_call_target="tpu_custom_call" | custom-call | bytes 1048576 | tf_op jit(solution)/shard_map/pallas_call | solution.py:135
  318.1 0.8 copy.14
  319.0 0.8 fusion.6
  319.7 5.8 %cholesky.55 = f32[64,64]{1,0:T(8,128)S(1)} custom-call(f32[64,64]{1,0:T(8,128)S(1)} %fusion.6), custom_call_target="Cholesky" | custom-call | tf_op jit(solution)/shard_map/jit(cholesky)/cholesky | solution.py:225
  326.3 0.7 fusion.3
  326.9 4.9 %custom-call.7 = f32[1,64,64]{1,2,0:T(8,128)S(1)} custom-call(f32[1,64,64]{2,1,0:T(8,128)S(1)} %fusion.3), custom_call_target="InvertDiagBlocksLowerTriangular" | custom-call | tf_op jit(solution)/shard_map/triangular_solve/custom-call.0 | solution.py:226
  331.8 1.1 copy.18
  (10 shorter events, 3.8 us)

commit v6 on v5

--- a/solution.py
+++ b/solution.py
@@ -44,6 +44,13 @@
 
     def other(s, k):
         return lax.rem(mine[s] + k, factors[s])
+
+    barrier = pltpu.get_barrier_semaphore()
+    for s in range(stages):
+        for k in range(1, factors[s]):
+            pl.semaphore_signal(barrier, inc=1, device_id=_device(axis, peer_of(s, other(s, k))),
+                                device_id_type=pl.DeviceIdType.MESH)
+    pl.semaphore_wait(barrier, sum(f - 1 for f in factors))
 
     def exchange_stage(kind, s, src_of, dst_of):
         copies = []
@@ -139,7 +146,7 @@
         in_specs=[pl.BlockSpec(memory_space=pltpu.VMEM)] * len(args),
         out_specs=pl.BlockSpec(memory_space=pltpu.VMEM),
         scratch_shapes=scratch,
-        compiler_params=pltpu.CompilerParams(has_side_effects=True),
+        compiler_params=pltpu.CompilerParams(collective_id=cid, has_side_effects=True),
         cost_estimate=pl.CostEstimate(flops=0, transcendentals=0, bytes_accessed=2 * nbytes),
     )(*args)
     if mode == "sum":
@@ -176,10 +183,11 @@
         fetch(g).start()
     out_ref[...] = jnp.zeros_like(out_ref)
     src_row, dst_row = (1, 0) if forward else (0, 1)
-
-    def body(k, carry):
-        @pl.when(k < count_ref[0])
-        def _():
+    count = count_ref[0]
+    for g in range(groups):
+        fetch(g).wait()
+        ys = []
+        for k in range(g * GROUP, (g + 1) * GROUP):
             x = src_ref[ids_ref[src_row, k]]
             t = tiles[k]
             if forward:
@@ -187,14 +195,10 @@
                                     preferred_element_type=jnp.float32)
             else:
                 y = jnp.dot(x, t, preferred_element_type=jnp.float32)
+            ys.append(jnp.where(k < count, y, 0.0))
+        for k, y in zip(range(g * GROUP, (g + 1) * GROUP), ys):
             d = ids_ref[dst_row, k]
             out_ref[d] = out_ref[d] + y
-
-        return carry
-
-    for g in range(groups):
-        fetch(g).wait()
-        lax.fori_loop(g * GROUP, (g + 1) * GROUP, body, 0)
 
 
 def tile_products(slot_ids, live_count, src, tile_set, blocks, forward):

time: 338 us -> 244 us (0.72)
  Pallas kernels: 290 us -> 199 us
    pallas_call x7, Pallas kernels: 262 us -> 179 us  [staged(): pl.pallas_call(functools.partial(_staged_kernel, axis=axis, factors=tuple...]
    pallas_call x4, Pallas kernels: 28 us -> 19.6 us  [tile_products(): pl.pallas_call(functools.partial(_products_kernel, forward=forward), out_...]
where the time goes in v6:
time: 244 us; the launch traced here: 243 us
  Pallas kernels  199 us (82%)
  other arithmetic  29.8 us (12%)
  local copies, waits for them, and re-layouts  7.12 us (3%)
  matrix products  6.02 us (2%)
    pallas_call x7, Pallas kernels, staged(): pl.pallas_call(functools.partial(_staged_kernel, axis=axis, factors=tuple...  179 us
    pallas_call x4, Pallas kernels, tile_products(): pl.pallas_call(functools.partial(_products_kernel, forward=forward), out_...  19.6 us
    another operation x6, other arithmetic, orthonormal(): lower = jnp.linalg.cholesky(gram)  13 us
    another operation x4, other arithmetic, orthonormal(): lax.linalg.triangular_solve(lower, lifted, left_side=True, lower=True)  11.1 us

profile of v6, /device:TPU:6, one launch (start us, length us, event | category | flops | bytes accessed | tf_op | source)
XLA Modules:
  0.0 242.8 jit_solution(18352128624745266873)
XLA Ops:
  0.7 0.7 convert_rsqrt_fusion.1
  2.0 0.7 convert_rsqrt_fusion
  3.2 1.4 multiply_convert_fusion.refs_0_
  4.6 16.2 %shard_map.64 = bf16[4,4,64,128]{3,2,1,0:T(8,128)(2,1)} custom-call(bf16[64,128]{1,0:T(8,128)(2,1)} %multiply_convert_fusion.refs_0_), custom_call_target="tpu_custom_call" | custom-call | bytes 1048576 | tf_op jit(solution)/shard_map/pallas_call | solution.py:142
  20.8 1.2 copy.25
  22.1 0.9 reshape.31.src_ref
  22.9 5.2 %shard_map.65 = f32[8,64,256]{2,1,0:T(8,128)} custom-call(s32[2,32]{1,0:T(2,128)} %bitcast.92, s32[1]{0:T(128)} %bitcast.68.count_ref, bf16[8,64,256]{2,1,0:T(8,128)(2,1)} %reshape.31.src_ref, bf16[32,256,256]{2,1,0:T(8,128)(2,1)} %bitcast.72), custom_call_target="tpu_custom_call" | custom-call | flops 268435456 | bytes 4980736 | tf_op jit(solution)/shard_map/pallas_call | solution.py:207
  28.2 32.5 %shard_map.66 = bf16[4,4,2,16,256]{4,3,2,1,0:T(8,128)(2,1)} custom-call(f32[4,4,2,16,256]{4,3,2,1,0:T(8,128)} %bitcast.83, f32[1,256]{1,0:T(1,128)} %dynamic-slice_bitcast_fusion.1.refs_1_), custom_call_target="tpu_custom_call" | custom-call | bytes 1048576 | tf_op jit(solution)/shard_map/pallas_call | solution.py:142
  60.7 4.6 %shard_map.67 = f32[8,64,256]{2,1,0:T(8,128)} custom-call(s32[2,32]{1,0:T(2,128)} %bitcast.93, s32[1]{0:T(128)} %bitcast.69.count_ref, bf16[8,64,256]{2,1,0:T(8,128)(2,1)} %bitcast.88, bf16[32,256,256]{2,1,0:T(8,128)(2,1)} %bitcast.73), custom_call_target="tpu_custom_call" | custom-call | flops 268435456 | bytes 4980736 | tf_op jit(solution)/shard_map/pallas_call | solution.py:207
  65.3 32.4 %shard_map.68 = f32[4,4,32,256]{3,2,1,0:T(8,128)} custom-call(f32[4,4,32,256]{3,2,1,0:T(8,128)} %bitcast.81, f32[1,256]{1,0:T(1,128)} %dynamic-slice_bitcast_fusion.refs_1_), custom_call_target="tpu_custom_call" | custom-call | bytes 1048576 | tf_op jit(solution)/shard_map/pallas_call | solution.py:142
  97.7 2.4 convolution_bitcast_fusion.1.refs_0_
  100.1 20.6 %shard_map.69 = f32[64,64]{1,0:T(8,128)} custom-call(f32[64,64]{1,0:T(8,128)} %convolution_bitcast_fusion.1.refs_0_), custom_call_target="tpu_custom_call" | custom-call | bytes 1048576 | tf_op jit(solution)/shard_map/pallas_call | solution.py:142
  120.6 0.8 copy.11
  121.4 0.8 fusion.9
  122.2 5.8 %cholesky.44 = f32[64,64]{1,0:T(8,128)S(1)} custom-call(f32[64,64]{1,0:T(8,128)S(1)} %fusion.9), custom_call_target="Cholesky" | custom-call | tf_op jit(solution)/shard_map/jit(cholesky)/cholesky | solution.py:229
  128.1 0.6 compare_reduce_fusion.1
  128.7 0.7 fusion.2
  129.4 4.9 %custom-call.6 = f32[1,64,64]{1,2,0:T(8,128)S(1)} custom-call(f32[1,64,64]{2,1,0:T(8,128)S(1)} %fusion.2), custom_call_target="InvertDiagBlocksLowerTriangular" | custom-call | tf_op jit(solution)/shard_map/triangular_solve/custom-call.0 | solution.py:230
  134.3 1.1 copy.17
  136.0 0.8 fusion.1.src_ref
  136.8 5.2 %shard_map.70 = f32[8,64,256]{2,1,0:T(8,128)} custom-call(s32[2,32]{1,0:T(2,128)} %bitcast.94, s32[1]{0:T(128)} %bitcast.70.count_ref, bf16[8,64,256]{2,1,0:T(8,128)(2,1)} %fusion.1.src_ref, bf16[32,256,256]{2,1,0:T(8,128)(2,1)} %bitcast.74), custom_call_target="tpu_custom_call" | custom-call | flops 268435456 | bytes 4980736 | tf_op jit(solution)/shard_map/pallas_call | solution.py:207
  142.0 26.5 %shard_map.71 = bf16[4,4,2,16,256]{4,3,2,1,0:T(8,128)(2,1)} custom-call(f32[4,4,2,16,256]{4,3,2,1,0:T(8,128)} %bitcast.82, f32[1,256]{1,0:T(1,128)} %dynamic-slice_bitcast_fusion.1.refs_1_), custom_call_target="tpu_custom_call" | custom-call | bytes 1048576 | tf_op jit(solution)/shard_map/pallas_call | solution.py:142
  168.5 4.6 %shard_map.72 = f32[8,64,256]{2,1,0:T(8,128)} custom-call(s32[2,32]{1,0:T(2,128)} %bitcast.95, s32[1]{0:T(128)} %bitcast.71.count_ref, bf16[8,64,256]{2,1,0:T(8,128)(2,1)} %bitcast.87, bf16[32,256,256]{2,1,0:T(8,128)(2,1)} %bitcast.75), custom_call_target="tpu_custom_call" | custom-call | flops 268435456 | bytes 4980736 | tf_op jit(solution)/shard_map/pallas_call | solution.py:207
  173.1 29.8 %shard_map.73 = f32[4,4,32,256]{3,2,1,0:T(8,128)} custom-call(f32[4,4,32,256]{3,2,1,0:T(8,128)} %bitcast.80, f32[1,256]{1,0:T(1,128)} %dynamic-slice_bitcast_fusion.refs_1_), custom_call_target="tpu_custom_call" | custom-call | bytes 1048576 | tf_op jit(solution)/shard_map/pallas_call | solution.py:142
  202.9 2.4 convolution_bitcast_fusion.refs_0_
  205.3 21.5 %shard_map.74 = f32[64,64]{1,0:T(8,128)} custom-call(f32[64,64]{1,0:T(8,128)} %convolution_bitcast_fusion.refs_0_), custom_call_target="tpu_custom_call" | custom-call | bytes 1048576 | tf_op jit(solution)/shard_map/pallas_call | solution.py:142
  226.7 0.8 copy.14
  227.6 0.8 fusion.6
  228.4 5.8 %cholesky.55 = f32[64,64]{1,0:T(8,128)S(1)} custom-call(f32[64,64]{1,0:T(8,128)S(1)} %fusion.6), custom_call_target="Cholesky" | custom-call | tf_op jit(solution)/shard_map/jit(cholesky)/cholesky | solution.py:229
  234.9 0.7 fusion.3
  235.5 4.9 %custom-call.7 = f32[1,64,64]{1,2,0:T(8,128)S(1)} custom-call(f32[1,64,64]{2,1,0:T(8,128)S(1)} %fusion.3), custom_call_target="InvertDiagBlocksLowerTriangular" | custom-call | tf_op jit(solution)/shard_map/triangular_solve/custom-call.0 | solution.py:230
  240.4 1.1 copy.18
  (10 shorter events, 3.8 us)

commit v7 on v6

--- a/solution.py
+++ b/solution.py
@@ -20,6 +20,100 @@
     if axis == "row":
         return (peer, lax.axis_index("col"))
     return (lax.axis_index("row"), peer)
+
+
+class _Plan:
+    def __init__(self, axis, factors):
+        self.axis = axis
+        self.factors = tuple(factors)
+        self.stages = len(factors)
+        self.me = lax.axis_index(axis)
+        self.strides = [math.prod(factors[:s]) for s in range(self.stages)]
+        self.mine = [lax.rem(lax.div(self.me, self.strides[s]), factors[s])
+                     for s in range(self.stages)]
+
+    def peer(self, s, d):
+        return _device(self.axis, self.me + (d - self.mine[s]) * self.strides[s])
+
+    def other(self, s, k):
+        return lax.rem(self.mine[s] + k, self.factors[s])
+
+    def peers(self):
+        return [self.peer(s, self.other(s, k)) for s in range(self.stages)
+                for k in range(1, self.factors[s])]
+
+
+def _barrier(plans):
+    barrier = pltpu.get_barrier_semaphore()
+    count = 0
+    for plan in plans:
+        for dev in plan.peers():
+            pl.semaphore_signal(barrier, inc=1, device_id=dev, device_id_type=pl.DeviceIdType.MESH)
+            count += 1
+    pl.semaphore_wait(barrier, count)
+
+
+def _exchange(plan, sems, kind, s, src_of, dst_of):
+    copies = []
+    mine = plan.mine[s]
+    for k in range(1, plan.factors[s]):
+        d = plan.other(s, k)
+        c = pltpu.make_async_remote_copy(
+            src_ref=src_of(d), dst_ref=dst_of(mine),
+            send_sem=sems.at[kind, s, d], recv_sem=sems.at[kind + 1, s, mine],
+            device_id=plan.peer(s, d), device_id_type=pl.DeviceIdType.MESH,
+        )
+        c.start()
+        copies.append((d, c))
+    for d, c in copies:
+        c.wait_send()
+        pltpu.make_async_remote_copy(
+            src_ref=src_of(d), dst_ref=dst_of(d),
+            send_sem=sems.at[kind, s, d], recv_sem=sems.at[kind + 1, s, d],
+            device_id=plan.peer(s, d), device_id_type=pl.DeviceIdType.MESH,
+        ).wait_recv()
+
+
+def _reduce_scatter(plan, sems, kind, x_ref, rbufs):
+    cur = x_ref
+    for s in range(plan.stages):
+        lead = plan.stages - 1 - s
+
+        def src_of(d, cur=cur, lead=lead):
+            return cur.at[(slice(None),) * lead + (d,)]
+
+        rb = rbufs[s]
+        _exchange(plan, sems, kind, s, src_of, lambda d, rb=rb: rb.at[d])
+        total = cur[(slice(None),) * lead + (plan.mine[s],)]
+        for k in range(1, plan.factors[s]):
+            total = total + rb[plan.other(s, k)]
+        rb[plan.mine[s]] = total
+        cur = rb.at[plan.mine[s]]
+    return cur
+
+
+def _all_gather(plan, sems, kind, gbuf, own):
+    mine = plan.mine
+    gbuf[tuple(mine[::-1])] = own.astype(gbuf.dtype)
+    for s in reversed(range(plan.stages)):
+        lead = plan.stages - 1 - s
+
+        def view(d, s=s, lead=lead):
+            return gbuf.at[(slice(None),) * lead + (d,) + tuple(mine[s - 1::-1] if s else ())]
+
+        _exchange(plan, sems, kind, s, lambda d, s=s: view(mine[s]), view)
+
+
+def _sum(plan, sems, kind, value, rbufs):
+    for s in range(plan.stages):
+        rb = rbufs[s]
+        rb[plan.mine[s]] = value
+        src = rb.at[plan.mine[s]]
+        _exchange(plan, sems, kind, s, lambda d, src=src: src, lambda d, rb=rb: rb.at[d])
+        value = rb[0]
+        for d in range(1, plan.factors[s]):
+            value = value + rb[d]
+    return value
 
 
 def _staged_kernel(*refs, axis, factors, mode, has_scale, epilogue):
@@ -30,90 +124,77 @@
         x_ref, y_ref = refs[:2]
         s_ref = None
         rest = refs[2:]
-    stages = len(factors)
-    n_rs = stages if mode in ("reduce", "sum") else 0
+    plan = _Plan(axis, factors)
+    n_rs = plan.stages if mode in ("reduce", "sum") else 0
     rbufs = rest[:n_rs]
     gbuf = rest[n_rs] if mode != "sum" else None
     sems = rest[-1]
-    me = lax.axis_index(axis)
-    strides = [math.prod(factors[:s]) for s in range(stages)]
-    mine = [lax.rem(lax.div(me, strides[s]), factors[s]) for s in range(stages)]
-
-    def peer_of(s, d):
-        return me + (d - mine[s]) * strides[s]
-
-    def other(s, k):
-        return lax.rem(mine[s] + k, factors[s])
-
-    barrier = pltpu.get_barrier_semaphore()
-    for s in range(stages):
-        for k in range(1, factors[s]):
-            pl.semaphore_signal(barrier, inc=1, device_id=_device(axis, peer_of(s, other(s, k))),
-                                device_id_type=pl.DeviceIdType.MESH)
-    pl.semaphore_wait(barrier, sum(f - 1 for f in factors))
-
-    def exchange_stage(kind, s, src_of, dst_of):
-        copies = []
-        for k in range(1, factors[s]):
-            d = other(s, k)
-            c = pltpu.make_async_remote_copy(
-                src_ref=src_of(d), dst_ref=dst_of(mine[s]),
-                send_sem=sems.at[kind, s, d], recv_sem=sems.at[kind + 1, s, mine[s]],
-                device_id=_device(axis, peer_of(s, d)), device_id_type=pl.DeviceIdType.MESH,
-            )
-            c.start()
-            copies.append((d, c))
-        for d, c in copies:
-            c.wait_send()
-            pltpu.make_async_remote_copy(
-                src_ref=src_of(d), dst_ref=dst_of(d),
-                send_sem=sems.at[kind, s, d], recv_sem=sems.at[kind + 1, s, d],
-                device_id=_device(axis, peer_of(s, d)), device_id_type=pl.DeviceIdType.MESH,
-            ).wait_recv()
-
+    _barrier([plan])
     if mode == "sum":
-        acc = x_ref
-        for s in range(stages):
-            rb = rbufs[s]
-            rb[mine[s]] = acc[...]
-            exchange_stage(0, s, lambda d: acc, lambda d, rb=rb: rb.at[d])
-            total = rb[0]
-            for d in range(1, factors[s]):
-                total = total + rb[d]
-            if s == stages - 1:
-                y_ref[...] = total
-            else:
-                rbufs[s + 1][mine[s + 1]] = total
-                acc = rbufs[s + 1].at[mine[s + 1]]
+        y_ref[...] = _sum(plan, sems, 0, x_ref[...], rbufs)
         return
-
     if mode == "reduce":
-        cur = x_ref
-        for s in range(stages):
-            lead = stages - 1 - s
-
-            def src_of(d, cur=cur, lead=lead):
-                return cur.at[(slice(None),) * lead + (d,)]
-
-            rb = rbufs[s]
-            exchange_stage(0, s, src_of, lambda d, rb=rb: rb.at[d])
-            total = cur[(slice(None),) * lead + (mine[s],)]
-            for k in range(1, factors[s]):
-                total = total + rb[other(s, k)]
-            rb[mine[s]] = total
-            cur = rb.at[mine[s]]
-        own = epilogue(cur[...], s_ref)
+        own = epilogue(_reduce_scatter(plan, sems, 0, x_ref, rbufs)[...], s_ref)
     else:
         own = x_ref[...]
-    gbuf[tuple(mine[::-1])] = own.astype(gbuf.dtype)
-    for s in reversed(range(stages)):
-        lead = stages - 1 - s
-
-        def view(d, s=s, lead=lead):
-            return gbuf.at[(slice(None),) * lead + (d,) + tuple(mine[s - 1::-1] if s else ())]
-
-        exchange_stage(2, s, lambda d, s=s: view(mine[s]), view)
+    _all_gather(plan, sems, 2, gbuf, own)
     y_ref[...] = gbuf[...]
+
+
+def _digits(j, factors):
+    return tuple((j // math.prod(factors[:s])) % factors[s] for s in reversed(range(len(factors))))
+
+
+def _product_gram_kernel(x_ref, s_ref, y_ref, g_ref, *rest, row_factors, col_factors):
+    rows = _Plan("row", row_factors)
+    cols = _Plan("col", col_factors)
+    rbufs = rest[:rows.stages]
+    gbuf = rest[rows.stages]
+    cbufs = rest[rows.stages + 1:rows.stages + 1 + cols.stages]
+    sems = rest[-1]
+    _barrier([rows, cols])
+    own = _reduce_scatter(rows, sems, 0, x_ref, rbufs)[...] * s_ref[...]
+    _all_gather(rows, sems, 2, gbuf, own)
+    y_ref[...] = gbuf[...]
+    n = math.prod(row_factors)
+    per = y_ref.shape[-2]
+    width = g_ref.shape[0]
+    gram = None
+    for p in range(n * per // width):
+        parts = [y_ref[_digits(p * width // per + i, row_factors)] for i in range(width // per)]
+        block = jnp.concatenate(parts, axis=0)
+        term = lax.dot_general(block, block, (((1,), (1,)), ((), ())), precision=HIGH,
+                               preferred_element_type=jnp.float32)
+        gram = term if gram is None else gram + term
+    g_ref[...] = _sum(cols, sems, 4, gram, cbufs)
+
+
+def product_gram(x, scale, row_factors, col_factors, cid, width):
+    n = math.prod(row_factors)
+    chunk = x.shape[1:]
+    x = x.reshape(tuple(reversed(row_factors)) + chunk)
+    scratch = []
+    for s in range(len(row_factors)):
+        scratch.append(pltpu.VMEM((row_factors[s],) + tuple(reversed(row_factors[s + 1:])) + chunk,
+                                  jnp.float32))
+    scratch.append(pltpu.VMEM(tuple(reversed(row_factors)) + chunk, jnp.float32))
+    for s in range(len(col_factors)):
+        scratch.append(pltpu.VMEM((col_factors[s], width, width), jnp.float32))
+    scratch.append(pltpu.SemaphoreType.DMA((6, max(len(row_factors), len(col_factors)),
+                                            max(row_factors + col_factors))))
+    nbytes = n * math.prod(chunk) * 4
+    y, g = pl.pallas_call(
+        functools.partial(_product_gram_kernel, row_factors=tuple(row_factors),
+                          col_factors=tuple(col_factors)),
+        out_shape=(jax.ShapeDtypeStruct(tuple(reversed(row_factors)) + chunk, jnp.float32),
+                   jax.ShapeDtypeStruct((width, width), jnp.float32)),
+        in_specs=[pl.BlockSpec(memory_space=pltpu.VMEM)] * 2,
+        out_specs=(pl.BlockSpec(memory_space=pltpu.VMEM), pl.BlockSpec(memory_space=pltpu.VMEM)),
+        scratch_shapes=scratch,
+        compiler_params=pltpu.CompilerParams(collective_id=cid, has_side_effects=True),
+        cost_estimate=pl.CostEstimate(flops=0, transcendentals=0, bytes_accessed=2 * nbytes),
+    )(x, scale)
+    return y.reshape((n,) + chunk), g
 
 
 def staged(x, axis, factors, mode, cid, scale=None, epilogue=None, out_dtype=None):
@@ -167,7 +248,7 @@
     return total * s_ref[...]
 
 
-GROUP = 4
+GROUP = 8
 
 
 def _products_kernel(ids_ref, count_ref, src_ref, tiles_hbm, out_ref, tiles, sems, *, forward):
@@ -273,12 +354,11 @@
         product_partial = tile_products(
             slot_ids, live_count, query_tiles_panel, tile_set, product_tiles, False
         )
-        lifted_tiles = staged(
-            product_partial.reshape(n_row, width // p_per_tile, side), "row", ROW_FACTORS, "reduce", 2,
-            scale=my_pscale, epilogue=_product_epilogue,
-        ).reshape(product_tiles, width, side)
-        gram_part = jnp.einsum("pri,psi->rs", lifted_tiles, lifted_tiles, precision=HIGH)
-        gram = staged(gram_part, "col", GRAM_FACTORS, "sum", 3)
+        lifted_pieces, gram = product_gram(
+            product_partial.reshape(n_row, width // p_per_tile, side), my_pscale, ROW_FACTORS,
+            GRAM_FACTORS, 2, width,
+        )
+        lifted_tiles = lifted_pieces.reshape(product_tiles, width, side)
         lifted = jnp.transpose(lifted_tiles, (1, 0, 2)).reshape(width, block)
         current = orthonormal(lifted, gram)
     mine = lax.dynamic_slice_in_dim(current, row_at * share, share, axis=1)

time: 244 us -> 229 us (0.939)
  Pallas kernels: 199 us -> 188 us
  matrix products: 6.02 us -> 1.28 us
    pallas_call x7 -> x3, Pallas kernels: 179 us -> 76.2 us  [staged(): pl.pallas_call(functools.partial(_staged_kernel, axis=axis, factors=tuple...]
    pallas_call x0 -> x2, Pallas kernels: none -> 94.1 us  [product_gram(): pl.pallas_call(functools.partial(_product_gram_kernel, row_factors=tuple(...]
    dot_general x2 -> x0, matrix products: 4.76 us -> none  [shards(): jnp.einsum('pri,psi->rs', lifted_tiles, lifted_tiles, precision=HIGH)]
where the time goes in v7:
time: 229 us; the launch traced here: 228 us
  Pallas kernels  188 us (82%)
  other arithmetic  29.8 us (13%)
  local copies, waits for them, and re-layouts  7.15 us (3%)
    pallas_call x2, Pallas kernels, product_gram(): pl.pallas_call(functools.partial(_product_gram_kernel, row_factors=tuple(...  94.1 us
    pallas_call x3, Pallas kernels, staged(): pl.pallas_call(functools.partial(_staged_kernel, axis=axis, factors=tuple...  76.2 us
    pallas_call x4, Pallas kernels, tile_products(): pl.pallas_call(functools.partial(_products_kernel, forward=forward), out_...  18.2 us
    another operation x6, other arithmetic, orthonormal(): lower = jnp.linalg.cholesky(gram)  13 us
    another operation x4, other arithmetic, orthonormal(): lax.linalg.triangular_solve(lower, lifted, left_side=True, lower=True)  11.1 us

profile of v7, /device:TPU:6, one launch (start us, length us, event | category | flops | bytes accessed | tf_op | source)
XLA Modules:
  0.0 227.5 jit_solution(3043477220979832433)
XLA Ops:
  0.7 0.7 convert_rsqrt_fusion.1
  2.0 0.7 convert_rsqrt_fusion
  3.3 1.4 multiply_convert_fusion.refs_0_
  4.7 16.2 %shard_map.64 = bf16[4,4,64,128]{3,2,1,0:T(8,128)(2,1)} custom-call(bf16[64,128]{1,0:T(8,128)(2,1)} %multiply_convert_fusion.refs_0_), custom_call_target="tpu_custom_call" | custom-call | bytes 1048576 | tf_op jit(solution)/shard_map/pallas_call | solution.py:223
  20.9 1.2 copy.25
  22.1 0.9 reshape.31.src_ref
  23.0 4.8 %shard_map.65 = f32[8,64,256]{2,1,0:T(8,128)} custom-call(s32[2,32]{1,0:T(2,128)} %bitcast.82, s32[1]{0:T(128)} %bitcast.60.count_ref, bf16[8,64,256]{2,1,0:T(8,128)(2,1)} %reshape.31.src_ref, bf16[32,256,256]{2,1,0:T(8,128)(2,1)} %bitcast.64), custom_call_target="tpu_custom_call" | custom-call | flops 268435456 | bytes 4980736 | tf_op jit(solution)/shard_map/pallas_call | solution.py:288
  27.8 32.5 %shard_map.66 = bf16[4,4,2,16,256]{4,3,2,1,0:T(8,128)(2,1)} custom-call(f32[4,4,2,16,256]{4,3,2,1,0:T(8,128)} %bitcast.71, f32[1,256]{1,0:T(1,128)} %dynamic-slice_bitcast_fusion.1.refs_1_), custom_call_target="tpu_custom_call" | custom-call | bytes 1048576 | tf_op jit(solution)/shard_map/pallas_call | solution.py:223
  60.3 4.3 %shard_map.67 = f32[8,64,256]{2,1,0:T(8,128)} custom-call(s32[2,32]{1,0:T(2,128)} %bitcast.83, s32[1]{0:T(128)} %bitcast.61.count_ref, bf16[8,64,256]{2,1,0:T(8,128)(2,1)} %bitcast.76, bf16[32,256,256]{2,1,0:T(8,128)(2,1)} %bitcast.65), custom_call_target="tpu_custom_call" | custom-call | flops 268435456 | bytes 4980736 | tf_op jit(solution)/shard_map/pallas_call | solution.py:288
  64.6 46.8 %shard_map.68 = (f32[4,4,32,256]{3,2,1,0:T(8,128)}, f32[64,64]{1,0:T(8,128)}) custom-call(f32[4,4,32,256]{3,2,1,0:T(8,128)} %bitcast.69, f32[1,256]{1,0:T(1,128)} %dynamic-slice_bitcast_fusion.s_ref), custom_call_target="tpu_custom_call" | custom-call | bytes 1048576 | tf_op jit(solution)/shard_map/pallas_call | solution.py:186
  111.4 1.1 copy.17
  112.5 0.8 copy.11
  113.3 0.8 fusion.9
  114.1 5.8 %cholesky.44 = f32[64,64]{1,0:T(8,128)S(1)} custom-call(f32[64,64]{1,0:T(8,128)S(1)} %fusion.9), custom_call_target="Cholesky" | custom-call | tf_op jit(solution)/shard_map/jit(cholesky)/cholesky | solution.py:310
  120.0 0.6 compare_reduce_fusion.1
  120.6 0.7 fusion.2
  121.3 4.9 %custom-call.6 = f32[1,64,64]{1,2,0:T(8,128)S(1)} custom-call(f32[1,64,64]{2,1,0:T(8,128)S(1)} %fusion.2), custom_call_target="InvertDiagBlocksLowerTriangular" | custom-call | tf_op jit(solution)/shard_map/triangular_solve/custom-call.0 | solution.py:311
  126.2 0.6 fusion.7
  126.8 0.8 fusion.1.src_ref
  127.6 4.8 %shard_map.69 = f32[8,64,256]{2,1,0:T(8,128)} custom-call(s32[2,32]{1,0:T(2,128)} %bitcast.84, s32[1]{0:T(128)} %bitcast.62.count_ref, bf16[8,64,256]{2,1,0:T(8,128)(2,1)} %fusion.1.src_ref, bf16[32,256,256]{2,1,0:T(8,128)(2,1)} %bitcast.66), custom_call_target="tpu_custom_call" | custom-call | flops 268435456 | bytes 4980736 | tf_op jit(solution)/shard_map/pallas_call | solution.py:288
  132.4 27.5 %shard_map.70 = bf16[4,4,2,16,256]{4,3,2,1,0:T(8,128)(2,1)} custom-call(f32[4,4,2,16,256]{4,3,2,1,0:T(8,128)} %bitcast.70, f32[1,256]{1,0:T(1,128)} %dynamic-slice_bitcast_fusion.1.refs_1_), custom_call_target="tpu_custom_call" | custom-call | bytes 1048576 | tf_op jit(solution)/shard_map/pallas_call | solution.py:223
  159.9 4.3 %shard_map.71 = f32[8,64,256]{2,1,0:T(8,128)} custom-call(s32[2,32]{1,0:T(2,128)} %bitcast.85, s32[1]{0:T(128)} %bitcast.63.count_ref, bf16[8,64,256]{2,1,0:T(8,128)(2,1)} %bitcast.75, bf16[32,256,256]{2,1,0:T(8,128)(2,1)} %bitcast.67), custom_call_target="tpu_custom_call" | custom-call | flops 268435456 | bytes 4980736 | tf_op jit(solution)/shard_map/pallas_call | solution.py:288
  164.2 47.3 %shard_map.72 = (f32[4,4,32,256]{3,2,1,0:T(8,128)}, f32[64,64]{1,0:T(8,128)}) custom-call(f32[4,4,32,256]{3,2,1,0:T(8,128)} %bitcast.68, f32[1,256]{1,0:T(1,128)} %dynamic-slice_bitcast_fusion.s_ref), custom_call_target="tpu_custom_call" | custom-call | bytes 1048576 | tf_op jit(solution)/shard_map/pallas_call | solution.py:186
  211.5 1.1 copy.18
  212.6 0.8 copy.14
  213.4 0.8 fusion.6
  214.2 5.8 %cholesky.55 = f32[64,64]{1,0:T(8,128)S(1)} custom-call(f32[64,64]{1,0:T(8,128)S(1)} %fusion.6), custom_call_target="Cholesky" | custom-call | tf_op jit(solution)/shard_map/jit(cholesky)/cholesky | solution.py:310
  220.1 0.6 compare_reduce_fusion
  220.7 0.7 fusion.3
  221.4 4.9 %custom-call.7 = f32[1,64,64]{1,2,0:T(8,128)S(1)} custom-call(f32[1,64,64]{2,1,0:T(8,128)S(1)} %fusion.3), custom_call_target="InvertDiagBlocksLowerTriangular" | custom-call | tf_op jit(solution)/shard_map/triangular_solve/custom-call.0 | solution.py:311
  226.3 0.6 fusion.4
  226.9 0.6 dynamic-slice_multiply_fusion
  (6 shorter events, 1.3 us)

commit v8 on v7

--- a/solution.py
+++ b/solution.py
@@ -306,9 +306,10 @@
     )(slot_ids, live_count.reshape(1), src, tile_set)
 
 
-def orthonormal(lifted, gram):
+def lower_inverse(gram):
     lower = jnp.linalg.cholesky(gram)
-    return lax.linalg.triangular_solve(lower, lifted, left_side=True, lower=True)
+    eye = jnp.eye(gram.shape[0], dtype=gram.dtype)
+    return lax.linalg.triangular_solve(lower, eye, left_side=True, lower=True)
 
 
 def shards(tiles, tile_ids, tile_count, query_degree, product_degree, panel):
@@ -340,12 +341,10 @@
     scaled_tiles = jnp.transpose(
         gathered.reshape(product_tiles, per_tile, width, share), (0, 2, 1, 3)
     ).reshape(product_tiles, width, side)
-    current = None
     for iteration in range(ITERS):
-        if current is not None:
-            scaled_tiles = (
-                jnp.transpose(current.reshape(width, product_tiles, side), (1, 0, 2)) * pscale
-            ).astype(jnp.bfloat16)
+        if iteration:
+            current_tiles = jnp.einsum("rs,psi->pri", inverse, lifted_tiles, precision=HIGH)
+            scaled_tiles = (current_tiles * pscale).astype(jnp.bfloat16)
         partial_sum = tile_products(slot_ids, live_count, scaled_tiles, tile_set, query_tiles, True)
         query_tiles_panel = staged(
             partial_sum.reshape(n_col, width // q_per_tile, side), "col", QUERY_FACTORS, "reduce", 1,
@@ -359,10 +358,10 @@
             GRAM_FACTORS, 2, width,
         )
         lifted_tiles = lifted_pieces.reshape(product_tiles, width, side)
-        lifted = jnp.transpose(lifted_tiles, (1, 0, 2)).reshape(width, block)
-        current = orthonormal(lifted, gram)
-    mine = lax.dynamic_slice_in_dim(current, row_at * share, share, axis=1)
-    return mine * root_count
+        inverse = lower_inverse(gram)
+    my_tile = lax.dynamic_index_in_dim(lifted_tiles, row_at // per_tile, keepdims=False)
+    my_lifted = lax.dynamic_slice_in_dim(my_tile, (row_at % per_tile) * share, share, axis=1)
+    return jnp.einsum("rs,si->ri", inverse, my_lifted, precision=HIGH) * root_count
 
 
 def solution(mesh):

time: 229 us -> 228 us (level)
  matrix products: 1.28 us -> 4.55 us
    dot_general x0 -> x2, matrix products: none -> 4.04 us  [the longest x1 2.34 us: shards(): jnp.einsum('rs,psi->pri', inverse, lifted_tiles, precision=HIGH)]
where the time goes in v8:
time: 228 us; the launch traced here: 227 us
  Pallas kernels  188 us (82%)
  other arithmetic  28.5 us (12%)
  local copies, waits for them, and re-layouts  4.99 us (2%)
  matrix products  4.55 us (2%)
    pallas_call x2, Pallas kernels, product_gram(): pl.pallas_call(functools.partial(_product_gram_kernel, row_factors=tuple(...  93.7 us
    pallas_call x3, Pallas kernels, staged(): pl.pallas_call(functools.partial(_staged_kernel, axis=axis, factors=tuple...  76.3 us
    pallas_call x4, Pallas kernels, tile_products(): pl.pallas_call(functools.partial(_products_kernel, forward=forward), out_...  18.2 us
    another operation x6, other arithmetic, lower_inverse(): lower = jnp.linalg.cholesky(gram)  13 us
    another operation x4, other arithmetic, lower_inverse(): return lax.linalg.triangular_solve(lower, eye, left_side=True, lower=True)  11.1 us

profile of v8, /device:TPU:6, one launch (start us, length us, event | category | flops | bytes accessed | tf_op | source)
XLA Modules:
  0.0 226.9 jit_solution(3088126683717668836)
XLA Ops:
  0.7 0.7 convert_rsqrt_fusion.1
  1.4 0.6 dynamic-slice_bitcast_fusion.s_ref
  2.0 0.7 convert_rsqrt_fusion
  2.7 0.6 dynamic-slice_bitcast_fusion.1.refs_1_
  3.3 1.4 multiply_convert_fusion.refs_0_
  4.7 16.2 %shard_map.64 = bf16[4,4,64,128]{3,2,1,0:T(8,128)(2,1)} custom-call(bf16[64,128]{1,0:T(8,128)(2,1)} %multiply_convert_fusion.refs_0_), custom_call_target="tpu_custom_call" | custom-call | bytes 1048576 | tf_op jit(solution)/shard_map/pallas_call | solution.py:223
  20.9 1.2 copy.11
  22.1 0.9 reshape.23.src_ref
  23.0 4.8 %shard_map.65 = f32[8,64,256]{2,1,0:T(8,128)} custom-call(s32[2,32]{1,0:T(2,128)} %bitcast.67, s32[1]{0:T(128)} %bitcast.49.count_ref, bf16[8,64,256]{2,1,0:T(8,128)(2,1)} %reshape.23.src_ref, bf16[32,256,256]{2,1,0:T(8,128)(2,1)} %bitcast.53), custom_call_target="tpu_custom_call" | custom-call | flops 268435456 | bytes 4980736 | tf_op jit(solution)/shard_map/pallas_call | solution.py:288
  27.8 32.5 %shard_map.66 = bf16[4,4,2,16,256]{4,3,2,1,0:T(8,128)(2,1)} custom-call(f32[4,4,2,16,256]{4,3,2,1,0:T(8,128)} %bitcast.60, f32[1,256]{1,0:T(1,128)} %dynamic-slice_bitcast_fusion.1.refs_1_), custom_call_target="tpu_custom_call" | custom-call | bytes 1048576 | tf_op jit(solution)/shard_map/pallas_call | solution.py:223
  60.3 4.3 %shard_map.67 = f32[8,64,256]{2,1,0:T(8,128)} custom-call(s32[2,32]{1,0:T(2,128)} %bitcast.68, s32[1]{0:T(128)} %bitcast.50.count_ref, bf16[8,64,256]{2,1,0:T(8,128)(2,1)} %bitcast.62, bf16[32,256,256]{2,1,0:T(8,128)(2,1)} %bitcast.54), custom_call_target="tpu_custom_call" | custom-call | flops 268435456 | bytes 4980736 | tf_op jit(solution)/shard_map/pallas_call | solution.py:288
  64.6 46.7 %shard_map.68 = (f32[4,4,32,256]{3,2,1,0:T(8,128)}, f32[64,64]{1,0:T(8,128)}) custom-call(f32[4,4,32,256]{3,2,1,0:T(8,128)} %bitcast.58, f32[1,256]{1,0:T(1,128)} %dynamic-slice_bitcast_fusion.s_ref), custom_call_target="tpu_custom_call" | custom-call | bytes 1048576 | tf_op jit(solution)/shard_map/pallas_call | solution.py:186
  111.3 0.8 copy.8
  112.1 0.8 fusion.11
  112.9 5.8 %cholesky.44 = f32[64,64]{1,0:T(8,128)S(1)} custom-call(f32[64,64]{1,0:T(8,128)S(1)} %fusion.11), custom_call_target="Cholesky" | custom-call | tf_op jit(solution)/shard_map/jit(cholesky)/cholesky | solution.py:310
  118.7 0.6 compare_reduce_fusion.1
  119.4 0.7 fusion.5
  120.1 4.9 %custom-call.6 = f32[1,64,64]{1,2,0:T(8,128)S(1)} custom-call(f32[1,64,64]{2,1,0:T(8,128)S(1)} %fusion.5), custom_call_target="InvertDiagBlocksLowerTriangular" | custom-call | tf_op jit(solution)/shard_map/triangular_solve/custom-call.0 | solution.py:312
  124.9 0.3 convolution_bitcast_fusion
  125.2 2.3 %fusion.1.src_ref = bf16[8,64,256]{2,1,0:T(8,128)(2,1)} fusion(f32[8,64,256]{2,1,0:T(8,128)} %bitcast.65, f32[64,64,1]{1,0,2:T(8,128)S(1)} %convolution_bitcast_fusion, f32[8,256]{1,0:T(8,128)S(1)} %mul.34), kind=kOutput, calls=%fused_computation.2 | convolution fusion | flops 100925440 | bytes 811008 | tf_op jit(solution)/shard_map/rs,psi->pri/dot_general | solution.py:346
  127.5 4.8 %shard_map.69 = f32[8,64,256]{2,1,0:T(8,128)} custom-call(s32[2,32]{1,0:T(2,128)} %bitcast.69, s32[1]{0:T(128)} %bitcast.51.count_ref, bf16[8,64,256]{2,1,0:T(8,128)(2,1)} %fusion.1.src_ref, bf16[32,256,256]{2,1,0:T(8,128)(2,1)} %bitcast.55), custom_call_target="tpu_custom_call" | custom-call | flops 268435456 | bytes 4980736 | tf_op jit(solution)/shard_map/pallas_call | solution.py:288
  132.4 27.6 %shard_map.70 = bf16[4,4,2,16,256]{4,3,2,1,0:T(8,128)(2,1)} custom-call(f32[4,4,2,16,256]{4,3,2,1,0:T(8,128)} %bitcast.59, f32[1,256]{1,0:T(1,128)} %dynamic-slice_bitcast_fusion.1.refs_1_), custom_call_target="tpu_custom_call" | custom-call | bytes 1048576 | tf_op jit(solution)/shard_map/pallas_call | solution.py:223
  160.0 4.3 %shard_map.71 = f32[8,64,256]{2,1,0:T(8,128)} custom-call(s32[2,32]{1,0:T(2,128)} %bitcast.70, s32[1]{0:T(128)} %bitcast.52.count_ref, bf16[8,64,256]{2,1,0:T(8,128)(2,1)} %bitcast.61, bf16[32,256,256]{2,1,0:T(8,128)(2,1)} %bitcast.56), custom_call_target="tpu_custom_call" | custom-call | flops 268435456 | bytes 4980736 | tf_op jit(solution)/shard_map/pallas_call | solution.py:288
  164.3 47.0 %shard_map.72 = (f32[4,4,32,256]{3,2,1,0:T(8,128)}, f32[64,64]{1,0:T(8,128)}) custom-call(f32[4,4,32,256]{3,2,1,0:T(8,128)} %bitcast.57, f32[1,256]{1,0:T(1,128)} %dynamic-slice_bitcast_fusion.s_ref), custom_call_target="tpu_custom_call" | custom-call | bytes 1048576 | tf_op jit(solution)/shard_map/pallas_call | solution.py:186
  211.3 0.8 copy.9
  212.1 0.8 fusion.9
  212.9 5.8 %cholesky.55 = f32[64,64]{1,0:T(8,128)S(1)} custom-call(f32[64,64]{1,0:T(8,128)S(1)} %fusion.9), custom_call_target="Cholesky" | custom-call | tf_op jit(solution)/shard_map/jit(cholesky)/cholesky | solution.py:310
  218.7 0.6 compare_reduce_fusion
  219.4 0.7 fusion.6
  220.1 4.9 %custom-call.7 = f32[1,64,64]{1,2,0:T(8,128)S(1)} custom-call(f32[1,64,64]{2,1,0:T(8,128)S(1)} %fusion.6), custom_call_target="InvertDiagBlocksLowerTriangular" | custom-call | tf_op jit(solution)/shard_map/triangular_solve/custom-call.0 | solution.py:312
  224.9 0.3 fusion.2
  225.2 1.7 convolution_multiply_fusion.1
  (4 shorter events, 0.1 us)

commit v9 on v8

--- a/solution.py
+++ b/solution.py
@@ -53,7 +53,7 @@
     pl.semaphore_wait(barrier, count)
 
 
-def _exchange(plan, sems, kind, s, src_of, dst_of):
+def _exchange(plan, sems, kind, s, src_of, dst_of, pending):
     copies = []
     mine = plan.mine[s]
     for k in range(1, plan.factors[s]):
@@ -65,8 +65,8 @@
         )
         c.start()
         copies.append((d, c))
+    pending.extend(c for _, c in copies)
     for d, c in copies:
-        c.wait_send()
         pltpu.make_async_remote_copy(
             src_ref=src_of(d), dst_ref=dst_of(d),
             send_sem=sems.at[kind, s, d], recv_sem=sems.at[kind + 1, s, d],
@@ -74,7 +74,7 @@
         ).wait_recv()
 
 
-def _reduce_scatter(plan, sems, kind, x_ref, rbufs):
+def _reduce_scatter(plan, sems, kind, x_ref, rbufs, pending):
     cur = x_ref
     for s in range(plan.stages):
         lead = plan.stages - 1 - s
@@ -83,7 +83,7 @@
             return cur.at[(slice(None),) * lead + (d,)]
 
         rb = rbufs[s]
-        _exchange(plan, sems, kind, s, src_of, lambda d, rb=rb: rb.at[d])
+        _exchange(plan, sems, kind, s, src_of, lambda d, rb=rb: rb.at[d], pending)
         total = cur[(slice(None),) * lead + (plan.mine[s],)]
         for k in range(1, plan.factors[s]):
             total = total + rb[plan.other(s, k)]
@@ -92,7 +92,7 @@
     return cur
 
 
-def _all_gather(plan, sems, kind, gbuf, own):
+def _all_gather(plan, sems, kind, gbuf, own, pending):
     mine = plan.mine
     gbuf[tuple(mine[::-1])] = own.astype(gbuf.dtype)
     for s in reversed(range(plan.stages)):
@@ -101,15 +101,15 @@
         def view(d, s=s, lead=lead):
             return gbuf.at[(slice(None),) * lead + (d,) + tuple(mine[s - 1::-1] if s else ())]
 
-        _exchange(plan, sems, kind, s, lambda d, s=s: view(mine[s]), view)
-
-
-def _sum(plan, sems, kind, value, rbufs):
+        _exchange(plan, sems, kind, s, lambda d, s=s: view(mine[s]), view, pending)
+
+
+def _sum(plan, sems, kind, value, rbufs, pending):
     for s in range(plan.stages):
         rb = rbufs[s]
         rb[plan.mine[s]] = value
         src = rb.at[plan.mine[s]]
-        _exchange(plan, sems, kind, s, lambda d, src=src: src, lambda d, rb=rb: rb.at[d])
+        _exchange(plan, sems, kind, s, lambda d, src=src: src, lambda d, rb=rb: rb.at[d], pending)
         value = rb[0]
         for d in range(1, plan.factors[s]):
             value = value + rb[d]
@@ -130,15 +130,18 @@
     gbuf = rest[n_rs] if mode != "sum" else None
     sems = rest[-1]
     _barrier([plan])
+    pending = []
     if mode == "sum":
-        y_ref[...] = _sum(plan, sems, 0, x_ref[...], rbufs)
-        return
-    if mode == "reduce":
-        own = epilogue(_reduce_scatter(plan, sems, 0, x_ref, rbufs)[...], s_ref)
+        y_ref[...] = _sum(plan, sems, 0, x_ref[...], rbufs, pending)
     else:
-        own = x_ref[...]
-    _all_gather(plan, sems, 2, gbuf, own)
-    y_ref[...] = gbuf[...]
+        if mode == "reduce":
+            own = epilogue(_reduce_scatter(plan, sems, 0, x_ref, rbufs, pending)[...], s_ref)
+        else:
+            own = x_ref[...]
+        _all_gather(plan, sems, 2, gbuf, own, pending)
+        y_ref[...] = gbuf[...]
+    for c in pending:
+        c.wait_send()
 
 
 def _digits(j, factors):
@@ -153,8 +156,9 @@
     cbufs = rest[rows.stages + 1:rows.stages + 1 + cols.stages]
     sems = rest[-1]
     _barrier([rows, cols])
-    own = _reduce_scatter(rows, sems, 0, x_ref, rbufs)[...] * s_ref[...]
-    _all_gather(rows, sems, 2, gbuf, own)
+    pending = []
+    own = _reduce_scatter(rows, sems, 0, x_ref, rbufs, pending)[...] * s_ref[...]
+    _all_gather(rows, sems, 2, gbuf, own, pending)
     y_ref[...] = gbuf[...]
     n = math.prod(row_factors)
     per = y_ref.shape[-2]
@@ -166,7 +170,9 @@
         term = lax.dot_general(block, block, (((1,), (1,)), ((), ())), precision=HIGH,
                                preferred_element_type=jnp.float32)
         gram = term if gram is None else gram + term
-    g_ref[...] = _sum(cols, sems, 4, gram, cbufs)
+    g_ref[...] = _sum(cols, sems, 4, gram, cbufs, pending)
+    for c in pending:
+        c.wait_send()
 
 
 def product_gram(x, scale, row_factors, col_factors, cid, width):

time: 228 us -> 227 us (level)
  no operation moved by 1% of the time
where the time goes in v9:
time: 227 us; the launch traced here: 226 us
  Pallas kernels  187 us (82%)
  other arithmetic  28.5 us (13%)
  local copies, waits for them, and re-layouts  4.99 us (2%)
  matrix products  4.55 us (2%)
    pallas_call x2, Pallas kernels, product_gram(): pl.pallas_call(functools.partial(_product_gram_kernel, row_factors=tuple(...  94.2 us
    pallas_call x3, Pallas kernels, staged(): pl.pallas_call(functools.partial(_staged_kernel, axis=axis, factors=tuple...  74.4 us
    pallas_call x4, Pallas kernels, tile_products(): pl.pallas_call(functools.partial(_products_kernel, forward=forward), out_...  18.2 us
    another operation x6, other arithmetic, lower_inverse(): lower = jnp.linalg.cholesky(gram)  13 us
    another operation x4, other arithmetic, lower_inverse(): return lax.linalg.triangular_solve(lower, eye, left_side=True, lower=True)  11.1 us

profile of v9, /device:TPU:6, one launch (start us, length us, event | category | flops | bytes accessed | tf_op | source)
XLA Modules:
  0.0 225.5 jit_solution(11017388976618091629)
XLA Ops:
  0.7 0.7 convert_rsqrt_fusion.1
  1.4 0.6 dynamic-slice_bitcast_fusion.s_ref
  2.0 0.7 convert_rsqrt_fusion
  2.7 0.6 dynamic-slice_bitcast_fusion.1.refs_1_
  3.3 1.4 multiply_convert_fusion.refs_0_
  4.7 16.2 %shard_map.64 = bf16[4,4,64,128]{3,2,1,0:T(8,128)(2,1)} custom-call(bf16[64,128]{1,0:T(8,128)(2,1)} %multiply_convert_fusion.refs_0_), custom_call_target="tpu_custom_call" | custom-call | bytes 1048576 | tf_op jit(solution)/shard_map/pallas_call | solution.py:229
  20.9 1.2 copy.11
  22.1 0.9 reshape.23.src_ref
  23.0 4.8 %shard_map.65 = f32[8,64,256]{2,1,0:T(8,128)} custom-call(s32[2,32]{1,0:T(2,128)} %bitcast.67, s32[1]{0:T(128)} %bitcast.49.count_ref, bf16[8,64,256]{2,1,0:T(8,128)(2,1)} %reshape.23.src_ref, bf16[32,256,256]{2,1,0:T(8,128)(2,1)} %bitcast.53), custom_call_target="tpu_custom_call" | custom-call | flops 268435456 | bytes 4980736 | tf_op jit(solution)/shard_map/pallas_call | solution.py:294
  27.8 31.5 %shard_map.66 = bf16[4,4,2,16,256]{4,3,2,1,0:T(8,128)(2,1)} custom-call(f32[4,4,2,16,256]{4,3,2,1,0:T(8,128)} %bitcast.60, f32[1,256]{1,0:T(1,128)} %dynamic-slice_bitcast_fusion.1.refs_1_), custom_call_target="tpu_custom_call" | custom-call | bytes 1048576 | tf_op jit(solution)/shard_map/pallas_call | solution.py:229
  59.3 4.3 %shard_map.67 = f32[8,64,256]{2,1,0:T(8,128)} custom-call(s32[2,32]{1,0:T(2,128)} %bitcast.68, s32[1]{0:T(128)} %bitcast.50.count_ref, bf16[8,64,256]{2,1,0:T(8,128)(2,1)} %bitcast.62, bf16[32,256,256]{2,1,0:T(8,128)(2,1)} %bitcast.54), custom_call_target="tpu_custom_call" | custom-call | flops 268435456 | bytes 4980736 | tf_op jit(solution)/shard_map/pallas_call | solution.py:294
  63.6 46.9 %shard_map.68 = (f32[4,4,32,256]{3,2,1,0:T(8,128)}, f32[64,64]{1,0:T(8,128)}) custom-call(f32[4,4,32,256]{3,2,1,0:T(8,128)} %bitcast.58, f32[1,256]{1,0:T(1,128)} %dynamic-slice_bitcast_fusion.s_ref), custom_call_target="tpu_custom_call" | custom-call | bytes 1048576 | tf_op jit(solution)/shard_map/pallas_call | solution.py:192
  110.5 0.8 copy.8
  111.3 0.8 fusion.11
  112.1 5.8 %cholesky.44 = f32[64,64]{1,0:T(8,128)S(1)} custom-call(f32[64,64]{1,0:T(8,128)S(1)} %fusion.11), custom_call_target="Cholesky" | custom-call | tf_op jit(solution)/shard_map/jit(cholesky)/cholesky | solution.py:316
  118.0 0.6 compare_reduce_fusion.1
  118.6 0.7 fusion.5
  119.3 4.9 %custom-call.6 = f32[1,64,64]{1,2,0:T(8,128)S(1)} custom-call(f32[1,64,64]{2,1,0:T(8,128)S(1)} %fusion.5), custom_call_target="InvertDiagBlocksLowerTriangular" | custom-call | tf_op jit(solution)/shard_map/triangular_solve/custom-call.0 | solution.py:318
  124.2 0.3 convolution_bitcast_fusion
  124.5 2.3 %fusion.1.src_ref = bf16[8,64,256]{2,1,0:T(8,128)(2,1)} fusion(f32[8,64,256]{2,1,0:T(8,128)} %bitcast.65, f32[64,64,1]{1,0,2:T(8,128)S(1)} %convolution_bitcast_fusion, f32[8,256]{1,0:T(8,128)S(1)} %mul.34), kind=kOutput, calls=%fused_computation.2 | convolution fusion | flops 100925440 | bytes 811008 | tf_op jit(solution)/shard_map/rs,psi->pri/dot_general | solution.py:352
  126.8 4.8 %shard_map.69 = f32[8,64,256]{2,1,0:T(8,128)} custom-call(s32[2,32]{1,0:T(2,128)} %bitcast.69, s32[1]{0:T(128)} %bitcast.51.count_ref, bf16[8,64,256]{2,1,0:T(8,128)(2,1)} %fusion.1.src_ref, bf16[32,256,256]{2,1,0:T(8,128)(2,1)} %bitcast.55), custom_call_target="tpu_custom_call" | custom-call | flops 268435456 | bytes 4980736 | tf_op jit(solution)/shard_map/pallas_call | solution.py:294
  131.6 26.6 %shard_map.70 = bf16[4,4,2,16,256]{4,3,2,1,0:T(8,128)(2,1)} custom-call(f32[4,4,2,16,256]{4,3,2,1,0:T(8,128)} %bitcast.59, f32[1,256]{1,0:T(1,128)} %dynamic-slice_bitcast_fusion.1.refs_1_), custom_call_target="tpu_custom_call" | custom-call | bytes 1048576 | tf_op jit(solution)/shard_map/pallas_call | solution.py:229
  158.3 4.3 %shard_map.71 = f32[8,64,256]{2,1,0:T(8,128)} custom-call(s32[2,32]{1,0:T(2,128)} %bitcast.70, s32[1]{0:T(128)} %bitcast.52.count_ref, bf16[8,64,256]{2,1,0:T(8,128)(2,1)} %bitcast.61, bf16[32,256,256]{2,1,0:T(8,128)(2,1)} %bitcast.56), custom_call_target="tpu_custom_call" | custom-call | flops 268435456 | bytes 4980736 | tf_op jit(solution)/shard_map/pallas_call | solution.py:294
  162.5 47.3 %shard_map.72 = (f32[4,4,32,256]{3,2,1,0:T(8,128)}, f32[64,64]{1,0:T(8,128)}) custom-call(f32[4,4,32,256]{3,2,1,0:T(8,128)} %bitcast.57, f32[1,256]{1,0:T(1,128)} %dynamic-slice_bitcast_fusion.s_ref), custom_call_target="tpu_custom_call" | custom-call | bytes 1048576 | tf_op jit(solution)/shard_map/pallas_call | solution.py:192
  209.9 0.8 copy.9
  210.7 0.8 fusion.9
  211.5 5.8 %cholesky.55 = f32[64,64]{1,0:T(8,128)S(1)} custom-call(f32[64,64]{1,0:T(8,128)S(1)} %fusion.9), custom_call_target="Cholesky" | custom-call | tf_op jit(solution)/shard_map/jit(cholesky)/cholesky | solution.py:316
  217.4 0.6 compare_reduce_fusion
  218.0 0.7 fusion.6
  218.7 4.9 %custom-call.7 = f32[1,64,64]{1,2,0:T(8,128)S(1)} custom-call(f32[1,64,64]{2,1,0:T(8,128)S(1)} %fusion.6), custom_call_target="InvertDiagBlocksLowerTriangular" | custom-call | tf_op jit(solution)/shard_map/triangular_solve/custom-call.0 | solution.py:318
  223.6 0.3 fusion.2
  223.8 1.7 convolution_multiply_fusion.1
  (4 shorter events, 0.1 us)

commit v10 on v9

--- a/solution.py
+++ b/solution.py
@@ -139,7 +139,14 @@
         else:
             own = x_ref[...]
         _all_gather(plan, sems, 2, gbuf, own, pending)
-        y_ref[...] = gbuf[...]
+        if mode == "gather" and len(y_ref.shape) == 3:
+            n = math.prod(factors)
+            share = own.shape[-1]
+            per = y_ref.shape[-1] // share
+            for j in range(n):
+                y_ref[j // per, :, pl.ds((j % per) * share, share)] = gbuf[_digits(j, factors)]
+        else:
+            y_ref[...] = gbuf[...]
     for c in pending:
         c.wait_send()
 
@@ -203,7 +210,7 @@
     return y.reshape((n,) + chunk), g
 
 
-def staged(x, axis, factors, mode, cid, scale=None, epilogue=None, out_dtype=None):
+def staged(x, axis, factors, mode, cid, scale=None, epilogue=None, out_dtype=None, tiled=None):
     n = math.prod(factors)
     stages = len(factors)
     out_dtype = out_dtype or x.dtype
@@ -222,6 +229,8 @@
     scratch.append(pltpu.SemaphoreType.DMA((4, stages, max(factors))))
     if mode == "sum":
         out_shape = chunk
+    elif tiled is not None:
+        out_shape = tiled
     else:
         out_shape = tuple(reversed(factors)) + chunk
     args = (x,) if scale is None else (x, scale)
@@ -236,7 +245,7 @@
         compiler_params=pltpu.CompilerParams(collective_id=cid, has_side_effects=True),
         cost_estimate=pl.CostEstimate(flops=0, transcendentals=0, bytes_accessed=2 * nbytes),
     )(*args)
-    if mode == "sum":
+    if mode == "sum" or tiled is not None:
         return y
     return y.reshape((n,) + chunk)
 
@@ -313,7 +322,7 @@
 
 
 def lower_inverse(gram):
-    lower = jnp.linalg.cholesky(gram)
+    lower = lax.linalg.cholesky(gram, symmetrize_input=False)
     eye = jnp.eye(gram.shape[0], dtype=gram.dtype)
     return lax.linalg.triangular_solve(lower, eye, left_side=True, lower=True)
 
@@ -342,11 +351,9 @@
 
     panel_pscale = lax.dynamic_slice_in_dim(pscale.reshape(block), row_at * share, share)
     scaled0 = (panel * panel_pscale[None, :]).astype(jnp.bfloat16)
-    gathered = staged(scaled0, "row", ROW_FACTORS, "gather", 0)
+    scaled_tiles = staged(scaled0, "row", ROW_FACTORS, "gather", 0,
+                          tiled=(product_tiles, width, side))
     per_tile = side // share
-    scaled_tiles = jnp.transpose(
-        gathered.reshape(product_tiles, per_tile, width, share), (0, 2, 1, 3)
-    ).reshape(product_tiles, width, side)
     for iteration in range(ITERS):
         if iteration:
             current_tiles = jnp.einsum("rs,psi->pri", inverse, lifted_tiles, precision=HIGH)

time: 227 us -> 223 us (0.982)
  local copies, waits for them, and re-layouts: 4.99 us -> 1.24 us
where the time goes in v10:
time: 223 us; the launch traced here: 222 us
  Pallas kernels  187 us (84%)
  other arithmetic  28.4 us (13%)
  matrix products  4.55 us (2%)
    pallas_call x2, Pallas kernels, product_gram(): pl.pallas_call(functools.partial(_product_gram_kernel, row_factors=tuple(...  94.8 us
    pallas_call x3, Pallas kernels, staged(): pl.pallas_call(functools.partial(_staged_kernel, axis=axis, factors=tuple...  74.2 us
    pallas_call x4, Pallas kernels, tile_products(): pl.pallas_call(functools.partial(_products_kernel, forward=forward), out_...  18.2 us
    another operation x6, other arithmetic, lower_inverse(): lower = lax.linalg.cholesky(gram, symmetrize_input=False)  14.5 us
    another operation x4, other arithmetic, lower_inverse(): return lax.linalg.triangular_solve(lower, eye, left_side=True, lower=True)  11.1 us

profile of v10, /device:TPU:6, one launch (start us, length us, event | category | flops | bytes accessed | tf_op | source)
XLA Modules:
  0.0 222.2 jit_solution(11625608154644125899)
XLA Ops:
  0.7 0.7 convert_rsqrt_fusion.1
  1.4 0.1 dynamic_slice.17
  1.4 0.6 dynamic-slice_bitcast_fusion.s_ref
  2.0 0.7 convert_rsqrt_fusion
  2.7 0.6 dynamic-slice_bitcast_fusion.1.refs_1_
  3.3 1.4 multiply_convert_fusion.refs_0_
  4.7 16.3 %shard_map.64.src_ref = bf16[8,64,256]{2,1,0:T(8,128)(2,1)} custom-call(bf16[64,128]{1,0:T(8,128)(2,1)} %multiply_convert_fusion.refs_0_), custom_call_target="tpu_custom_call" | custom-call | bytes 1048576 | tf_op jit(solution)/shard_map/pallas_call | solution.py:238
  20.9 4.8 %shard_map.65 = f32[8,64,256]{2,1,0:T(8,128)} custom-call(s32[2,32]{1,0:T(2,128)} %bitcast.53, s32[1]{0:T(128)} %bitcast.37.count_ref, bf16[8,64,256]{2,1,0:T(8,128)(2,1)} %shard_map.64.src_ref, bf16[32,256,256]{2,1,0:T(8,128)(2,1)} %bitcast.41), custom_call_target="tpu_custom_call" | custom-call | flops 268435456 | bytes 4980736 | tf_op jit(solution)/shard_map/pallas_call | solution.py:303
  25.8 31.5 %shard_map.66 = bf16[4,4,2,16,256]{4,3,2,1,0:T(8,128)(2,1)} custom-call(f32[4,4,2,16,256]{4,3,2,1,0:T(8,128)} %bitcast.48, f32[1,256]{1,0:T(1,128)} %dynamic-slice_bitcast_fusion.1.refs_1_), custom_call_target="tpu_custom_call" | custom-call | bytes 1048576 | tf_op jit(solution)/shard_map/pallas_call | solution.py:238
  57.3 4.3 %shard_map.67 = f32[8,64,256]{2,1,0:T(8,128)} custom-call(s32[2,32]{1,0:T(2,128)} %bitcast.54, s32[1]{0:T(128)} %bitcast.38.count_ref, bf16[8,64,256]{2,1,0:T(8,128)(2,1)} %bitcast.50, bf16[32,256,256]{2,1,0:T(8,128)(2,1)} %bitcast.42), custom_call_target="tpu_custom_call" | custom-call | flops 268435456 | bytes 4980736 | tf_op jit(solution)/shard_map/pallas_call | solution.py:303
  61.6 47.1 %shard_map.68 = (f32[4,4,32,256]{3,2,1,0:T(8,128)}, f32[64,64]{1,0:T(8,128)}) custom-call(f32[4,4,32,256]{3,2,1,0:T(8,128)} %bitcast.46, f32[1,256]{1,0:T(1,128)} %dynamic-slice_bitcast_fusion.s_ref), custom_call_target="tpu_custom_call" | custom-call | bytes 1048576 | tf_op jit(solution)/shard_map/pallas_call | solution.py:199
  108.7 6.6 %custom-call.8 = f32[64,64]{1,0:T(8,128)S(1)} custom-call(f32[64,64]{1,0:T(8,128)} %get-tuple-element.12), custom_call_target="Cholesky" | custom-call | tf_op jit(solution)/shard_map/cholesky/custom-call.1 | solution.py:325
  115.3 0.6 compare_reduce_fusion.1
  115.9 0.7 fusion.5
  116.6 4.9 %custom-call.9 = f32[1,64,64]{1,2,0:T(8,128)S(1)} custom-call(f32[1,64,64]{2,1,0:T(8,128)S(1)} %fusion.5), custom_call_target="InvertDiagBlocksLowerTriangular" | custom-call | tf_op jit(solution)/shard_map/triangular_solve/custom-call.0 | solution.py:327
  121.5 0.3 convolution_bitcast_fusion
  121.8 2.3 %fusion.1.src_ref = bf16[8,64,256]{2,1,0:T(8,128)(2,1)} fusion(f32[8,64,256]{2,1,0:T(8,128)} %bitcast.51, f32[64,64,1]{1,0,2:T(8,128)S(1)} %convolution_bitcast_fusion, f32[8,256]{1,0:T(8,128)S(1)} %mul.34), kind=kOutput, calls=%fused_computation.2 | convolution fusion | flops 100925440 | bytes 811008 | tf_op jit(solution)/shard_map/rs,psi->pri/dot_general | solution.py:359
  124.1 4.8 %shard_map.69 = f32[8,64,256]{2,1,0:T(8,128)} custom-call(s32[2,32]{1,0:T(2,128)} %bitcast.55, s32[1]{0:T(128)} %bitcast.39.count_ref, bf16[8,64,256]{2,1,0:T(8,128)(2,1)} %fusion.1.src_ref, bf16[32,256,256]{2,1,0:T(8,128)(2,1)} %bitcast.43), custom_call_target="tpu_custom_call" | custom-call | flops 268435456 | bytes 4980736 | tf_op jit(solution)/shard_map/pallas_call | solution.py:303
  128.9 26.4 %shard_map.70 = bf16[4,4,2,16,256]{4,3,2,1,0:T(8,128)(2,1)} custom-call(f32[4,4,2,16,256]{4,3,2,1,0:T(8,128)} %bitcast.47, f32[1,256]{1,0:T(1,128)} %dynamic-slice_bitcast_fusion.1.refs_1_), custom_call_target="tpu_custom_call" | custom-call | bytes 1048576 | tf_op jit(solution)/shard_map/pallas_call | solution.py:238
  155.3 4.3 %shard_map.71 = f32[8,64,256]{2,1,0:T(8,128)} custom-call(s32[2,32]{1,0:T(2,128)} %bitcast.56, s32[1]{0:T(128)} %bitcast.40.count_ref, bf16[8,64,256]{2,1,0:T(8,128)(2,1)} %bitcast.49, bf16[32,256,256]{2,1,0:T(8,128)(2,1)} %bitcast.44), custom_call_target="tpu_custom_call" | custom-call | flops 268435456 | bytes 4980736 | tf_op jit(solution)/shard_map/pallas_call | solution.py:303
  159.6 47.8 %shard_map.72 = (f32[4,4,32,256]{3,2,1,0:T(8,128)}, f32[64,64]{1,0:T(8,128)}) custom-call(f32[4,4,32,256]{3,2,1,0:T(8,128)} %bitcast.45, f32[1,256]{1,0:T(1,128)} %dynamic-slice_bitcast_fusion.s_ref), custom_call_target="tpu_custom_call" | custom-call | bytes 1048576 | tf_op jit(solution)/shard_map/pallas_call | solution.py:199
  207.4 6.6 %custom-call.10 = f32[64,64]{1,0:T(8,128)S(1)} custom-call(f32[64,64]{1,0:T(8,128)} %get-tuple-element.13), custom_call_target="Cholesky" | custom-call | tf_op jit(solution)/shard_map/cholesky/custom-call.1 | solution.py:325
  214.0 0.6 compare_reduce_fusion
  214.6 0.7 fusion.6
  215.3 4.9 %custom-call.11 = f32[1,64,64]{1,2,0:T(8,128)S(1)} custom-call(f32[1,64,64]{2,1,0:T(8,128)S(1)} %fusion.6), custom_call_target="InvertDiagBlocksLowerTriangular" | custom-call | tf_op jit(solution)/shard_map/triangular_solve/custom-call.0 | solution.py:327
  220.2 0.3 fusion.2
  220.5 1.7 convolution_multiply_fusion.1
  (3 shorter events, 0.1 us)

commit v11 on v10

--- a/solution.py
+++ b/solution.py
@@ -321,7 +321,35 @@
     )(slot_ids, live_count.reshape(1), src, tile_set)
 
 
+def _lower_inverse_kernel(m_ref, out_ref):
+    rows, cols = m_ref.shape
+    row = lax.broadcasted_iota(jnp.int32, (rows, cols), 0)
+    lane = lax.broadcasted_iota(jnp.int32, (rows, cols), 1)
+
+    def step(j, m):
+        pivot_row = jnp.sum(jnp.where(row == j, m, 0.0), axis=0, keepdims=True)
+        pivot = jnp.sum(jnp.where(lane[:1] == j, pivot_row, 0.0), axis=1, keepdims=True)
+        root = jnp.sqrt(pivot)
+        scaled_row = pivot_row / root
+        column = jnp.sum(jnp.where(lane == j, m, 0.0), axis=1, keepdims=True) / root
+        return jnp.where(row == j, scaled_row, jnp.where(row > j, m - column * scaled_row, m))
+
+    out_ref[...] = lax.fori_loop(0, rows, step, m_ref[...])
+
+
 def lower_inverse(gram):
+    width = gram.shape[0]
+    augmented = jnp.concatenate([gram, jnp.eye(width, dtype=gram.dtype)], axis=1)
+    reduced = pl.pallas_call(
+        _lower_inverse_kernel,
+        out_shape=jax.ShapeDtypeStruct(augmented.shape, augmented.dtype),
+        in_specs=[pl.BlockSpec(memory_space=pltpu.VMEM)],
+        out_specs=pl.BlockSpec(memory_space=pltpu.VMEM),
+    )(augmented)
+    return reduced[:, width:]
+
+
+def lower_inverse_native(gram):
     lower = lax.linalg.cholesky(gram, symmetrize_input=False)
     eye = jnp.eye(gram.shape[0], dtype=gram.dtype)
     return lax.linalg.triangular_solve(lower, eye, left_side=True, lower=True)

time: 223 us -> 216 us (0.969)
  other arithmetic: 28.4 us -> 5.69 us
  Pallas kernels: 187 us -> 202 us
    another operation x10 -> x0, other arithmetic: 25.6 us -> none  [the longest x6 14.5 us: lower_inverse(): lower = lax.linalg.cholesky(gram, symmetrize_input=False)]
    pallas_call x0 -> x2, Pallas kernels: none -> 16.9 us  [lower_inverse(): pl.pallas_call(_lower_inverse_kernel, out_shape=jax.ShapeDtypeStruct(augm...]
    concatenate x0 -> x2, other arithmetic: none -> 2.91 us  [lower_inverse(): jnp.concatenate([gram, jnp.eye(width, dtype=gram.dtype)], axis=1)]
where the time goes in v11:
time: 216 us; the launch traced here: 214 us
  Pallas kernels  202 us (94%)
  other arithmetic  5.69 us (3%)
  matrix products  4.1 us (2%)
    pallas_call x2, Pallas kernels, product_gram(): pl.pallas_call(functools.partial(_product_gram_kernel, row_factors=tuple(...  92.6 us
    pallas_call x3, Pallas kernels, staged(): pl.pallas_call(functools.partial(_staged_kernel, axis=axis, factors=tuple...  74.1 us
    pallas_call x4, Pallas kernels, tile_products(): pl.pallas_call(functools.partial(_products_kernel, forward=forward), out_...  18.1 us
    pallas_call x2, Pallas kernels, lower_inverse(): pl.pallas_call(_lower_inverse_kernel, out_shape=jax.ShapeDtypeStruct(augm...  16.9 us

profile of v11, /device:TPU:6, one launch (start us, length us, event | category | flops | bytes accessed | tf_op | source)
XLA Modules:
  0.0 213.6 jit_solution(18169501649842572540)
XLA Ops:
  0.0 0.7 convert_rsqrt_fusion
  0.7 0.6 dynamic-slice_bitcast_fusion.1.refs_1_
  1.3 0.7 convert_rsqrt_fusion.1
  2.0 0.1 dynamic_slice.17
  2.1 1.4 multiply_convert_fusion.refs_0_
  3.4 16.3 %shard_map.64.src_ref = bf16[8,64,256]{2,1,0:T(8,128)(2,1)} custom-call(bf16[64,128]{1,0:T(8,128)(2,1)} %multiply_convert_fusion.refs_0_), custom_call_target="tpu_custom_call" | custom-call | bytes 1048576 | tf_op jit(solution)/shard_map/pallas_call | solution.py:238
  20.3 4.8 %shard_map.65 = f32[8,64,256]{2,1,0:T(8,128)} custom-call(s32[2,32]{1,0:T(2,128)} %bitcast.42, s32[1]{0:T(128)} %bitcast.26.count_ref, bf16[8,64,256]{2,1,0:T(8,128)(2,1)} %shard_map.64.src_ref, bf16[32,256,256]{2,1,0:T(8,128)(2,1)} %bitcast.30), custom_call_target="tpu_custom_call" | custom-call | flops 268435456 | bytes 4980736 | tf_op jit(solution)/shard_map/pallas_call | solution.py:303
  25.2 31.5 %shard_map.66 = bf16[4,4,2,16,256]{4,3,2,1,0:T(8,128)(2,1)} custom-call(f32[4,4,2,16,256]{4,3,2,1,0:T(8,128)} %bitcast.37, f32[1,256]{1,0:T(1,128)} %dynamic-slice_bitcast_fusion.1.refs_1_), custom_call_target="tpu_custom_call" | custom-call | bytes 1048576 | tf_op jit(solution)/shard_map/pallas_call | solution.py:238
  56.7 4.3 %shard_map.67 = f32[8,64,256]{2,1,0:T(8,128)} custom-call(s32[2,32]{1,0:T(2,128)} %bitcast.43, s32[1]{0:T(128)} %bitcast.27.count_ref, bf16[8,64,256]{2,1,0:T(8,128)(2,1)} %bitcast.39, bf16[32,256,256]{2,1,0:T(8,128)(2,1)} %bitcast.31), custom_call_target="tpu_custom_call" | custom-call | flops 268435456 | bytes 4980736 | tf_op jit(solution)/shard_map/pallas_call | solution.py:303
  61.0 0.6 dynamic-slice_bitcast_fusion.s_ref
  61.5 47.1 %shard_map.68 = (f32[4,4,32,256]{3,2,1,0:T(8,128)}, f32[64,64]{1,0:T(8,128)}) custom-call(f32[4,4,32,256]{3,2,1,0:T(8,128)} %bitcast.34, f32[1,256]{1,0:T(1,128)} %dynamic-slice_bitcast_fusion.s_ref), custom_call_target="tpu_custom_call" | custom-call | bytes 1048576 | tf_op jit(solution)/shard_map/pallas_call | solution.py:199
  108.6 1.5 pad_maximum_fusion.m_ref
  110.1 8.5 %shard_map.69 = f32[64,128]{1,0:T(8,128)} custom-call(f32[64,128]{1,0:T(8,128)} %pad_maximum_fusion.m_ref), custom_call_target="tpu_custom_call" | custom-call | tf_op jit(solution)/shard_map/pallas_call | solution.py:343
  118.6 2.4 %fusion.1.src_ref = bf16[8,64,256]{2,1,0:T(8,128)(2,1)} fusion(f32[8,64,256]{2,1,0:T(8,128)} %bitcast.40, f32[8,256]{1,0:T(8,128)S(1)} %mul.34, f32[64,128]{1,0:T(8,128)} %shard_map.69), kind=kOutput, calls=%fused_computation.2 | convolution fusion | flops 100925440 | bytes 827392 | tf_op jit(solution)/shard_map/rs,psi->pri/dot_general | solution.py:387
  121.0 4.8 %shard_map.70 = f32[8,64,256]{2,1,0:T(8,128)} custom-call(s32[2,32]{1,0:T(2,128)} %bitcast.44, s32[1]{0:T(128)} %bitcast.28.count_ref, bf16[8,64,256]{2,1,0:T(8,128)(2,1)} %fusion.1.src_ref, bf16[32,256,256]{2,1,0:T(8,128)(2,1)} %bitcast.32), custom_call_target="tpu_custom_call" | custom-call | flops 268435456 | bytes 4980736 | tf_op jit(solution)/shard_map/pallas_call | solution.py:303
  125.8 26.3 %shard_map.71 = bf16[4,4,2,16,256]{4,3,2,1,0:T(8,128)(2,1)} custom-call(f32[4,4,2,16,256]{4,3,2,1,0:T(8,128)} %bitcast.36, f32[1,256]{1,0:T(1,128)} %dynamic-slice_bitcast_fusion.1.refs_1_), custom_call_target="tpu_custom_call" | custom-call | bytes 1048576 | tf_op jit(solution)/shard_map/pallas_call | solution.py:238
  152.1 4.3 %shard_map.72 = f32[8,64,256]{2,1,0:T(8,128)} custom-call(s32[2,32]{1,0:T(2,128)} %bitcast.45, s32[1]{0:T(128)} %bitcast.29.count_ref, bf16[8,64,256]{2,1,0:T(8,128)(2,1)} %bitcast.38, bf16[32,256,256]{2,1,0:T(8,128)(2,1)} %bitcast.33), custom_call_target="tpu_custom_call" | custom-call | flops 268435456 | bytes 4980736 | tf_op jit(solution)/shard_map/pallas_call | solution.py:303
  156.4 45.6 %shard_map.73 = (f32[4,4,32,256]{3,2,1,0:T(8,128)}, f32[64,64]{1,0:T(8,128)}) custom-call(f32[4,4,32,256]{3,2,1,0:T(8,128)} %bitcast.35, f32[1,256]{1,0:T(1,128)} %dynamic-slice_bitcast_fusion.s_ref), custom_call_target="tpu_custom_call" | custom-call | bytes 1048576 | tf_op jit(solution)/shard_map/pallas_call | solution.py:199
  201.9 1.5 pad_maximum_fusion.1.m_ref
  203.4 8.5 %shard_map.74 = f32[64,128]{1,0:T(8,128)} custom-call(f32[64,128]{1,0:T(8,128)} %pad_maximum_fusion.1.m_ref), custom_call_target="tpu_custom_call" | custom-call | tf_op jit(solution)/shard_map/pallas_call | solution.py:343
  211.9 1.7 convolution_multiply_fusion.1
  (2 shorter events, 0.0 us)

commit v12 on v11

--- a/solution.py
+++ b/solution.py
@@ -174,10 +174,14 @@
     for p in range(n * per // width):
         parts = [y_ref[_digits(p * width // per + i, row_factors)] for i in range(width // per)]
         block = jnp.concatenate(parts, axis=0)
-        term = lax.dot_general(block, block, (((1,), (1,)), ((), ())), precision=HIGH,
+        padded = jnp.concatenate([block, jnp.zeros_like(block)], axis=0)
+        term = lax.dot_general(block, padded, (((1,), (1,)), ((), ())), precision=HIGH,
                                preferred_element_type=jnp.float32)
         gram = term if gram is None else gram + term
-    g_ref[...] = _sum(cols, sems, 4, gram, cbufs, pending)
+    total = _sum(cols, sems, 4, gram, cbufs, pending)
+    row = lax.broadcasted_iota(jnp.int32, total.shape, 0)
+    lane = lax.broadcasted_iota(jnp.int32, total.shape, 1)
+    g_ref[...] = _eliminate(total + jnp.where(lane == row + width, 1.0, 0.0))
     for c in pending:
         c.wait_send()
 
@@ -192,7 +196,7 @@
                                   jnp.float32))
     scratch.append(pltpu.VMEM(tuple(reversed(row_factors)) + chunk, jnp.float32))
     for s in range(len(col_factors)):
-        scratch.append(pltpu.VMEM((col_factors[s], width, width), jnp.float32))
+        scratch.append(pltpu.VMEM((col_factors[s], width, 2 * width), jnp.float32))
     scratch.append(pltpu.SemaphoreType.DMA((6, max(len(row_factors), len(col_factors)),
                                             max(row_factors + col_factors))))
     nbytes = n * math.prod(chunk) * 4
@@ -200,14 +204,14 @@
         functools.partial(_product_gram_kernel, row_factors=tuple(row_factors),
                           col_factors=tuple(col_factors)),
         out_shape=(jax.ShapeDtypeStruct(tuple(reversed(row_factors)) + chunk, jnp.float32),
-                   jax.ShapeDtypeStruct((width, width), jnp.float32)),
+                   jax.ShapeDtypeStruct((width, 2 * width), jnp.float32)),
         in_specs=[pl.BlockSpec(memory_space=pltpu.VMEM)] * 2,
         out_specs=(pl.BlockSpec(memory_space=pltpu.VMEM), pl.BlockSpec(memory_space=pltpu.VMEM)),
         scratch_shapes=scratch,
         compiler_params=pltpu.CompilerParams(collective_id=cid, has_side_effects=True),
         cost_estimate=pl.CostEstimate(flops=0, transcendentals=0, bytes_accessed=2 * nbytes),
     )(x, scale)
-    return y.reshape((n,) + chunk), g
+    return y.reshape((n,) + chunk), g[:, width:]
 
 
 def staged(x, axis, factors, mode, cid, scale=None, epilogue=None, out_dtype=None, tiled=None):
@@ -321,20 +325,24 @@
     )(slot_ids, live_count.reshape(1), src, tile_set)
 
 
-def _lower_inverse_kernel(m_ref, out_ref):
-    rows, cols = m_ref.shape
+def _eliminate(m):
+    rows, cols = m.shape
     row = lax.broadcasted_iota(jnp.int32, (rows, cols), 0)
     lane = lax.broadcasted_iota(jnp.int32, (rows, cols), 1)
 
     def step(j, m):
         pivot_row = jnp.sum(jnp.where(row == j, m, 0.0), axis=0, keepdims=True)
         pivot = jnp.sum(jnp.where(lane[:1] == j, pivot_row, 0.0), axis=1, keepdims=True)
-        root = jnp.sqrt(pivot)
-        scaled_row = pivot_row / root
-        column = jnp.sum(jnp.where(lane == j, m, 0.0), axis=1, keepdims=True) / root
+        inv_root = 1.0 / jnp.sqrt(pivot)
+        scaled_row = pivot_row * inv_root
+        column = jnp.sum(jnp.where(lane == j, m, 0.0), axis=1, keepdims=True) * inv_root
         return jnp.where(row == j, scaled_row, jnp.where(row > j, m - column * scaled_row, m))
 
-    out_ref[...] = lax.fori_loop(0, rows, step, m_ref[...])
+    return lax.fori_loop(0, rows, step, m, unroll=2)
+
+
+def _lower_inverse_kernel(m_ref, out_ref):
+    out_ref[...] = _eliminate(m_ref[...])
 
 
 def lower_inverse(gram):
@@ -394,12 +402,11 @@
         product_partial = tile_products(
             slot_ids, live_count, query_tiles_panel, tile_set, product_tiles, False
         )
-        lifted_pieces, gram = product_gram(
+        lifted_pieces, inverse = product_gram(
             product_partial.reshape(n_row, width // p_per_tile, side), my_pscale, ROW_FACTORS,
             GRAM_FACTORS, 2, width,
         )
         lifted_tiles = lifted_pieces.reshape(product_tiles, width, side)
-        inverse = lower_inverse(gram)
     my_tile = lax.dynamic_index_in_dim(lifted_tiles, row_at // per_tile, keepdims=False)
     my_lifted = lax.dynamic_slice_in_dim(my_tile, (row_at % per_tile) * share, share, axis=1)
     return jnp.einsum("rs,si->ri", inverse, my_lifted, precision=HIGH) * root_count

time: 216 us -> 209 us (0.968)
  other arithmetic: 5.69 us -> 2.77 us
    pallas_call x2 -> x0, Pallas kernels: 16.9 us -> none  [lower_inverse(): pl.pallas_call(_lower_inverse_kernel, out_shape=jax.ShapeDtypeStruct(augm...]
    pallas_call x2, Pallas kernels: 92.6 us -> 107 us  [product_gram(): pl.pallas_call(functools.partial(_product_gram_kernel, row_factors=tuple(...]
    concatenate x2 -> x0, other arithmetic: 2.91 us -> none  [lower_inverse(): jnp.concatenate([gram, jnp.eye(width, dtype=gram.dtype)], axis=1)]
where the time goes in v12:
time: 209 us
  Pallas kernels  200 us (96%)
  matrix products  4.08 us (2%)
  other arithmetic  2.77 us (1%)
    pallas_call x2, Pallas kernels, product_gram(): pl.pallas_call(functools.partial(_product_gram_kernel, row_factors=tuple(...  107 us
    pallas_call x3, Pallas kernels, staged(): pl.pallas_call(functools.partial(_staged_kernel, axis=axis, factors=tuple...  74.3 us
    pallas_call x4, Pallas kernels, tile_products(): pl.pallas_call(functools.partial(_products_kernel, forward=forward), out_...  18.2 us

profile of v12, /device:TPU:6, one launch (start us, length us, event | category | flops | bytes accessed | tf_op | source)
XLA Modules:
  0.0 208.7 jit_solution(3122061017251176365)
XLA Ops:
  0.7 0.7 convert_rsqrt_fusion.1
  1.4 0.1 dynamic_slice.17
  1.4 0.6 dynamic-slice_bitcast_fusion.s_ref
  2.0 0.7 convert_rsqrt_fusion
  2.7 0.5 dynamic-slice_bitcast_fusion.1.refs_1_
  3.2 1.4 multiply_convert_fusion.refs_0_
  4.6 16.3 %shard_map.64.src_ref = bf16[8,64,256]{2,1,0:T(8,128)(2,1)} custom-call(bf16[64,128]{1,0:T(8,128)(2,1)} %multiply_convert_fusion.refs_0_), custom_call_target="tpu_custom_call" | custom-call | bytes 1048576 | tf_op jit(solution)/shard_map/pallas_call | solution.py:242
  20.9 4.8 %shard_map.65 = f32[8,64,256]{2,1,0:T(8,128)} custom-call(s32[2,32]{1,0:T(2,128)} %bitcast.42, s32[1]{0:T(128)} %bitcast.26.count_ref, bf16[8,64,256]{2,1,0:T(8,128)(2,1)} %shard_map.64.src_ref, bf16[32,256,256]{2,1,0:T(8,128)(2,1)} %bitcast.30), custom_call_target="tpu_custom_call" | custom-call | flops 268435456 | bytes 4980736 | tf_op jit(solution)/shard_map/pallas_call | solution.py:307
  25.7 31.5 %shard_map.66 = bf16[4,4,2,16,256]{4,3,2,1,0:T(8,128)(2,1)} custom-call(f32[4,4,2,16,256]{4,3,2,1,0:T(8,128)} %bitcast.37, f32[1,256]{1,0:T(1,128)} %dynamic-slice_bitcast_fusion.1.refs_1_), custom_call_target="tpu_custom_call" | custom-call | bytes 1048576 | tf_op jit(solution)/shard_map/pallas_call | solution.py:242
  57.2 4.3 %shard_map.67 = f32[8,64,256]{2,1,0:T(8,128)} custom-call(s32[2,32]{1,0:T(2,128)} %bitcast.43, s32[1]{0:T(128)} %bitcast.27.count_ref, bf16[8,64,256]{2,1,0:T(8,128)(2,1)} %bitcast.39, bf16[32,256,256]{2,1,0:T(8,128)(2,1)} %bitcast.31), custom_call_target="tpu_custom_call" | custom-call | flops 268435456 | bytes 4980736 | tf_op jit(solution)/shard_map/pallas_call | solution.py:307
  61.5 54.1 %shard_map.68 = (f32[4,4,32,256]{3,2,1,0:T(8,128)}, f32[64,128]{1,0:T(8,128)}) custom-call(f32[4,4,32,256]{3,2,1,0:T(8,128)} %bitcast.35, f32[1,256]{1,0:T(1,128)} %dynamic-slice_bitcast_fusion.s_ref), custom_call_target="tpu_custom_call" | custom-call | bytes 1048576 | tf_op jit(solution)/shard_map/pallas_call | solution.py:203
  115.6 2.4 %fusion.1.src_ref = bf16[8,64,256]{2,1,0:T(8,128)(2,1)} fusion(f32[8,64,256]{2,1,0:T(8,128)} %bitcast.40, f32[8,256]{1,0:T(8,128)S(1)} %mul.34, f32[64,128]{1,0:T(8,128)} %get-tuple-element.10), kind=kOutput, calls=%fused_computation.2 | convolution fusion | flops 100925440 | bytes 827392 | tf_op jit(solution)/shard_map/rs,psi->pri/dot_general | solution.py:395
  118.0 4.8 %shard_map.69 = f32[8,64,256]{2,1,0:T(8,128)} custom-call(s32[2,32]{1,0:T(2,128)} %bitcast.44, s32[1]{0:T(128)} %bitcast.28.count_ref, bf16[8,64,256]{2,1,0:T(8,128)(2,1)} %fusion.1.src_ref, bf16[32,256,256]{2,1,0:T(8,128)(2,1)} %bitcast.32), custom_call_target="tpu_custom_call" | custom-call | flops 268435456 | bytes 4980736 | tf_op jit(solution)/shard_map/pallas_call | solution.py:307
  122.8 26.5 %shard_map.70 = bf16[4,4,2,16,256]{4,3,2,1,0:T(8,128)(2,1)} custom-call(f32[4,4,2,16,256]{4,3,2,1,0:T(8,128)} %bitcast.36, f32[1,256]{1,0:T(1,128)} %dynamic-slice_bitcast_fusion.1.refs_1_), custom_call_target="tpu_custom_call" | custom-call | bytes 1048576 | tf_op jit(solution)/shard_map/pallas_call | solution.py:242
  149.3 4.3 %shard_map.71 = f32[8,64,256]{2,1,0:T(8,128)} custom-call(s32[2,32]{1,0:T(2,128)} %bitcast.45, s32[1]{0:T(128)} %bitcast.29.count_ref, bf16[8,64,256]{2,1,0:T(8,128)(2,1)} %bitcast.38, bf16[32,256,256]{2,1,0:T(8,128)(2,1)} %bitcast.33), custom_call_target="tpu_custom_call" | custom-call | flops 268435456 | bytes 4980736 | tf_op jit(solution)/shard_map/pallas_call | solution.py:307
  153.5 53.4 %shard_map.72 = (f32[4,4,32,256]{3,2,1,0:T(8,128)}, f32[64,128]{1,0:T(8,128)}) custom-call(f32[4,4,32,256]{3,2,1,0:T(8,128)} %bitcast.34, f32[1,256]{1,0:T(1,128)} %dynamic-slice_bitcast_fusion.s_ref), custom_call_target="tpu_custom_call" | custom-call | bytes 1048576 | tf_op jit(solution)/shard_map/pallas_call | solution.py:203
  207.0 1.7 convolution_multiply_fusion.1
  (1 shorter events, 0.0 us)

commit v13 on v12

--- a/solution.py
+++ b/solution.py
@@ -270,7 +270,11 @@
 GROUP = 8
 
 
-def _products_kernel(ids_ref, count_ref, src_ref, tiles_hbm, out_ref, tiles, sems, *, forward):
+def _products_kernel(*refs, forward, lift):
+    if lift:
+        ids_ref, count_ref, inv_ref, lifted_ref, scale_ref, tiles_hbm, out_ref, tiles, sems, src_ref = refs
+    else:
+        ids_ref, count_ref, src_ref, tiles_hbm, out_ref, tiles, sems = refs
     slots = tiles.shape[0]
     groups = slots // GROUP
 
@@ -281,6 +285,11 @@
 
     for g in range(groups):
         fetch(g).start()
+    if lift:
+        inv = inv_ref[...]
+        for p in range(src_ref.shape[0]):
+            current = jnp.dot(inv, lifted_ref[p], precision=HIGH, preferred_element_type=jnp.float32)
+            src_ref[p] = (current * scale_ref[p]).astype(src_ref.dtype)
     out_ref[...] = jnp.zeros_like(out_ref)
     src_row, dst_row = (1, 0) if forward else (0, 1)
     count = count_ref[0]
@@ -301,28 +310,28 @@
             out_ref[d] = out_ref[d] + y
 
 
-def tile_products(slot_ids, live_count, src, tile_set, blocks, forward):
+def tile_products(slot_ids, live_count, src, tile_set, blocks, forward, lift=None):
     slots, side, _ = tile_set.shape
-    width = src.shape[1]
+    width = src.shape[1] if lift is None else lift[1].shape[1]
+    scratch = [pltpu.VMEM(tile_set.shape, tile_set.dtype), pltpu.SemaphoreType.DMA((slots // GROUP,))]
+    if lift is None:
+        operands = (src,)
+    else:
+        operands = lift
+        scratch.append(pltpu.VMEM(lift[1].shape, jnp.bfloat16))
+    vmem = pl.BlockSpec(memory_space=pltpu.VMEM)
+    smem = pl.BlockSpec(memory_space=pltpu.SMEM)
     return pl.pallas_call(
-        functools.partial(_products_kernel, forward=forward),
+        functools.partial(_products_kernel, forward=forward, lift=lift is not None),
         out_shape=jax.ShapeDtypeStruct((blocks, width, side), jnp.float32),
-        in_specs=[
-            pl.BlockSpec(memory_space=pltpu.SMEM),
-            pl.BlockSpec(memory_space=pltpu.SMEM),
-            pl.BlockSpec(memory_space=pltpu.VMEM),
-            pl.BlockSpec(memory_space=pl.ANY),
-        ],
-        out_specs=pl.BlockSpec(memory_space=pltpu.VMEM),
-        scratch_shapes=[
-            pltpu.VMEM(tile_set.shape, tile_set.dtype),
-            pltpu.SemaphoreType.DMA((slots // GROUP,)),
-        ],
+        in_specs=[smem, smem] + [vmem] * len(operands) + [pl.BlockSpec(memory_space=pl.ANY)],
+        out_specs=vmem,
+        scratch_shapes=scratch,
         cost_estimate=pl.CostEstimate(
             flops=2 * slots * width * side * side, transcendentals=0,
-            bytes_accessed=slots * side * side * 2 + src.size * 2 + blocks * width * side * 4,
+            bytes_accessed=slots * side * side * 2 + blocks * width * side * 6,
         ),
-    )(slot_ids, live_count.reshape(1), src, tile_set)
+    )(slot_ids, live_count.reshape(1), *operands, tile_set)
 
 
 def _eliminate(m):
@@ -392,9 +401,10 @@
     per_tile = side // share
     for iteration in range(ITERS):
         if iteration:
-            current_tiles = jnp.einsum("rs,psi->pri", inverse, lifted_tiles, precision=HIGH)
-            scaled_tiles = (current_tiles * pscale).astype(jnp.bfloat16)
-        partial_sum = tile_products(slot_ids, live_count, scaled_tiles, tile_set, query_tiles, True)
+            partial_sum = tile_products(slot_ids, live_count, None, tile_set, query_tiles, True,
+                                        lift=(inverse, lifted_tiles, pscale))
+        else:
+            partial_sum = tile_products(slot_ids, live_count, scaled_tiles, tile_set, query_tiles, True)
         query_tiles_panel = staged(
             partial_sum.reshape(n_col, width // q_per_tile, side), "col", QUERY_FACTORS, "reduce", 1,
             scale=my_qscale, epilogue=_query_epilogue, out_dtype=jnp.bfloat16,

time: 209 us -> 209 us (level)
  matrix products: 4.08 us -> 1.72 us
    dot_general x1 -> x0, matrix products: 2.36 us -> none  [shards(): jnp.einsum('rs,psi->pri', inverse, lifted_tiles, precision=HIGH)]
where the time goes in v13:
time: 209 us; the launch traced here: 207 us
  Pallas kernels  199 us (95%)
  other arithmetic  2.77 us (1%)
  local copies, waits for them, and re-layouts  2.69 us (1%)
    pallas_call x2, Pallas kernels, product_gram(): pl.pallas_call(functools.partial(_product_gram_kernel, row_factors=tuple(...  107 us
    pallas_call x3, Pallas kernels, staged(): pl.pallas_call(functools.partial(_staged_kernel, axis=axis, factors=tuple...  74.2 us
    pallas_call x4, Pallas kernels, tile_products(): pl.pallas_call(functools.partial(_products_kernel, forward=forward, lift=...  18.3 us

profile of v13, /device:TPU:6, one launch (start us, length us, event | category | flops | bytes accessed | tf_op | source)
XLA Modules:
  0.0 207.2 jit_solution(15658914136690761335)
XLA Ops:
  0.7 0.7 convert_rsqrt_fusion.1
  1.4 0.0 copy-start
  1.4 0.1 dynamic_slice.17
  1.4 0.6 dynamic-slice_bitcast_fusion.s_ref
  2.0 0.7 convert_rsqrt_fusion
  2.7 0.6 dynamic-slice_bitcast_fusion.1.refs_1_
  3.3 1.4 multiply_convert_fusion.refs_0_
  4.7 16.3 %shard_map.64.refs_2_ = bf16[8,64,256]{2,1,0:T(8,128)(2,1)} custom-call(bf16[64,128]{1,0:T(8,128)(2,1)} %multiply_convert_fusion.refs_0_), custom_call_target="tpu_custom_call" | custom-call | bytes 1048576 | tf_op jit(solution)/shard_map/pallas_call | solution.py:242
  20.9 4.8 %shard_map.65 = f32[8,64,256]{2,1,0:T(8,128)} custom-call(s32[2,32]{1,0:T(2,128)} %bitcast.37, s32[1]{0:T(128)} %bitcast.20.refs_1_, bf16[8,64,256]{2,1,0:T(8,128)(2,1)} %shard_map.64.refs_2_, bf16[32,256,256]{2,1,0:T(8,128)(2,1)} %bitcast.24), custom_call_target="tpu_custom_call" | custom-call | flops 268435456 | bytes 4980736 | tf_op jit(solution)/shard_map/pallas_call | solution.py:324
  25.8 31.5 %shard_map.66 = bf16[4,4,2,16,256]{4,3,2,1,0:T(8,128)(2,1)} custom-call(f32[4,4,2,16,256]{4,3,2,1,0:T(8,128)} %bitcast.31, f32[1,256]{1,0:T(1,128)} %dynamic-slice_bitcast_fusion.1.refs_1_), custom_call_target="tpu_custom_call" | custom-call | bytes 1048576 | tf_op jit(solution)/shard_map/pallas_call | solution.py:242
  57.3 4.3 %shard_map.67 = f32[8,64,256]{2,1,0:T(8,128)} custom-call(s32[2,32]{1,0:T(2,128)} %bitcast.38, s32[1]{0:T(128)} %bitcast.21.refs_1_, bf16[8,64,256]{2,1,0:T(8,128)(2,1)} %bitcast.33, bf16[32,256,256]{2,1,0:T(8,128)(2,1)} %bitcast.25), custom_call_target="tpu_custom_call" | custom-call | flops 268435456 | bytes 4980736 | tf_op jit(solution)/shard_map/pallas_call | solution.py:324
  61.6 0.0 copy-done
  61.6 54.1 %shard_map.68 = (f32[4,4,32,256]{3,2,1,0:T(8,128)}, f32[64,128]{1,0:T(8,128)}) custom-call(f32[4,4,32,256]{3,2,1,0:T(8,128)} %bitcast.30, f32[1,256]{1,0:T(1,128)} %dynamic-slice_bitcast_fusion.s_ref), custom_call_target="tpu_custom_call" | custom-call | bytes 1048576 | tf_op jit(solution)/shard_map/pallas_call | solution.py:203
  115.7 1.4 slice.6.refs_2_
  117.1 4.9 %shard_map.69 = f32[8,64,256]{2,1,0:T(8,128)} custom-call(s32[2,32]{1,0:T(2,128)} %bitcast.39, s32[1]{0:T(128)} %bitcast.22.refs_1_, f32[64,64]{1,0:T(8,128)} %slice.6.refs_2_, f32[8,64,256]{2,1,0:T(8,128)} %bitcast.34, f32[8,1,256]{2,1,0:T(1,128)} %bitcast.36, bf16[32,256,256]{2,1,0:T(8,128)(2,1)} %bitcast.26), custom_call_target="tpu_custom_call" | custom-call | flops 268435456 | bytes 4980736 | tf_op jit(solution)/shard_map/pallas_call | solution.py:324
  122.1 26.4 %shard_map.70 = bf16[4,4,2,16,256]{4,3,2,1,0:T(8,128)(2,1)} custom-call(f32[4,4,2,16,256]{4,3,2,1,0:T(8,128)} %bitcast.29, f32[1,256]{1,0:T(1,128)} %dynamic-slice_bitcast_fusion.1.refs_1_), custom_call_target="tpu_custom_call" | custom-call | bytes 1048576 | tf_op jit(solution)/shard_map/pallas_call | solution.py:242
  148.5 4.3 %shard_map.71 = f32[8,64,256]{2,1,0:T(8,128)} custom-call(s32[2,32]{1,0:T(2,128)} %bitcast.40, s32[1]{0:T(128)} %bitcast.23.refs_1_, bf16[8,64,256]{2,1,0:T(8,128)(2,1)} %bitcast.32, bf16[32,256,256]{2,1,0:T(8,128)(2,1)} %bitcast.27), custom_call_target="tpu_custom_call" | custom-call | flops 268435456 | bytes 4980736 | tf_op jit(solution)/shard_map/pallas_call | solution.py:324
  152.8 52.7 %shard_map.72 = (f32[4,4,32,256]{3,2,1,0:T(8,128)}, f32[64,128]{1,0:T(8,128)}) custom-call(f32[4,4,32,256]{3,2,1,0:T(8,128)} %bitcast.28, f32[1,256]{1,0:T(1,128)} %dynamic-slice_bitcast_fusion.s_ref), custom_call_target="tpu_custom_call" | custom-call | bytes 1048576 | tf_op jit(solution)/shard_map/pallas_call | solution.py:203
  205.5 1.7 convolution_multiply_fusion
Async XLA Ops:
  1.4 60.2 %copy-start = (f32[2048]{0:T(1024)}, f32[2048]{0:T(1024)S(1)}, u32[]{:S(2)}) copy-start(f32[2048]{0:T(1024)S(1)} %convert_rsqrt_fusion.1) | copy-start | bytes 24580

commit v14 on v13

--- a/solution.py
+++ b/solution.py
@@ -347,7 +347,7 @@
         column = jnp.sum(jnp.where(lane == j, m, 0.0), axis=1, keepdims=True) * inv_root
         return jnp.where(row == j, scaled_row, jnp.where(row > j, m - column * scaled_row, m))
 
-    return lax.fori_loop(0, rows, step, m, unroll=2)
+    return lax.fori_loop(0, rows, step, m, unroll=4)
 
 
 def _lower_inverse_kernel(m_ref, out_ref):

time: 209 us -> 209 us (level)
  no operation moved by 1% of the time
where the time goes in v14:
time: 209 us; the launch traced here: 208 us
  Pallas kernels  200 us (96%)
  other arithmetic  2.77 us (1%)
  local copies, waits for them, and re-layouts  2.69 us (1%)
    pallas_call x2, Pallas kernels, product_gram(): pl.pallas_call(functools.partial(_product_gram_kernel, row_factors=tuple(...  107 us
    pallas_call x3, Pallas kernels, staged(): pl.pallas_call(functools.partial(_staged_kernel, axis=axis, factors=tuple...  74.2 us
    pallas_call x4, Pallas kernels, tile_products(): pl.pallas_call(functools.partial(_products_kernel, forward=forward, lift=...  18.3 us

profile of v14, /device:TPU:6, one launch (start us, length us, event | category | flops | bytes accessed | tf_op | source)
XLA Modules:
  0.0 207.8 jit_solution(6406397614581388040)
XLA Ops:
  0.7 0.7 convert_rsqrt_fusion.1
  1.4 0.0 copy-start
  1.4 0.1 dynamic_slice.17
  1.4 0.6 dynamic-slice_bitcast_fusion.s_ref
  2.0 0.7 convert_rsqrt_fusion
  2.7 0.6 dynamic-slice_bitcast_fusion.1.refs_1_
  3.3 1.4 multiply_convert_fusion.refs_0_
  4.7 16.3 %shard_map.64.refs_2_ = bf16[8,64,256]{2,1,0:T(8,128)(2,1)} custom-call(bf16[64,128]{1,0:T(8,128)(2,1)} %multiply_convert_fusion.refs_0_), custom_call_target="tpu_custom_call" | custom-call | bytes 1048576 | tf_op jit(solution)/shard_map/pallas_call | solution.py:242
  20.9 4.8 %shard_map.65 = f32[8,64,256]{2,1,0:T(8,128)} custom-call(s32[2,32]{1,0:T(2,128)} %bitcast.37, s32[1]{0:T(128)} %bitcast.20.refs_1_, bf16[8,64,256]{2,1,0:T(8,128)(2,1)} %shard_map.64.refs_2_, bf16[32,256,256]{2,1,0:T(8,128)(2,1)} %bitcast.24), custom_call_target="tpu_custom_call" | custom-call | flops 268435456 | bytes 4980736 | tf_op jit(solution)/shard_map/pallas_call | solution.py:324
  25.8 31.5 %shard_map.66 = bf16[4,4,2,16,256]{4,3,2,1,0:T(8,128)(2,1)} custom-call(f32[4,4,2,16,256]{4,3,2,1,0:T(8,128)} %bitcast.31, f32[1,256]{1,0:T(1,128)} %dynamic-slice_bitcast_fusion.1.refs_1_), custom_call_target="tpu_custom_call" | custom-call | bytes 1048576 | tf_op jit(solution)/shard_map/pallas_call | solution.py:242
  57.3 4.3 %shard_map.67 = f32[8,64,256]{2,1,0:T(8,128)} custom-call(s32[2,32]{1,0:T(2,128)} %bitcast.38, s32[1]{0:T(128)} %bitcast.21.refs_1_, bf16[8,64,256]{2,1,0:T(8,128)(2,1)} %bitcast.33, bf16[32,256,256]{2,1,0:T(8,128)(2,1)} %bitcast.25), custom_call_target="tpu_custom_call" | custom-call | flops 268435456 | bytes 4980736 | tf_op jit(solution)/shard_map/pallas_call | solution.py:324
  61.6 0.0 copy-done
  61.6 54.0 %shard_map.68 = (f32[4,4,32,256]{3,2,1,0:T(8,128)}, f32[64,128]{1,0:T(8,128)}) custom-call(f32[4,4,32,256]{3,2,1,0:T(8,128)} %bitcast.30, f32[1,256]{1,0:T(1,128)} %dynamic-slice_bitcast_fusion.s_ref), custom_call_target="tpu_custom_call" | custom-call | bytes 1048576 | tf_op jit(solution)/shard_map/pallas_call | solution.py:203
  115.6 1.4 slice.6.refs_2_
  117.1 4.9 %shard_map.69 = f32[8,64,256]{2,1,0:T(8,128)} custom-call(s32[2,32]{1,0:T(2,128)} %bitcast.39, s32[1]{0:T(128)} %bitcast.22.refs_1_, f32[64,64]{1,0:T(8,128)} %slice.6.refs_2_, f32[8,64,256]{2,1,0:T(8,128)} %bitcast.34, f32[8,1,256]{2,1,0:T(1,128)} %bitcast.36, bf16[32,256,256]{2,1,0:T(8,128)(2,1)} %bitcast.26), custom_call_target="tpu_custom_call" | custom-call | flops 268435456 | bytes 4980736 | tf_op jit(solution)/shard_map/pallas_call | solution.py:324
  122.0 26.4 %shard_map.70 = bf16[4,4,2,16,256]{4,3,2,1,0:T(8,128)(2,1)} custom-call(f32[4,4,2,16,256]{4,3,2,1,0:T(8,128)} %bitcast.29, f32[1,256]{1,0:T(1,128)} %dynamic-slice_bitcast_fusion.1.refs_1_), custom_call_target="tpu_custom_call" | custom-call | bytes 1048576 | tf_op jit(solution)/shard_map/pallas_call | solution.py:242
  148.4 4.3 %shard_map.71 = f32[8,64,256]{2,1,0:T(8,128)} custom-call(s32[2,32]{1,0:T(2,128)} %bitcast.40, s32[1]{0:T(128)} %bitcast.23.refs_1_, bf16[8,64,256]{2,1,0:T(8,128)(2,1)} %bitcast.32, bf16[32,256,256]{2,1,0:T(8,128)(2,1)} %bitcast.27), custom_call_target="tpu_custom_call" | custom-call | flops 268435456 | bytes 4980736 | tf_op jit(solution)/shard_map/pallas_call | solution.py:324
  152.7 53.4 %shard_map.72 = (f32[4,4,32,256]{3,2,1,0:T(8,128)}, f32[64,128]{1,0:T(8,128)}) custom-call(f32[4,4,32,256]{3,2,1,0:T(8,128)} %bitcast.28, f32[1,256]{1,0:T(1,128)} %dynamic-slice_bitcast_fusion.s_ref), custom_call_target="tpu_custom_call" | custom-call | bytes 1048576 | tf_op jit(solution)/shard_map/pallas_call | solution.py:203
  206.1 1.7 convolution_multiply_fusion
Async XLA Ops:
  1.4 60.2 %copy-start = (f32[2048]{0:T(1024)}, f32[2048]{0:T(1024)S(1)}, u32[]{:S(2)}) copy-start(f32[2048]{0:T(1024)S(1)} %convert_rsqrt_fusion.1) | copy-start | bytes 24580

commit v15 on v13

--- a/solution.py
+++ b/solution.py
@@ -136,6 +136,8 @@
     else:
         if mode == "reduce":
             own = epilogue(_reduce_scatter(plan, sems, 0, x_ref, rbufs, pending)[...], s_ref)
+        elif epilogue is not None:
+            own = epilogue(x_ref[...], s_ref.at[pl.ds(plan.me, 1)])
         else:
             own = x_ref[...]
         _all_gather(plan, sems, 2, gbuf, own, pending)
@@ -263,6 +265,11 @@
     return (total * s_ref[...]).astype(jnp.bfloat16)
 
 
+def _panel_epilogue(panel, degree_ref):
+    scale = 1.0 / jnp.sqrt(degree_ref[...].astype(jnp.float32))
+    return (panel * scale).astype(jnp.bfloat16)
+
+
 def _product_epilogue(total, s_ref):
     return total * s_ref[...]
 
@@ -394,10 +401,9 @@
     my_pscale = lax.dynamic_index_in_dim(pscale, row_at // p_per_tile, keepdims=False)
     root_count = math.sqrt(product_degree.shape[0] * n_col)
 
-    panel_pscale = lax.dynamic_slice_in_dim(pscale.reshape(block), row_at * share, share)
-    scaled0 = (panel * panel_pscale[None, :]).astype(jnp.bfloat16)
-    scaled_tiles = staged(scaled0, "row", ROW_FACTORS, "gather", 0,
-                          tiled=(product_tiles, width, side))
+    scaled_tiles = staged(panel, "row", ROW_FACTORS, "gather", 0,
+                          scale=product_degree.reshape(n_row, share), epilogue=_panel_epilogue,
+                          out_dtype=jnp.bfloat16, tiled=(product_tiles, width, side))
     per_tile = side // share
     for iteration in range(ITERS):
         if iteration:

time: 209 us -> 208 us (level)
  no operation moved by 1% of the time
where the time goes in v15:
time: 208 us; the launch traced here: 206 us
  Pallas kernels  199 us (96%)
  local copies, waits for them, and re-layouts  2.62 us (1%)
    pallas_call x2, Pallas kernels, product_gram(): pl.pallas_call(functools.partial(_product_gram_kernel, row_factors=tuple(...  107 us
    pallas_call x3, Pallas kernels, staged(): pl.pallas_call(functools.partial(_staged_kernel, axis=axis, factors=tuple...  74.3 us
    pallas_call x4, Pallas kernels, tile_products(): pl.pallas_call(functools.partial(_products_kernel, forward=forward, lift=...  18.3 us

profile of v15, /device:TPU:6, one launch (start us, length us, event | category | flops | bytes accessed | tf_op | source)
XLA Modules:
  0.0 205.9 jit_solution(10362954771276776681)
XLA Ops:
  0.7 0.7 convert_rsqrt_fusion.1
  1.4 0.6 dynamic-slice_bitcast_fusion.1.refs_1_
  1.9 0.7 convert_rsqrt_fusion
  2.6 0.0 copy-start
  2.6 0.6 dynamic-slice_bitcast_fusion.s_ref
  3.2 16.3 %shard_map.64.refs_2_ = bf16[8,64,256]{2,1,0:T(8,128)(2,1)} custom-call(f32[64,128]{1,0:T(8,128)} %refs_0_.1, s32[16,128]{1,0:T(8,128)} %bitcast.38), custom_call_target="tpu_custom_call" | custom-call | bytes 1048576 | tf_op jit(solution)/shard_map/pallas_call | solution.py:244
  19.6 4.8 %shard_map.65 = f32[8,64,256]{2,1,0:T(8,128)} custom-call(s32[2,32]{1,0:T(2,128)} %bitcast.39, s32[1]{0:T(128)} %bitcast.21.refs_1_, bf16[8,64,256]{2,1,0:T(8,128)(2,1)} %shard_map.64.refs_2_, bf16[32,256,256]{2,1,0:T(8,128)(2,1)} %bitcast.25), custom_call_target="tpu_custom_call" | custom-call | flops 268435456 | bytes 4980736 | tf_op jit(solution)/shard_map/pallas_call | solution.py:331
  24.4 31.5 %shard_map.66 = bf16[4,4,2,16,256]{4,3,2,1,0:T(8,128)(2,1)} custom-call(f32[4,4,2,16,256]{4,3,2,1,0:T(8,128)} %bitcast.32, f32[1,256]{1,0:T(1,128)} %dynamic-slice_bitcast_fusion.1.refs_1_), custom_call_target="tpu_custom_call" | custom-call | bytes 1048576 | tf_op jit(solution)/shard_map/pallas_call | solution.py:244
  55.9 4.3 %shard_map.67 = f32[8,64,256]{2,1,0:T(8,128)} custom-call(s32[2,32]{1,0:T(2,128)} %bitcast.40, s32[1]{0:T(128)} %bitcast.22.refs_1_, bf16[8,64,256]{2,1,0:T(8,128)(2,1)} %bitcast.34, bf16[32,256,256]{2,1,0:T(8,128)(2,1)} %bitcast.26), custom_call_target="tpu_custom_call" | custom-call | flops 268435456 | bytes 4980736 | tf_op jit(solution)/shard_map/pallas_call | solution.py:331
  60.2 0.0 copy-done
  60.2 54.1 %shard_map.68 = (f32[4,4,32,256]{3,2,1,0:T(8,128)}, f32[64,128]{1,0:T(8,128)}) custom-call(f32[4,4,32,256]{3,2,1,0:T(8,128)} %bitcast.31, f32[1,256]{1,0:T(1,128)} %dynamic-slice_bitcast_fusion.s_ref), custom_call_target="tpu_custom_call" | custom-call | bytes 1048576 | tf_op jit(solution)/shard_map/pallas_call | solution.py:205
  114.3 1.4 slice.6.refs_2_
  115.8 4.9 %shard_map.69 = f32[8,64,256]{2,1,0:T(8,128)} custom-call(s32[2,32]{1,0:T(2,128)} %bitcast.41, s32[1]{0:T(128)} %bitcast.23.refs_1_, f32[64,64]{1,0:T(8,128)} %slice.6.refs_2_, f32[8,64,256]{2,1,0:T(8,128)} %bitcast.35, f32[8,1,256]{2,1,0:T(1,128)} %bitcast.37, bf16[32,256,256]{2,1,0:T(8,128)(2,1)} %bitcast.27), custom_call_target="tpu_custom_call" | custom-call | flops 268435456 | bytes 4980736 | tf_op jit(solution)/shard_map/pallas_call | solution.py:331
  120.7 26.4 %shard_map.70 = bf16[4,4,2,16,256]{4,3,2,1,0:T(8,128)(2,1)} custom-call(f32[4,4,2,16,256]{4,3,2,1,0:T(8,128)} %bitcast.30, f32[1,256]{1,0:T(1,128)} %dynamic-slice_bitcast_fusion.1.refs_1_), custom_call_target="tpu_custom_call" | custom-call | bytes 1048576 | tf_op jit(solution)/shard_map/pallas_call | solution.py:244
  147.1 4.3 %shard_map.71 = f32[8,64,256]{2,1,0:T(8,128)} custom-call(s32[2,32]{1,0:T(2,128)} %bitcast.42, s32[1]{0:T(128)} %bitcast.24.refs_1_, bf16[8,64,256]{2,1,0:T(8,128)(2,1)} %bitcast.33, bf16[32,256,256]{2,1,0:T(8,128)(2,1)} %bitcast.28), custom_call_target="tpu_custom_call" | custom-call | flops 268435456 | bytes 4980736 | tf_op jit(solution)/shard_map/pallas_call | solution.py:331
  151.4 52.8 %shard_map.72 = (f32[4,4,32,256]{3,2,1,0:T(8,128)}, f32[64,128]{1,0:T(8,128)}) custom-call(f32[4,4,32,256]{3,2,1,0:T(8,128)} %bitcast.29, f32[1,256]{1,0:T(1,128)} %dynamic-slice_bitcast_fusion.s_ref), custom_call_target="tpu_custom_call" | custom-call | bytes 1048576 | tf_op jit(solution)/shard_map/pallas_call | solution.py:205
  204.2 1.7 convolution_multiply_fusion
Async XLA Ops:
  2.6 57.6 %copy-start = (f32[2048]{0:T(1024)}, f32[2048]{0:T(1024)S(1)}, u32[]{:S(2)}) copy-start(f32[2048]{0:T(1024)S(1)} %convert_rsqrt_fusion) | copy-start | bytes 24580

commit v16 on v15

--- a/solution.py
+++ b/solution.py
@@ -135,6 +135,8 @@
         y_ref[...] = _sum(plan, sems, 0, x_ref[...], rbufs, pending)
     else:
         if mode == "reduce":
+            if s_ref.shape[0] > 1:
+                s_ref = s_ref.at[pl.ds(plan.me // (math.prod(factors) // s_ref.shape[0]), 1)]
             own = epilogue(_reduce_scatter(plan, sems, 0, x_ref, rbufs, pending)[...], s_ref)
         elif epilogue is not None:
             own = epilogue(x_ref[...], s_ref.at[pl.ds(plan.me, 1)])
@@ -261,8 +263,8 @@
 ROW_FACTORS = (4, 4)
 
 
-def _query_epilogue(total, s_ref):
-    return (total * s_ref[...]).astype(jnp.bfloat16)
+def _query_epilogue(total, degree_ref):
+    return (total * (1.0 / jnp.sqrt(degree_ref[...].astype(jnp.float32)))).astype(jnp.bfloat16)
 
 
 def _panel_epilogue(panel, degree_ref):
@@ -413,7 +415,8 @@
             partial_sum = tile_products(slot_ids, live_count, scaled_tiles, tile_set, query_tiles, True)
         query_tiles_panel = staged(
             partial_sum.reshape(n_col, width // q_per_tile, side), "col", QUERY_FACTORS, "reduce", 1,
-            scale=my_qscale, epilogue=_query_epilogue, out_dtype=jnp.bfloat16,
+            scale=query_degree.reshape(query_tiles, side), epilogue=_query_epilogue,
+            out_dtype=jnp.bfloat16,
         ).reshape(query_tiles, width, side)
         product_partial = tile_products(
             slot_ids, live_count, query_tiles_panel, tile_set, product_tiles, False

time: 208 us -> 208 us (level)
  no operation moved by 1% of the time
where the time goes in v16:
time: 208 us; the launch traced here: 206 us
  Pallas kernels  199 us (96%)
  local copies, waits for them, and re-layouts  3.33 us (2%)
    pallas_call x2, Pallas kernels, product_gram(): pl.pallas_call(functools.partial(_product_gram_kernel, row_factors=tuple(...  107 us
    pallas_call x3, Pallas kernels, staged(): pl.pallas_call(functools.partial(_staged_kernel, axis=axis, factors=tuple...  74.3 us
    pallas_call x4, Pallas kernels, tile_products(): pl.pallas_call(functools.partial(_products_kernel, forward=forward, lift=...  18.3 us

profile of v16, /device:TPU:6, one launch (start us, length us, event | category | flops | bytes accessed | tf_op | source)
XLA Modules:
  0.0 205.8 jit_solution(5587709857373118819)
XLA Ops:
  0.7 1.3 reshape.12.refs_1_
  1.9 0.7 convert_rsqrt_fusion
  2.6 0.0 copy-start
  2.7 0.6 dynamic-slice_bitcast_fusion.s_ref
  3.2 16.3 %shard_map.64.refs_2_ = bf16[8,64,256]{2,1,0:T(8,128)(2,1)} custom-call(f32[64,128]{1,0:T(8,128)} %refs_0_.1, s32[16,128]{1,0:T(8,128)} %bitcast.35), custom_call_target="tpu_custom_call" | custom-call | bytes 1048576 | tf_op jit(solution)/shard_map/pallas_call | solution.py:246
  19.6 4.8 %shard_map.65 = f32[8,64,256]{2,1,0:T(8,128)} custom-call(s32[2,32]{1,0:T(2,128)} %bitcast.36, s32[1]{0:T(128)} %bitcast.18.refs_1_, bf16[8,64,256]{2,1,0:T(8,128)(2,1)} %shard_map.64.refs_2_, bf16[32,256,256]{2,1,0:T(8,128)(2,1)} %bitcast.22), custom_call_target="tpu_custom_call" | custom-call | flops 268435456 | bytes 4980736 | tf_op jit(solution)/shard_map/pallas_call | solution.py:333
  24.4 31.6 %shard_map.66 = bf16[4,4,2,16,256]{4,3,2,1,0:T(8,128)(2,1)} custom-call(f32[4,4,2,16,256]{4,3,2,1,0:T(8,128)} %bitcast.29, s32[8,256]{1,0:T(8,128)} %reshape.12.refs_1_), custom_call_target="tpu_custom_call" | custom-call | bytes 1048576 | tf_op jit(solution)/shard_map/pallas_call | solution.py:246
  55.9 4.3 %shard_map.67 = f32[8,64,256]{2,1,0:T(8,128)} custom-call(s32[2,32]{1,0:T(2,128)} %bitcast.37, s32[1]{0:T(128)} %bitcast.19.refs_1_, bf16[8,64,256]{2,1,0:T(8,128)(2,1)} %bitcast.31, bf16[32,256,256]{2,1,0:T(8,128)(2,1)} %bitcast.23), custom_call_target="tpu_custom_call" | custom-call | flops 268435456 | bytes 4980736 | tf_op jit(solution)/shard_map/pallas_call | solution.py:333
  60.2 0.0 copy-done
  60.2 54.1 %shard_map.68 = (f32[4,4,32,256]{3,2,1,0:T(8,128)}, f32[64,128]{1,0:T(8,128)}) custom-call(f32[4,4,32,256]{3,2,1,0:T(8,128)} %bitcast.28, f32[1,256]{1,0:T(1,128)} %dynamic-slice_bitcast_fusion.s_ref), custom_call_target="tpu_custom_call" | custom-call | bytes 1048576 | tf_op jit(solution)/shard_map/pallas_call | solution.py:207
  114.3 1.4 slice.6.refs_2_
  115.8 4.9 %shard_map.69 = f32[8,64,256]{2,1,0:T(8,128)} custom-call(s32[2,32]{1,0:T(2,128)} %bitcast.38, s32[1]{0:T(128)} %bitcast.20.refs_1_, f32[64,64]{1,0:T(8,128)} %slice.6.refs_2_, f32[8,64,256]{2,1,0:T(8,128)} %bitcast.32, f32[8,1,256]{2,1,0:T(1,128)} %bitcast.34, bf16[32,256,256]{2,1,0:T(8,128)(2,1)} %bitcast.24), custom_call_target="tpu_custom_call" | custom-call | flops 268435456 | bytes 4980736 | tf_op jit(solution)/shard_map/pallas_call | solution.py:333
  120.7 26.5 %shard_map.70 = bf16[4,4,2,16,256]{4,3,2,1,0:T(8,128)(2,1)} custom-call(f32[4,4,2,16,256]{4,3,2,1,0:T(8,128)} %bitcast.27, s32[8,256]{1,0:T(8,128)} %reshape.12.refs_1_), custom_call_target="tpu_custom_call" | custom-call | bytes 1048576 | tf_op jit(solution)/shard_map/pallas_call | solution.py:246
  147.2 4.3 %shard_map.71 = f32[8,64,256]{2,1,0:T(8,128)} custom-call(s32[2,32]{1,0:T(2,128)} %bitcast.39, s32[1]{0:T(128)} %bitcast.21.refs_1_, bf16[8,64,256]{2,1,0:T(8,128)(2,1)} %bitcast.30, bf16[32,256,256]{2,1,0:T(8,128)(2,1)} %bitcast.25), custom_call_target="tpu_custom_call" | custom-call | flops 268435456 | bytes 4980736 | tf_op jit(solution)/shard_map/pallas_call | solution.py:333
  151.5 52.6 %shard_map.72 = (f32[4,4,32,256]{3,2,1,0:T(8,128)}, f32[64,128]{1,0:T(8,128)}) custom-call(f32[4,4,32,256]{3,2,1,0:T(8,128)} %bitcast.26, f32[1,256]{1,0:T(1,128)} %dynamic-slice_bitcast_fusion.s_ref), custom_call_target="tpu_custom_call" | custom-call | bytes 1048576 | tf_op jit(solution)/shard_map/pallas_call | solution.py:207
  204.1 1.7 convolution_multiply_fusion
Async XLA Ops:
  2.6 57.6 %copy-start = (f32[2048]{0:T(1024)}, f32[2048]{0:T(1024)S(1)}, u32[]{:S(2)}) copy-start(f32[2048]{0:T(1024)S(1)} %convert_rsqrt_fusion) | copy-start | bytes 24580

commit v17 on v16

--- a/solution.py
+++ b/solution.py
@@ -168,7 +168,9 @@
     sems = rest[-1]
     _barrier([rows, cols])
     pending = []
-    own = _reduce_scatter(rows, sems, 0, x_ref, rbufs, pending)[...] * s_ref[...]
+    degree = s_ref[pl.ds(rows.me // (math.prod(row_factors) // s_ref.shape[0]), 1)]
+    scale = 1.0 / jnp.sqrt(degree.astype(jnp.float32))
+    own = _reduce_scatter(rows, sems, 0, x_ref, rbufs, pending)[...] * scale
     _all_gather(rows, sems, 2, gbuf, own, pending)
     y_ref[...] = gbuf[...]
     n = math.prod(row_factors)
@@ -422,7 +424,8 @@
             slot_ids, live_count, query_tiles_panel, tile_set, product_tiles, False
         )
         lifted_pieces, inverse = product_gram(
-            product_partial.reshape(n_row, width // p_per_tile, side), my_pscale, ROW_FACTORS,
+            product_partial.reshape(n_row, width // p_per_tile, side),
+            product_degree.reshape(product_tiles, side), ROW_FACTORS,
             GRAM_FACTORS, 2, width,
         )
         lifted_tiles = lifted_pieces.reshape(product_tiles, width, side)

time: 208 us -> 207 us (level)
  no operation moved by 1% of the time
where the time goes in v17:
time: 207 us; the launch traced here: 205 us
  Pallas kernels  199 us (96%)
  local copies, waits for them, and re-layouts  2.65 us (1%)
    pallas_call x2, Pallas kernels, product_gram(): pl.pallas_call(functools.partial(_product_gram_kernel, row_factors=tuple(...  107 us
    pallas_call x3, Pallas kernels, staged(): pl.pallas_call(functools.partial(_staged_kernel, axis=axis, factors=tuple...  74.4 us
    pallas_call x4, Pallas kernels, tile_products(): pl.pallas_call(functools.partial(_products_kernel, forward=forward, lift=...  18.3 us

profile of v17, /device:TPU:6, one launch (start us, length us, event | category | flops | bytes accessed | tf_op | source)
XLA Modules:
  0.0 205.2 jit_solution(1869142634328426910)
XLA Ops:
  0.0 0.0 copy-start.1
  0.7 16.3 %shard_map.64.refs_2_ = bf16[8,64,256]{2,1,0:T(8,128)(2,1)} custom-call(f32[64,128]{1,0:T(8,128)} %refs_0_.1, s32[16,128]{1,0:T(8,128)} %bitcast.31), custom_call_target="tpu_custom_call" | custom-call | bytes 1048576 | tf_op jit(solution)/shard_map/pallas_call | solution.py:248
  17.0 0.0 copy-start
  17.0 4.8 %shard_map.65 = f32[8,64,256]{2,1,0:T(8,128)} custom-call(s32[2,32]{1,0:T(2,128)} %bitcast.33, s32[1]{0:T(128)} %bitcast.16.refs_1_, bf16[8,64,256]{2,1,0:T(8,128)(2,1)} %shard_map.64.refs_2_, bf16[32,256,256]{2,1,0:T(8,128)(2,1)} %bitcast.20), custom_call_target="tpu_custom_call" | custom-call | flops 268435456 | bytes 4980736 | tf_op jit(solution)/shard_map/pallas_call | solution.py:335
  21.8 0.0 copy-done.1
  21.8 0.6 reshape.16.refs_1_
  22.4 31.5 %shard_map.66 = bf16[4,4,2,16,256]{4,3,2,1,0:T(8,128)(2,1)} custom-call(f32[4,4,2,16,256]{4,3,2,1,0:T(8,128)} %bitcast.27, s32[8,256]{1,0:T(8,128)} %reshape.16.refs_1_), custom_call_target="tpu_custom_call" | custom-call | bytes 1048576 | tf_op jit(solution)/shard_map/pallas_call | solution.py:248
  54.0 4.3 %shard_map.67 = f32[8,64,256]{2,1,0:T(8,128)} custom-call(s32[2,32]{1,0:T(2,128)} %bitcast.34, s32[1]{0:T(128)} %bitcast.17.refs_1_, bf16[8,64,256]{2,1,0:T(8,128)(2,1)} %bitcast.29, bf16[32,256,256]{2,1,0:T(8,128)(2,1)} %bitcast.21), custom_call_target="tpu_custom_call" | custom-call | flops 268435456 | bytes 4980736 | tf_op jit(solution)/shard_map/pallas_call | solution.py:335
  58.2 0.0 copy-done
  58.3 0.6 reshape.17.s_ref
  58.9 54.0 %shard_map.68 = (f32[4,4,32,256]{3,2,1,0:T(8,128)}, f32[64,128]{1,0:T(8,128)}) custom-call(f32[4,4,32,256]{3,2,1,0:T(8,128)} %bitcast.25, s32[8,256]{1,0:T(8,128)} %reshape.17.s_ref), custom_call_target="tpu_custom_call" | custom-call | bytes 1048576 | tf_op jit(solution)/shard_map/pallas_call | solution.py:209
  112.9 1.4 slice.6.refs_2_
  114.3 0.6 convert_rsqrt_fusion
  115.0 4.9 %shard_map.69 = f32[8,64,256]{2,1,0:T(8,128)} custom-call(s32[2,32]{1,0:T(2,128)} %bitcast.35, s32[1]{0:T(128)} %bitcast.18.refs_1_, f32[64,64]{1,0:T(8,128)} %slice.6.refs_2_, f32[8,64,256]{2,1,0:T(8,128)} %bitcast.30, f32[8,1,256]{2,1,0:T(1,128)} %bitcast.32, bf16[32,256,256]{2,1,0:T(8,128)(2,1)} %bitcast.22), custom_call_target="tpu_custom_call" | custom-call | flops 268435456 | bytes 4980736 | tf_op jit(solution)/shard_map/pallas_call | solution.py:335
  119.9 26.5 %shard_map.70 = bf16[4,4,2,16,256]{4,3,2,1,0:T(8,128)(2,1)} custom-call(f32[4,4,2,16,256]{4,3,2,1,0:T(8,128)} %bitcast.26, s32[8,256]{1,0:T(8,128)} %reshape.16.refs_1_), custom_call_target="tpu_custom_call" | custom-call | bytes 1048576 | tf_op jit(solution)/shard_map/pallas_call | solution.py:248
  146.4 4.3 %shard_map.71 = f32[8,64,256]{2,1,0:T(8,128)} custom-call(s32[2,32]{1,0:T(2,128)} %bitcast.36, s32[1]{0:T(128)} %bitcast.19.refs_1_, bf16[8,64,256]{2,1,0:T(8,128)(2,1)} %bitcast.28, bf16[32,256,256]{2,1,0:T(8,128)(2,1)} %bitcast.23), custom_call_target="tpu_custom_call" | custom-call | flops 268435456 | bytes 4980736 | tf_op jit(solution)/shard_map/pallas_call | solution.py:335
  150.7 52.8 %shard_map.72 = (f32[4,4,32,256]{3,2,1,0:T(8,128)}, f32[64,128]{1,0:T(8,128)}) custom-call(f32[4,4,32,256]{3,2,1,0:T(8,128)} %bitcast.24, s32[8,256]{1,0:T(8,128)} %reshape.17.s_ref), custom_call_target="tpu_custom_call" | custom-call | bytes 1048576 | tf_op jit(solution)/shard_map/pallas_call | solution.py:209
  203.5 1.7 convolution_multiply_fusion
Async XLA Ops:
  0.0 21.8 %copy-start.1 = (s32[2048]{0:T(1024)S(1)}, s32[2048]{0:T(1024)}, u32[]{:S(2)}) copy-start(s32[2048]{0:T(1024)} %param.9) | copy-start | bytes 24580
  17.0 41.3 %copy-start = (s32[2048]{0:T(1024)S(1)}, s32[2048]{0:T(1024)}, u32[]{:S(2)}) copy-start(s32[2048]{0:T(1024)} %param.10) | copy-start | bytes 24580

commit v18 on v17

--- a/solution.py
+++ b/solution.py
@@ -300,7 +300,8 @@
         inv = inv_ref[...]
         for p in range(src_ref.shape[0]):
             current = jnp.dot(inv, lifted_ref[p], precision=HIGH, preferred_element_type=jnp.float32)
-            src_ref[p] = (current * scale_ref[p]).astype(src_ref.dtype)
+            scale = 1.0 / jnp.sqrt(scale_ref[p].astype(jnp.float32))
+            src_ref[p] = (current * scale).astype(src_ref.dtype)
     out_ref[...] = jnp.zeros_like(out_ref)
     src_row, dst_row = (1, 0) if forward else (0, 1)
     count = count_ref[0]
@@ -412,7 +413,8 @@
     for iteration in range(ITERS):
         if iteration:
             partial_sum = tile_products(slot_ids, live_count, None, tile_set, query_tiles, True,
-                                        lift=(inverse, lifted_tiles, pscale))
+                                        lift=(inverse, lifted_tiles,
+                                              product_degree.reshape(product_tiles, 1, side)))
         else:
             partial_sum = tile_products(slot_ids, live_count, scaled_tiles, tile_set, query_tiles, True)
         query_tiles_panel = staged(

time: 207 us -> 207 us (level)
  no operation moved by 1% of the time
where the time goes in v18:
time: 207 us; the launch traced here: 205 us
  Pallas kernels  200 us (97%)
  local copies, waits for them, and re-layouts  2.65 us (1%)
    pallas_call x2, Pallas kernels, product_gram(): pl.pallas_call(functools.partial(_product_gram_kernel, row_factors=tuple(...  107 us
    pallas_call x3, Pallas kernels, staged(): pl.pallas_call(functools.partial(_staged_kernel, axis=axis, factors=tuple...  74.4 us
    pallas_call x4, Pallas kernels, tile_products(): pl.pallas_call(functools.partial(_products_kernel, forward=forward, lift=...  18.3 us

profile of v18, /device:TPU:6, one launch (start us, length us, event | category | flops | bytes accessed | tf_op | source)
XLA Modules:
  0.0 204.9 jit_solution(16377199653586625519)
XLA Ops:
  0.0 0.0 copy-start.1
  0.7 16.3 %shard_map.64.refs_2_ = bf16[8,64,256]{2,1,0:T(8,128)(2,1)} custom-call(f32[64,128]{1,0:T(8,128)} %refs_0_.1, s32[16,128]{1,0:T(8,128)} %bitcast.31), custom_call_target="tpu_custom_call" | custom-call | bytes 1048576 | tf_op jit(solution)/shard_map/pallas_call | solution.py:248
  17.0 0.0 copy-start
  17.0 4.8 %shard_map.65 = f32[8,64,256]{2,1,0:T(8,128)} custom-call(s32[2,32]{1,0:T(2,128)} %bitcast.33, s32[1]{0:T(128)} %bitcast.16.refs_1_, bf16[8,64,256]{2,1,0:T(8,128)(2,1)} %shard_map.64.refs_2_, bf16[32,256,256]{2,1,0:T(8,128)(2,1)} %bitcast.20), custom_call_target="tpu_custom_call" | custom-call | flops 268435456 | bytes 4980736 | tf_op jit(solution)/shard_map/pallas_call | solution.py:336
  21.8 0.0 copy-done.1
  21.8 0.6 reshape.16.refs_1_
  22.4 31.5 %shard_map.66 = bf16[4,4,2,16,256]{4,3,2,1,0:T(8,128)(2,1)} custom-call(f32[4,4,2,16,256]{4,3,2,1,0:T(8,128)} %bitcast.27, s32[8,256]{1,0:T(8,128)} %reshape.16.refs_1_), custom_call_target="tpu_custom_call" | custom-call | bytes 1048576 | tf_op jit(solution)/shard_map/pallas_call | solution.py:248
  54.0 4.3 %shard_map.67 = f32[8,64,256]{2,1,0:T(8,128)} custom-call(s32[2,32]{1,0:T(2,128)} %bitcast.34, s32[1]{0:T(128)} %bitcast.17.refs_1_, bf16[8,64,256]{2,1,0:T(8,128)(2,1)} %bitcast.29, bf16[32,256,256]{2,1,0:T(8,128)(2,1)} %bitcast.21), custom_call_target="tpu_custom_call" | custom-call | flops 268435456 | bytes 4980736 | tf_op jit(solution)/shard_map/pallas_call | solution.py:336
  58.3 0.0 copy-done
  58.3 0.6 reshape.17.s_ref
  58.9 54.1 %shard_map.68 = (f32[4,4,32,256]{3,2,1,0:T(8,128)}, f32[64,128]{1,0:T(8,128)}) custom-call(f32[4,4,32,256]{3,2,1,0:T(8,128)} %bitcast.25, s32[8,256]{1,0:T(8,128)} %reshape.17.s_ref), custom_call_target="tpu_custom_call" | custom-call | bytes 1048576 | tf_op jit(solution)/shard_map/pallas_call | solution.py:209
  112.9 1.4 slice.6.refs_2_
  114.4 4.9 %shard_map.69 = f32[8,64,256]{2,1,0:T(8,128)} custom-call(s32[2,32]{1,0:T(2,128)} %bitcast.35, s32[1]{0:T(128)} %bitcast.18.refs_1_, f32[64,64]{1,0:T(8,128)} %slice.6.refs_2_, f32[8,64,256]{2,1,0:T(8,128)} %bitcast.30, s32[8,1,256]{2,1,0:T(1,128)} %bitcast.32, bf16[32,256,256]{2,1,0:T(8,128)(2,1)} %bitcast.22), custom_call_target="tpu_custom_call" | custom-call | flops 268435456 | bytes 4980736 | tf_op jit(solution)/shard_map/pallas_call | solution.py:336
  119.3 26.5 %shard_map.70 = bf16[4,4,2,16,256]{4,3,2,1,0:T(8,128)(2,1)} custom-call(f32[4,4,2,16,256]{4,3,2,1,0:T(8,128)} %bitcast.26, s32[8,256]{1,0:T(8,128)} %reshape.16.refs_1_), custom_call_target="tpu_custom_call" | custom-call | bytes 1048576 | tf_op jit(solution)/shard_map/pallas_call | solution.py:248
  145.8 4.3 %shard_map.71 = f32[8,64,256]{2,1,0:T(8,128)} custom-call(s32[2,32]{1,0:T(2,128)} %bitcast.36, s32[1]{0:T(128)} %bitcast.19.refs_1_, bf16[8,64,256]{2,1,0:T(8,128)(2,1)} %bitcast.28, bf16[32,256,256]{2,1,0:T(8,128)(2,1)} %bitcast.23), custom_call_target="tpu_custom_call" | custom-call | flops 268435456 | bytes 4980736 | tf_op jit(solution)/shard_map/pallas_call | solution.py:336
  150.1 53.0 %shard_map.72 = (f32[4,4,32,256]{3,2,1,0:T(8,128)}, f32[64,128]{1,0:T(8,128)}) custom-call(f32[4,4,32,256]{3,2,1,0:T(8,128)} %bitcast.24, s32[8,256]{1,0:T(8,128)} %reshape.17.s_ref), custom_call_target="tpu_custom_call" | custom-call | bytes 1048576 | tf_op jit(solution)/shard_map/pallas_call | solution.py:209
  203.2 1.7 convolution_multiply_fusion
Async XLA Ops:
  0.0 21.8 %copy-start.1 = (s32[2048]{0:T(1024)S(1)}, s32[2048]{0:T(1024)}, u32[]{:S(2)}) copy-start(s32[2048]{0:T(1024)} %param.9) | copy-start | bytes 24580
  17.0 41.3 %copy-start = (s32[2048]{0:T(1024)S(1)}, s32[2048]{0:T(1024)}, u32[]{:S(2)}) copy-start(s32[2048]{0:T(1024)} %param.10) | copy-start | bytes 24580
